TPU v7x, 256 devices: a whole 4x4x8 slice. The times are simulated.
256 devices in a mesh: row: 8 (over y, core), col: 32 (over z, x).
Axes of the slice: x: 4, y: 4, z: 8, core: 2. Of those that a mesh axis runs over, the one named last changes fastest.
Arguments:
- observed: float32 [16384, 128], P(('row', 'col')), may hold values from -60 to 60
- lengths: int32 [16384], P(('row', 'col')), may hold values from 0 to 128
- features: float32 [16384, 32], P(('row', 'col')), may hold values from -6 to 6
- length_scale: float32 [32], replicated, may hold values from 2 to 5
- epoch_gain: float32 [128], replicated, may hold values from 0.5 to 2
Outputs:
- solution_field: float32 [16384, 128], P(('row', 'col'))
- residual: float32 [16384, 128], P(('row', 'col'))
All inputs are finite; a program needn't handle non-finite values.
Results may differ from a plain program's by a relative error of at most 0.007.
Values may be sent and summed in bfloat16 or wider, within the bound.
No kernel may reach another device: no remote copies, remote signals or barrier semaphores. Data moves between devices by JAX's collectives and lax.ppermute only.
A program may use at most 64 MiB of HBM per device.

v0:
```python
import functools
import math

import jax
import jax.numpy as jnp
from jax import lax
from jax.sharding import Mesh
from jax.sharding import PartitionSpec as P

ITERS = 2
ROW = ("row_0", "row_1")
COL = ("col_0", "col_1")
ROW_COL = ("row_0", "row_1", "col_0", "col_1")


noise_level = 0.3
epoch_offset = 16.0


def side_by_side(arrays, axis, dim, along):
    widths = [math.prod(a.shape[along:]) for a in arrays]
    both = jnp.concatenate(
        [a.reshape(*a.shape[:along], w) for a, w in zip(arrays, widths)], axis=along
    )
    out = lax.all_gather(both, axis, axis=dim, tiled=True)
    blocks = jnp.split(out, [sum(widths[:k]) for k in range(1, len(widths))], axis=along)
    return tuple((b.reshape(*out.shape[:along], *a.shape[along:]) for a, b in zip(arrays, blocks)))


def in_order(blocks, dim):
    blocks = jnp.moveaxis(blocks, 0, dim)
    dims = blocks.shape
    return blocks.reshape(*dims[:dim], dims[dim] * dims[dim + 1], *dims[dim + 2 :])


def from_everyone(shard, axis):
    copies = jnp.broadcast_to(shard, (lax.axis_size(axis), *shard.shape))
    return lax.all_to_all(copies, axis, split_axis=0, concat_axis=0, tiled=True)


def collect(shard, axis, dim):
    return in_order(from_everyone(shard, axis), dim)


def split_up(shard, dim, devices):
    before, after = (shard.shape[:dim], shard.shape[dim + 1 :])
    return jnp.moveaxis(shard.reshape(*before, devices, -1, *after), dim, 0)


def sent_and_summed(shard, axis, dim):
    blocks = split_up(shard, dim, lax.axis_size(axis))
    arrived = lax.all_to_all(blocks, axis, split_axis=0, concat_axis=0, tiled=True)
    return arrived.sum(axis=0)


def over_axes(shard, axes):
    return functools.reduce(lax.psum, axes, shard)


def epoch_matrix(epoch_gain):
    steps = jnp.arange(epoch_gain.shape[0]).astype(jnp.float32)
    base = epoch_offset / (steps[:, None] + steps[None, :] + epoch_offset)
    return base + jnp.diag(epoch_gain)


def kernel_block(left, left_sq, right, right_sq):
    cross = jnp.dot(
        left, right.T, precision=lax.Precision.HIGHEST, preferred_element_type=jnp.float32
    )
    dist = jnp.maximum(left_sq[:, None] + right_sq[None, :] - 2.0 * cross, 0.0)
    return jnp.exp(-0.5 * dist).astype(jnp.bfloat16)


def blockwise(left, left_sq, right, right_sq, mixed, count):
    block = math.gcd(count, 512)

    def one_block(index):
        return jnp.dot(
            kernel_block(left, left_sq, right, right_sq), mixed, preferred_element_type=jnp.float32
        )

    result = lax.map(one_block, jnp.arange(count // block, dtype=jnp.int32))
    return result.reshape(count, mixed.shape[1])


def per_device(observed, lengths, features, length_scale, epoch_gain):
    rows_own, width = observed.shape
    scaled = features / length_scale[None, :]
    sq = jnp.sum(scaled * scaled, axis=1)
    mask = (jnp.arange(width)[None, :] < lengths[:, None]).astype(jnp.float32)
    epoch_kernel = epoch_matrix(epoch_gain)
    left_scaled, left_sq = side_by_side((scaled, sq), ROW, 0, 1)
    right_scaled, right_sq = side_by_side((scaled, sq), COL, 0, 1)

    def product(mixed):
        right_mixed = collect(mixed, COL, 0)
        return sent_and_summed(
            blockwise(
                left_scaled,
                left_sq,
                right_scaled,
                right_sq,
                right_mixed,
                rows_own * lax.axis_size(ROW),
            ),
            ROW,
            0,
        )

    def operate(field):
        mixed = jnp.dot(
            mask * field,
            epoch_kernel,
            precision=lax.Precision.HIGHEST,
            preferred_element_type=jnp.float32,
        ).astype(jnp.bfloat16)
        return mask * product(mixed) + noise_level * field

    def two_products(residual, image):
        return (
            over_axes(jnp.sum(residual * residual), ROW_COL),
            over_axes(jnp.sum(residual * image), ROW_COL),
        )

    solution_field = jnp.zeros_like(observed)
    residual = mask * observed
    image = operate(residual)
    norm_now, curve = two_products(residual, image)
    alpha = norm_now / curve
    direction, along = (residual, image)
    for step in range(ITERS):
        solution_field = solution_field + alpha * direction
        residual = residual - alpha * along
        if step + 1 < ITERS:
            image = operate(residual)
            norm_next, curve = two_products(residual, image)
            ratio = norm_next / norm_now
            alpha = norm_next / (curve - ratio * norm_next / alpha)
            direction = residual + ratio * direction
            along = image + ratio * along
            norm_now = norm_next
    return (solution_field, residual)


def solution(mesh):
    torus = Mesh(mesh.devices.reshape(4, 2, 8, 4), ("row_0", "row_1", "col_0", "col_1"))
    in_specs = (P(ROW_COL, None), P(ROW_COL), P(ROW_COL, None), P(), P())
    out_specs = (P(ROW_COL, None), P(ROW_COL, None))
    return jax.shard_map(
        per_device, mesh=torus, in_specs=in_specs, out_specs=out_specs, check_vma=False
    )
```

profile of v0, /device:TPU:32, one launch (start us, length us, event | category | flops | bytes accessed | tf_op | source)
XLA Modules:
  0.0 211.3 jit_solution(3449624680151245784)
XLA Ops:
  0.6 1.0 convolution_convert_fusion.1
  1.7 0.9 broadcast_in_dim.36
  2.6 11.2 %all-to-all-start = ((bf16[32,64,128]{2,1,0:T(8,128)(2,1)}), bf16[32,64,128]{2,1,0:T(8,128)(2,1)S(1)}, u32[]{:S(2)}, u32[]{:S(2)}) async-start(bf16[32,64,128]{2,1,0:T(8,128)(2,1)} %broadcast_in_dim.36), calls=%async_computation | async-start | bytes 1048576 | tf_op jit(solution)/shard_map/all_to_all | solution.py:38
  13.8 0.8 multiply_reduce_fusion.4
  14.6 13.3 %all-gather = f32[8,64,33]{1,2,0:T(8,128)S(1)} all-gather(f32[1,64,33]{1,2,0:T(8,128)S(1)} %maximum_bitcast_fusion), channel_id=1, replica_groups=mesh['row_0'=4,'row_1'=2,'col_0'=8,'col_1'=4] {'row_0','row_1'}, dimensions={0}, use_global_device_ids=true | all-gather | bytes 76032 | tf_op jit(solution)/shard_map/all_gather | solution.py:25
  28.0 49.3 %all-gather.1 = f32[32,64,33]{1,2,0:T(8,128)S(1)} all-gather(f32[1,64,33]{1,2,0:T(8,128)S(1)} %maximum_bitcast_fusion), channel_id=1, replica_groups=mesh['row_0'=4,'row_1'=2,'col_0'=8,'col_1'=4] {'col_0','col_1'}, dimensions={0}, use_global_device_ids=true | all-gather | bytes 278784 | tf_op jit(solution)/shard_map/all_gather | solution.py:25
  77.6 4.6 %exponential_convert_fusion = bf16[512,2048]{1,0:T(8,128)(2,1)S(1)} fusion(f32[2048]{0:T(1024)S(1)} %bitcast.24, f32[512]{0:T(512)S(1)} %bitcast.26, f32[2048,33]{0,1:T(8,128)S(1)} %reshape.36, f32[512,33]{0,1:T(8,128)S(1)} %reshape.34), kind=kOutput, calls=%fused_computation | convolution fusion | flops 408944640 | bytes 2435072 | tf_op jit(solution)/shard_map/while/body/eval_jaxpr/dot_general | solution.py:67
  82.3 0.7 fusion.25
  83.0 11.1 %all_to_all.20 = f32[8,64,128]{2,1,0:T(8,128)S(1)} all-to-all(f32[8,64,128]{2,1,0:T(8,128)S(1)} %fusion.25), channel_id=1, replica_groups=mesh['row_0'=4,'row_1'=2,'col_0'=8,'col_1'=4] {'row_0','row_1'}, dimensions={0} | all-to-all | bytes 524288 | tf_op jit(solution)/shard_map/all_to_all | solution.py:52
  94.1 0.7 multiply_reduce_fusion.2
  94.8 9.5 %all-reduce.5 = (f32[]{:T(128)}, f32[]{:T(128)}) all-reduce(f32[]{:T(128)} %get-tuple-element.31, f32[]{:T(128)} %get-tuple-element.30), channel_id=1, replica_groups=mesh['row_0'=4,'row_1'=2,'col_0'=8,'col_1'=4] {'row_0'}, use_global_device_ids=true, to_apply=%region_1.2 | all-reduce | flops 2 | bytes 16 | tf_op jit(solution)/shard_map/psum | solution.py:57
  104.3 3.1 %all-reduce.7 = (f32[]{:T(128)}, f32[]{:T(128)}) all-reduce(f32[]{:T(128)} %get-tuple-element.58, f32[]{:T(128)} %get-tuple-element.59), channel_id=1, replica_groups=mesh['row_0'=4,'row_1'=2,'col_0'=8,'col_1'=4] {'row_1'}, use_global_device_ids=true, to_apply=%region_2.3 | all-reduce | flops 2 | bytes 16 | tf_op jit(solution)/shard_map/psum | solution.py:57
  107.4 16.1 %all-reduce.1 = (f32[]{:T(128)}, f32[]{:T(128)}) all-reduce(f32[]{:T(128)} %get-tuple-element.62, f32[]{:T(128)} %get-tuple-element.63), channel_id=1, replica_groups=mesh['row_0'=4,'row_1'=2,'col_0'=8,'col_1'=4] {'col_0'}, use_global_device_ids=true, to_apply=%region_3.4 | all-reduce | flops 2 | bytes 16 | tf_op jit(solution)/shard_map/psum | solution.py:57
  123.5 10.3 %all-reduce.3 = (f32[]{:T(128)}, f32[]{:T(128)}) all-reduce(f32[]{:T(128)} %get-tuple-element.43, f32[]{:T(128)} %get-tuple-element.44), channel_id=1, replica_groups=mesh['row_0'=4,'row_1'=2,'col_0'=8,'col_1'=4] {'col_1'}, use_global_device_ids=true, to_apply=%region_4.5 | all-reduce | flops 2 | bytes 16 | tf_op jit(solution)/shard_map/psum | solution.py:57
  135.2 0.3 convolution_convert_fusion
  135.6 20.4 %all_to_all.21 = bf16[32,64,128]{2,1,0:T(8,128)(2,1)S(1)} all-to-all(bf16[32,64,128]{2,1,0:T(8,128)(2,1)S(1)} %broadcast_in_dim.37), channel_id=1, replica_groups=mesh['row_0'=4,'row_1'=2,'col_0'=8,'col_1'=4] {'col_0','col_1'}, dimensions={0} | all-to-all | bytes 1048576 | tf_op jit(solution)/shard_map/all_to_all | solution.py:38
  156.0 0.7 fusion.26
  156.7 9.9 %all_to_all.22 = f32[8,64,128]{2,1,0:T(8,128)S(1)} all-to-all(f32[8,64,128]{2,1,0:T(8,128)S(1)} %fusion.26), channel_id=1, replica_groups=mesh['row_0'=4,'row_1'=2,'col_0'=8,'col_1'=4] {'row_0','row_1'}, dimensions={0} | all-to-all | bytes 524288 | tf_op jit(solution)/shard_map/all_to_all | solution.py:52
  166.7 0.7 multiply_reduce_fusion
  167.5 9.6 %all-reduce.4 = (f32[]{:T(128)}, f32[]{:T(128)}) all-reduce(f32[]{:T(128)} %get-tuple-element.33, f32[]{:T(128)} %get-tuple-element.32), channel_id=1, replica_groups=mesh['row_0'=4,'row_1'=2,'col_0'=8,'col_1'=4] {'row_0'}, use_global_device_ids=true, to_apply=%region_13.14 | all-reduce | flops 2 | bytes 16 | tf_op jit(solution)/shard_map/psum | solution.py:57
  177.0 3.1 %all-reduce.6 = (f32[]{:T(128)}, f32[]{:T(128)}) all-reduce(f32[]{:T(128)} %get-tuple-element.56, f32[]{:T(128)} %get-tuple-element.57), channel_id=1, replica_groups=mesh['row_0'=4,'row_1'=2,'col_0'=8,'col_1'=4] {'row_1'}, use_global_device_ids=true, to_apply=%region_14.15 | all-reduce | flops 2 | bytes 16 | tf_op jit(solution)/shard_map/psum | solution.py:57
  180.2 15.8 %all-reduce = (f32[]{:T(128)}, f32[]{:T(128)}) all-reduce(f32[]{:T(128)} %get-tuple-element.60, f32[]{:T(128)} %get-tuple-element.61), channel_id=1, replica_groups=mesh['row_0'=4,'row_1'=2,'col_0'=8,'col_1'=4] {'col_0'}, use_global_device_ids=true, to_apply=%region_15.16 | all-reduce | flops 2 | bytes 16 | tf_op jit(solution)/shard_map/psum | solution.py:57
  196.0 10.0 %all-reduce.2 = (f32[]{:T(128)}, f32[]{:T(128)}) all-reduce(f32[]{:T(128)} %get-tuple-element.34, f32[]{:T(128)} %get-tuple-element.42), channel_id=1, replica_groups=mesh['row_0'=4,'row_1'=2,'col_0'=8,'col_1'=4] {'col_1'}, use_global_device_ids=true, to_apply=%region_16.17 | all-reduce | flops 2 | bytes 16 | tf_op jit(solution)/shard_map/psum | solution.py:57
  210.6 0.7 multiply_subtract_fusion
  (19 shorter events, 0.7 us)
Async XLA Ops:
  2.6 79.7 %all-to-all-start = ((bf16[32,64,128]{2,1,0:T(8,128)(2,1)}), bf16[32,64,128]{2,1,0:T(8,128)(2,1)S(1)}, u32[]{:S(2)}, u32[]{:S(2)}) async-start(bf16[32,64,128]{2,1,0:T(8,128)(2,1)} %broadcast_in_dim.36), calls=%async_computation | async-start | bytes 1048576 | tf_op jit(solution)/shard_map/all_to_all | solution.py:38
  82.2 11.9 %copy-start = (f32[64,128]{1,0:T(8,128)S(1)}, f32[64,128]{1,0:T(8,128)}, u32[]{:S(2)}) copy-start(f32[64,128]{1,0:T(8,128)} %param.5) | copy-start | bytes 98308
  82.2 11.9 %copy-start.1 = (s32[64]{0:T(128)S(1)}, s32[64]{0:T(128)}, u32[]{:S(2)}) copy-start(s32[64]{0:T(128)} %param.6) | copy-start | bytes 772
  82.3 53.0 %copy-start.2 = (f32[128]{0:T(128)S(1)}, f32[128]{0:T(128)}, u32[]{:S(2)}) copy-start(f32[128]{0:T(128)} %param.9) | copy-start | bytes 1540
where the time goes:
time: 212 us; the launch traced here: 211 us
  blocking collectives  182 us (86%)
  starting transfers between devices  11.2 us (5%)
  matrix products  7.32 us (3%)
  between operations  6.7 us (3%)
  other arithmetic  3.09 us (1%)
    psum x8, blocking collectives, over_axes(): return functools.reduce(lax.psum, axes, shard)  77.5 us
    all_gather x2, blocking collectives, side_by_side(): out = lax.all_gather(both, axis, axis=dim, tiled=True)  62.6 us
    all_to_all x2, blocking collectives, sent_and_summed(): lax.all_to_all(blocks, axis, split_axis=0, concat_axis=0, tiled=True)  21.1 us
    all_to_all x1, blocking collectives, from_everyone(): return lax.all_to_all(copies, axis, split_axis=0, concat_axis=0, tiled=True)  20.4 us
    all_to_all x1, starting transfers between devices, from_everyone(): return lax.all_to_all(copies, axis, split_axis=0, concat_axis=0, tiled=True)  11.2 us
    dot_general x1, matrix products, kernel_block(): jnp.dot(left, right.T, precision=lax.Precision.HIGHEST, preferred_element...  4.61 us
  transfers between devices with their start and end apart: 1, of which 0 were waited for; matrix products, arithmetic and copies ran while one was open for 3% of the time, Pallas kernels for 0%

commit v1 on v0

v1 whole, which is shorter than its diff:
```python
import math

import jax
import jax.numpy as jnp
from jax import lax
from jax.experimental import pallas as pl
from jax.experimental.pallas import tpu as pltpu
from jax.sharding import Mesh
from jax.sharding import PartitionSpec as P

Y, C, Z, X = "y", "c", "z", "x"
ALL = (Y, C, Z, X)

noise_level = 0.3
epoch_offset = 16.0
bf16 = jnp.bfloat16
f32 = jnp.float32
HIGHEST = lax.Precision.HIGHEST
VMEM = pl.BlockSpec(memory_space=pltpu.VMEM)


def ahead(x, axis, k):
    n = lax.axis_size(axis)
    return lax.ppermute(x, axis, [((i + k) % n, i) for i in range(n)])


def around(x, axis):
    n = lax.axis_size(axis)
    blocks = [x] + [ahead(x, axis, k) for k in range(1, n)]
    start = (n - lax.axis_index(axis)) % n * x.shape[0]
    return lax.dynamic_slice_in_dim(jnp.concatenate(blocks + blocks), start, n * x.shape[0], 0)


def to_all(x, axes):
    copies = jnp.broadcast_to(x, (lax.axis_size(axes), *x.shape))
    return lax.all_to_all(copies, axes, split_axis=0, concat_axis=0, tiled=True)


def epoch_matrix(gain_row):
    n = gain_row.shape[-1]
    s = lax.broadcasted_iota(jnp.int32, (n, n), 0)
    t = lax.broadcasted_iota(jnp.int32, (n, n), 1)
    base = epoch_offset / ((s + t).astype(f32) + epoch_offset)
    return base + jnp.where(s == t, gain_row, 0.0)


def prepare(observed, lengths, features, length_scale, epoch_gain):
    own, width = observed.shape
    n = features.shape[1]
    copies = 8

    def body(obs_ref, len_ref, feat_ref, scale_ref, gain_ref, v_ref, mask_ref, ek_ref, out_ref, left_ref):
        lane = lax.broadcasted_iota(jnp.int32, (own, width), 1)
        mask = (lane < len_ref[...]).astype(f32)
        v = mask * obs_ref[...]
        ek = epoch_matrix(gain_ref[...])
        mask_ref[...] = mask
        v_ref[...] = v
        ek_ref[...] = ek
        w = jnp.dot(v, ek, precision=HIGHEST, preferred_element_type=f32).astype(bf16)
        scaled = feat_ref[...] * (math.sqrt(math.log2(math.e)) / scale_ref[...])
        hi = scaled.astype(bf16)
        hi32 = hi.astype(f32)
        lo = (scaled - hi32).astype(bf16)
        lo32 = lo.astype(f32)
        sq = jnp.sum(hi32 * (-0.5 * hi32 - lo32), axis=1, keepdims=True)
        sq0 = sq.astype(bf16).astype(f32)
        sq1 = (sq - sq0).astype(bf16).astype(f32)
        sq2 = sq - sq0 - sq1
        col = lax.broadcasted_iota(jnp.int32, (n, width), 1)
        row = lax.broadcasted_iota(jnp.int32, (n, width), 0)
        first, second, third = (col == row + k * n for k in range(3))

        def place(x, *where):
            spot = either(where).astype(bf16)
            return jnp.dot(x, spot, preferred_element_type=f32)

        def tail(x, at):
            for k, piece in enumerate((sq0, sq1, sq2)):
                x = jnp.where(lane == at + k, piece, x)
            return x

        ones = ((lane >= 3 * n) & (lane < 3 * n + 6)).astype(f32)
        left = tail(place(hi, first, second) + place(lo, third) + ones, 3 * n)
        right = tail(place(hi, first, third) + place(lo, second) + ones, 3 * n + 3)
        left_ref[...] = left.astype(bf16)
        right = right.astype(bf16)
        for k in range(copies):
            out_ref[k, :own, :] = w
            out_ref[k, own:, :] = right

    return pl.pallas_call(
        body,
        out_shape=(
            jax.ShapeDtypeStruct((own, width), f32),
            jax.ShapeDtypeStruct((own, width), f32),
            jax.ShapeDtypeStruct((width, width), f32),
            jax.ShapeDtypeStruct((copies, 2 * own, width), bf16),
            jax.ShapeDtypeStruct((own, width), bf16),
        ),
        in_specs=[VMEM] * 5,
        out_specs=(VMEM,) * 5,
        name="prepare",
    )(observed, lengths[:, None], features, length_scale[None, :], epoch_gain[None, :])


def either(conditions):
    out = conditions[0]
    for c in conditions[1:]:
        out = out | c
    return out


def finish(moments, v0, v1, v2):
    def body(m_ref, v0_ref, v1_ref, v2_ref, x_ref, r_ref):
        m = jnp.sum(jnp.sum(m_ref[...], axis=0), axis=1, keepdims=True)
        m0, m1, m2, m3 = (m[k : k + 1, :] for k in range(4))
        alpha = m0 / m1
        norm = m0 + alpha * (alpha * m2 - 2.0 * m1)
        keep = 1.0 + norm / m0
        curve = keep * (keep * m1 - 2.0 * alpha * m2) + alpha * alpha * m3
        again = norm / curve
        on0 = alpha + again * keep
        on1 = again * alpha
        v0, v1 = v0_ref[...], v1_ref[...]
        x_ref[...] = on0 * v0 - on1 * v1
        r_ref[...] = v0 - on0 * v1 + on1 * v2_ref[...]

    out = jax.ShapeDtypeStruct(v0.shape, f32)
    return pl.pallas_call(
        body,
        out_shape=(out, out),
        in_specs=[VMEM] * 4,
        out_specs=(VMEM,) * 2,
        name="finish",
    )(moments, v0, v1, v2)


def block_kernel(left, right):
    e = lax.dot_general(left, right, (((1,), (1,)), ((), ())), preferred_element_type=f32)
    return jnp.exp2(jnp.minimum(e, 0.0)).astype(bf16)


def per_device(observed, lengths, features, length_scale, epoch_gain):
    own, width = observed.shape
    v0, mask, ek, outgoing, left = prepare(observed, lengths, features, length_scale, epoch_gain)
    got = lax.all_to_all(outgoing, Z, split_axis=0, concat_axis=0, tiled=True)
    lefts = around(around(left, Y), X)
    here = got.reshape(got.shape[0], 2, own, width)
    there = ahead(here, C, 1)
    k_here = block_kernel(lefts, here[:, 1].reshape(-1, width))
    k_there = block_kernel(lefts, there[:, 1].reshape(-1, width))

    def product(w_here, w_there):
        part = jnp.dot(k_here, w_here, preferred_element_type=f32)
        part = part + jnp.dot(k_there, w_there, preferred_element_type=f32)
        part = part.reshape(-1, own, width)
        got = lax.all_to_all(part, (X, Y), split_axis=0, concat_axis=0, tiled=True)
        return jnp.sum(got, axis=0)

    p = product(here[:, 0].reshape(-1, width), there[:, 0].reshape(-1, width))
    v1 = mask * p + noise_level * v0
    w = jnp.dot(mask * v1, ek, precision=HIGHEST, preferred_element_type=f32).astype(bf16)
    w_here = to_all(w, Z).reshape(-1, width)
    p = product(w_here, ahead(w_here, C, 1))
    v2 = mask * p + noise_level * v1
    m = jnp.concatenate(
        [jnp.sum(a * b, axis=0, keepdims=True) for a, b in ((v0, v0), (v0, v1), (v1, v1), (v1, v2))]
    )
    m = jnp.sum(to_all(m, (Y, X)), axis=0)
    return finish(to_all(m, (Z, C)), v0, v1, v2)


def solution(mesh):
    torus = Mesh(mesh.devices.reshape(4, 2, 8, 4), ALL)
    in_specs = (P(ALL, None), P(ALL), P(ALL, None), P(), P())
    out_specs = (P(ALL, None), P(ALL, None))
    return jax.shard_map(
        per_device, mesh=torus, in_specs=in_specs, out_specs=out_specs, check_vma=False
    )
```

time: 212 us -> 112 us (0.53)
  the two profiles are of different devices: /device:TPU:32 before, /device:TPU:1 now
where the time goes in v1:
time: 112 us; the launch traced here: 111 us
  blocking collectives  63.6 us (57%)
  starting transfers between devices  25.5 us (23%)
  waiting for transfers between devices  9.61 us (9%)
  local copies, waits for them, and re-layouts  4.5 us (4%)
  Pallas kernels  3.38 us (3%)
  matrix products  2.88 us (3%)
    all_to_all x3, blocking collectives, to_all(): return lax.all_to_all(copies, axes, split_axis=0, concat_axis=0, tiled=True)  36 us
    all_to_all x2, blocking collectives, product(): got = lax.all_to_all(part, (X, Y), split_axis=0, concat_axis=0, tiled=True)  27.5 us
    ppermute x8, starting transfers between devices, ahead(): return lax.ppermute(x, axis, [((i + k) % n, i) for i in range(n)])  17.3 us
    all_to_all x1, starting transfers between devices, per_device(): got = lax.all_to_all(outgoing, Z, split_axis=0, concat_axis=0, tiled=True)  8.19 us
    ppermute x8, waiting for transfers between devices, ahead(): return lax.ppermute(x, axis, [((i + k) % n, i) for i in range(n)])  5.33 us
    all_to_all x1, waiting for transfers between devices, per_device(): got = lax.all_to_all(outgoing, Z, split_axis=0, concat_axis=0, tiled=True)  4.28 us
    unnamed x23, local copies, waits for them, and re-layouts  3.05 us
  transfers between devices with their start and end apart: 9, of which 6 were waited for; matrix products, arithmetic and copies ran while one was open for 2% of the time, Pallas kernels for 0%

profile of v1, /device:TPU:1, one launch (start us, length us, event | category | flops | bytes accessed | tf_op | source)
XLA Modules:
  0.0 111.1 jit_solution(17593501730797377026)
XLA Ops:
  0.6 1.4 %copy.11.len_ref = s32[64,1]{1,0:T(8,128)} copy(s32[64,1]{0,1:T(1,128)} %bitcast.40) | data formatting | bytes 512 | tf_op jit(solution)/shard_map/broadcast_in_dim | solution.py:104
  2.0 1.4 %copy.12.feat_ref = f32[64,32]{1,0:T(8,128)} copy(f32[64,32]{0,1:T(8,128)} %param.7) | data formatting | bytes 16384 | tf_op args[2]
  3.4 1.8 %prepare.1 = (f32[64,128]{1,0:T(8,128)}, f32[64,128]{1,0:T(8,128)}, f32[128,128]{1,0:T(8,128)}, bf16[8,128,128]{2,1,0:T(8,128)(2,1)}, bf16[64,128]{1,0:T(8,128)(2,1)}) custom-call(f32[64,128]{1,0:T(8,128)} %obs_ref.1, s32[64,1]{1,0:T(8,128)} %copy.11.len_ref, f32[64,32]{1,0:T(8,128)} %copy.12.feat_ref, f32[1,32]{1,0:T(1,128)} %bitcast.41, f32[1,128]{1,0:T(1,128)} %bitcast.42), custom_call_target="tpu_custom_call" | custom-call | tf_op jit(solution)/shard_map/prepare/pallas_call | solution.py:92
  5.2 2.1 %collective-permute-start.2 = (bf16[64,128]{1,0:T(8,128)(2,1)}, bf16[64,128]{1,0:T(8,128)(2,1)S(1)}, u32[]{:S(2)}, u32[]{:S(2)}) collective-permute-start(bf16[64,128]{1,0:T(8,128)(2,1)} %get-tuple-element.9), channel_id=1, source_target_pairs={{192,0},{0,64},{64,128},{128,192},{193,1},{1,65},{65,129},{129,193... | collective-permute-start | bytes 49160 | tf_op jit(solution)/shard_map/ppermute | solution.py:24
  7.3 2.6 %collective-permute-start.1 = (bf16[64,128]{1,0:T(8,128)(2,1)}, bf16[64,128]{1,0:T(8,128)(2,1)S(1)}, u32[]{:S(2)}, u32[]{:S(2)}) collective-permute-start(bf16[64,128]{1,0:T(8,128)(2,1)} %get-tuple-element.9), channel_id=1, source_target_pairs={{128,0},{192,64},{0,128},{64,192},{129,1},{193,65},{1,129},{65,193... | collective-permute-start | bytes 49160 | tf_op jit(solution)/shard_map/ppermute | solution.py:24
  9.9 1.1 collective-permute-start
  11.0 0.8 constant_dynamic-update-slice_fusion.7
  11.8 1.3 %collective-permute-done = bf16[64,128]{1,0:T(8,128)(2,1)S(1)} collective-permute-done((bf16[64,128]{1,0:T(8,128)(2,1)}, bf16[64,128]{1,0:T(8,128)(2,1)S(1)}, u32[]{:S(2)}, u32[]{:S(2)}) %collective-permute-start) | collective-permute-done | bytes 16416 | tf_op jit(solution)/shard_map/ppermute | solution.py:24
  13.1 0.7 constant_dynamic-update-slice_fusion.3
  13.9 2.6 %collective-permute-start.3 = (bf16[256,128]{1,0:T(8,128)(2,1)S(1)}, bf16[256,128]{1,0:T(8,128)(2,1)S(1)}, u32[]{:S(2)}, u32[]{:S(2)}) collective-permute-start(bf16[256,128]{1,0:T(8,128)(2,1)S(1)} %get-tuple-element.18), channel_id=1, source_target_pairs={{1,0},{2,1},{3,2},{0,3},{5,4},{6,5},{7,6},{4,7},{9,8},{10,9},{11,1... | collective-permute-start | bytes 196616 | tf_op jit(solution)/shard_map/ppermute | solution.py:24
  16.4 8.2 %all-to-all-start = ((bf16[8,128,128]{2,1,0:T(8,128)(2,1)}), bf16[8,128,128]{2,1,0:T(8,128)(2,1)S(1)}, u32[]{:S(2)}, u32[]{:S(2)}) async-start(bf16[8,128,128]{2,1,0:T(8,128)(2,1)} %get-tuple-element.10), calls=%async_computation | async-start | bytes 524288 | tf_op jit(solution)/shard_map/all_to_all | solution.py:147
  24.6 1.7 %collective-permute-start.4 = (bf16[256,128]{1,0:T(8,128)(2,1)S(1)}, bf16[256,128]{1,0:T(8,128)(2,1)S(1)}, u32[]{:S(2)}, u32[]{:S(2)}) collective-permute-start(bf16[256,128]{1,0:T(8,128)(2,1)S(1)} %get-tuple-element.18), channel_id=1, source_target_pairs={{2,0},{3,1},{0,2},{1,3},{6,4},{7,5},{4,6},{5,7},{10,8},{11,9},{8,1... | collective-permute-start | bytes 196616 | tf_op jit(solution)/shard_map/ppermute | solution.py:24
  26.3 3.1 %collective-permute-done.4 = bf16[256,128]{1,0:T(8,128)(2,1)S(1)} collective-permute-done((bf16[256,128]{1,0:T(8,128)(2,1)S(1)}, bf16[256,128]{1,0:T(8,128)(2,1)S(1)}, u32[]{:S(2)}, u32[]{:S(2)}) %collective-permute-start.4) | collective-permute-done | bytes 65568 | tf_op jit(solution)/shard_map/ppermute | solution.py:24
  29.7 4.3 %all-to-all-done = bf16[8,128,128]{2,1,0:T(8,128)(2,1)S(1)} async-done(((bf16[8,128,128]{2,1,0:T(8,128)(2,1)}), bf16[8,128,128]{2,1,0:T(8,128)(2,1)S(1)}, u32[]{:S(2)}, u32[]{:S(2)}) %all-to-all-start) | async-done | bytes 262176 | tf_op jit(solution)/shard_map/all_to_all | solution.py:147
  34.0 3.8 %collective-permute-start.6 = (bf16[8,2,64,128]{3,2,1,0:T(8,128)(2,1)S(1)}, bf16[8,2,64,128]{3,2,1,0:T(8,128)(2,1)S(1)}, u32[]{:S(2)}, u32[]{:S(2)}) collective-permute-start(bf16[8,2,64,128]{3,2,1,0:T(8,128)(2,1)S(1)} %bitcast.29), channel_id=1, source_target_pairs={{32,0},{0,32},{33,1},{1,33},{34,2},{2,34},{35,3},{3,35},{36,4},{4,... | collective-permute-start | bytes 786440 | tf_op jit(solution)/shard_map/ppermute | solution.py:24
  40.0 14.2 %all_to_all.30 = f32[16,64,128]{2,1,0:T(8,128)S(1)} all-to-all(f32[16,64,128]{2,1,0:T(8,128)S(1)} %bitcast.27), channel_id=1, replica_groups=mesh['y'=4,'c'=2,'z'=8,'x'=4] {'x','y'}, dimensions={0} | all-to-all | bytes 1048576 | tf_op jit(solution)/shard_map/all_to_all | solution.py:158
  54.5 12.6 %all_to_all.31 = bf16[8,64,128]{2,1,0:T(8,128)(2,1)S(1)} all-to-all(bf16[8,64,128]{2,1,0:T(8,128)(2,1)S(1)} %broadcast_in_dim.36), channel_id=1, replica_groups=mesh['y'=4,'c'=2,'z'=8,'x'=4] {'z'}, dimensions={0} | all-to-all | bytes 262144 | tf_op jit(solution)/shard_map/all_to_all | solution.py:36
  67.1 3.4 %collective-permute-start.7 = (bf16[512,128]{1,0:T(8,128)(2,1)S(1)}, bf16[512,128]{1,0:T(8,128)(2,1)S(1)}, u32[]{:S(2)}, u32[]{:S(2)}) collective-permute-start(bf16[512,128]{1,0:T(8,128)(2,1)S(1)} %bitcast.31), channel_id=1, source_target_pairs={{32,0},{0,32},{33,1},{1,33},{34,2},{2,34},{35,3},{3,35},{36,4},{4,... | collective-permute-start | bytes 393224 | tf_op jit(solution)/shard_map/ppermute | solution.py:24
  71.0 0.6 collective-permute-done.7
  71.9 13.3 %all_to_all.32 = f32[16,64,128]{2,1,0:T(8,128)S(1)} all-to-all(f32[16,64,128]{2,1,0:T(8,128)S(1)} %bitcast.26), channel_id=1, replica_groups=mesh['y'=4,'c'=2,'z'=8,'x'=4] {'x','y'}, dimensions={0} | all-to-all | bytes 1048576 | tf_op jit(solution)/shard_map/all_to_all | solution.py:158
  85.3 0.6 multiply_reduce_fusion.3
  86.0 10.0 %all_to_all.33 = f32[16,4,128]{2,1,0:T(4,128)S(1)} all-to-all(f32[16,4,128]{2,1,0:T(4,128)S(1)} %broadcast_in_dim.38), channel_id=1, replica_groups=mesh['y'=4,'c'=2,'z'=8,'x'=4] {'y','x'}, dimensions={0} | all-to-all | bytes 65536 | tf_op jit(solution)/shard_map/all_to_all | solution.py:36
  96.0 13.5 %all_to_all.34.m_ref = f32[16,4,128]{2,1,0:T(4,128)} all-to-all(f32[16,4,128]{2,1,0:T(4,128)S(1)} %broadcast_in_dim.39), channel_id=1, replica_groups=mesh['y'=4,'c'=2,'z'=8,'x'=4] {'z','c'}, dimensions={0} | all-to-all | bytes 65536 | tf_op jit(solution)/shard_map/all_to_all | solution.py:36
  109.5 1.6 %finish.1 = (f32[64,128]{1,0:T(8,128)}, f32[64,128]{1,0:T(8,128)}) custom-call(f32[16,4,128]{2,1,0:T(4,128)} %all_to_all.34.m_ref, f32[64,128]{1,0:T(8,128)} %get-tuple-element.7.v0_ref, f32[64,128]{1,0:T(8,128)} %copy-done, f32[64,128]{1,0:T(8,128)} %get-tuple-element.16.v2_ref), custom_call_target="tpu_custom_call" | custom-call | tf_op jit(solution)/shard_map/finish/pallas_call | solution.py:130
  (45 shorter events, 3.7 us)
Async XLA Ops:
  5.2 7.9 %collective-permute-start.2 = (bf16[64,128]{1,0:T(8,128)(2,1)}, bf16[64,128]{1,0:T(8,128)(2,1)S(1)}, u32[]{:S(2)}, u32[]{:S(2)}) collective-permute-start(bf16[64,128]{1,0:T(8,128)(2,1)} %get-tuple-element.9), channel_id=1, source_target_pairs={{192,0},{0,64},{64,128},{128,192},{193,1},{1,65},{65,129},{129,193... | collective-permute-start | bytes 49160 | tf_op jit(solution)/shard_map/ppermute | solution.py:24
  7.3 5.7 %collective-permute-start.1 = (bf16[64,128]{1,0:T(8,128)(2,1)}, bf16[64,128]{1,0:T(8,128)(2,1)S(1)}, u32[]{:S(2)}, u32[]{:S(2)}) collective-permute-start(bf16[64,128]{1,0:T(8,128)(2,1)} %get-tuple-element.9), channel_id=1, source_target_pairs={{128,0},{192,64},{0,128},{64,192},{129,1},{193,65},{1,129},{65,193... | collective-permute-start | bytes 49160 | tf_op jit(solution)/shard_map/ppermute | solution.py:24
  9.9 3.1 %collective-permute-start = (bf16[64,128]{1,0:T(8,128)(2,1)}, bf16[64,128]{1,0:T(8,128)(2,1)S(1)}, u32[]{:S(2)}, u32[]{:S(2)}) collective-permute-start(bf16[64,128]{1,0:T(8,128)(2,1)} %get-tuple-element.9), channel_id=1, source_target_pairs={{64,0},{128,64},{192,128},{0,192},{65,1},{129,65},{193,129},{1,193... | collective-permute-start | bytes 49160 | tf_op jit(solution)/shard_map/ppermute | solution.py:24
  13.9 12.5 %collective-permute-start.3 = (bf16[256,128]{1,0:T(8,128)(2,1)S(1)}, bf16[256,128]{1,0:T(8,128)(2,1)S(1)}, u32[]{:S(2)}, u32[]{:S(2)}) collective-permute-start(bf16[256,128]{1,0:T(8,128)(2,1)S(1)} %get-tuple-element.18), channel_id=1, source_target_pairs={{1,0},{2,1},{3,2},{0,3},{5,4},{6,5},{7,6},{4,7},{9,8},{10,9},{11,1... | collective-permute-start | bytes 196616 | tf_op jit(solution)/shard_map/ppermute | solution.py:24
  16.4 17.6 %all-to-all-start = ((bf16[8,128,128]{2,1,0:T(8,128)(2,1)}), bf16[8,128,128]{2,1,0:T(8,128)(2,1)S(1)}, u32[]{:S(2)}, u32[]{:S(2)}) async-start(bf16[8,128,128]{2,1,0:T(8,128)(2,1)} %get-tuple-element.10), calls=%async_computation | async-start | bytes 524288 | tf_op jit(solution)/shard_map/all_to_all | solution.py:147
  24.6 5.0 %collective-permute-start.5 = (bf16[256,128]{1,0:T(8,128)(2,1)S(1)}, bf16[256,128]{1,0:T(8,128)(2,1)S(1)}, u32[]{:S(2)}, u32[]{:S(2)}) collective-permute-start(bf16[256,128]{1,0:T(8,128)(2,1)S(1)} %get-tuple-element.18), channel_id=1, source_target_pairs={{3,0},{0,1},{1,2},{2,3},{7,4},{4,5},{5,6},{6,7},{11,8},{8,9},{9,10... | collective-permute-start | bytes 196616 | tf_op jit(solution)/shard_map/ppermute | solution.py:24
  24.6 4.8 %collective-permute-start.4 = (bf16[256,128]{1,0:T(8,128)(2,1)S(1)}, bf16[256,128]{1,0:T(8,128)(2,1)S(1)}, u32[]{:S(2)}, u32[]{:S(2)}) collective-permute-start(bf16[256,128]{1,0:T(8,128)(2,1)S(1)} %get-tuple-element.18), channel_id=1, source_target_pairs={{2,0},{3,1},{0,2},{1,3},{6,4},{7,5},{4,6},{5,7},{10,8},{11,9},{8,1... | collective-permute-start | bytes 196616 | tf_op jit(solution)/shard_map/ppermute | solution.py:24
  34.0 5.0 %collective-permute-start.6 = (bf16[8,2,64,128]{3,2,1,0:T(8,128)(2,1)S(1)}, bf16[8,2,64,128]{3,2,1,0:T(8,128)(2,1)S(1)}, u32[]{:S(2)}, u32[]{:S(2)}) collective-permute-start(bf16[8,2,64,128]{3,2,1,0:T(8,128)(2,1)S(1)} %bitcast.29), channel_id=1, source_target_pairs={{32,0},{0,32},{33,1},{1,33},{34,2},{2,34},{35,3},{3,35},{36,4},{4,... | collective-permute-start | bytes 786440 | tf_op jit(solution)/shard_map/ppermute | solution.py:24
  40.0 14.3 %copy-start.1 = (f32[64,128]{1,0:T(8,128)S(1)}, f32[64,128]{1,0:T(8,128)}, u32[]{:S(2)}) copy-start(f32[64,128]{1,0:T(8,128)} %get-tuple-element.7.v0_ref) | copy-start | bytes 98308
  40.0 14.3 %copy-start.2 = (f32[64,128]{1,0:T(8,128)S(1)}, f32[64,128]{1,0:T(8,128)}, u32[]{:S(2)}) copy-start(f32[64,128]{1,0:T(8,128)} %get-tuple-element.8) | copy-start | bytes 98308
  40.0 14.3 %copy-start.3 = (f32[128,128]{1,0:T(8,128)S(1)}, f32[128,128]{1,0:T(8,128)}, u32[]{:S(2)}) copy-start(f32[128,128]{1,0:T(8,128)} %get-tuple-element.11) | copy-start | bytes 196612
  54.3 31.0 %copy-start = (f32[64,128]{1,0:T(8,128)}, f32[64,128]{1,0:T(8,128)S(1)}, u32[]{:S(2)}) copy-start(f32[64,128]{1,0:T(8,128)S(1)} %multiply_add_fusion.1.v1_ref) | copy-start | bytes 98308
  67.1 4.4 %collective-permute-start.7 = (bf16[512,128]{1,0:T(8,128)(2,1)S(1)}, bf16[512,128]{1,0:T(8,128)(2,1)S(1)}, u32[]{:S(2)}, u32[]{:S(2)}) collective-permute-start(bf16[512,128]{1,0:T(8,128)(2,1)S(1)} %bitcast.31), channel_id=1, source_target_pairs={{32,0},{0,32},{33,1},{1,33},{34,2},{2,34},{35,3},{3,35},{36,4},{4,... | collective-permute-start | bytes 393224 | tf_op jit(solution)/shard_map/ppermute | solution.py:24

commit v2 on v1

v2 whole, which is shorter than its diff:
```python
import math

import jax
import jax.numpy as jnp
from jax import lax
from jax.experimental import pallas as pl
from jax.experimental.pallas import tpu as pltpu
from jax.sharding import Mesh
from jax.sharding import PartitionSpec as P

Y, C, Z, X = "y", "c", "z", "x"
ALL = (Y, C, Z, X)

noise_level = 0.3
epoch_offset = 16.0
bf16 = jnp.bfloat16
f32 = jnp.float32
HIGHEST = lax.Precision.HIGHEST
VMEM = pl.BlockSpec(memory_space=pltpu.VMEM)


def ahead(x, axis, k):
    n = lax.axis_size(axis)
    return lax.ppermute(x, axis, [((i + k) % n, i) for i in range(n)])


def around(x, axis):
    return [x] + [ahead(x, axis, k) for k in range(1, lax.axis_size(axis))]


def to_all(x, axes):
    copies = jnp.broadcast_to(x, (lax.axis_size(axes), *x.shape))
    return lax.all_to_all(copies, axes, split_axis=0, concat_axis=0, tiled=True)


def epoch_matrix(gain_row):
    n = gain_row.shape[-1]
    s = lax.broadcasted_iota(jnp.int32, (n, n), 0)
    t = lax.broadcasted_iota(jnp.int32, (n, n), 1)
    base = epoch_offset / ((s + t).astype(f32) + epoch_offset)
    return base + jnp.where(s == t, gain_row, 0.0)


def column(row):
    n = row.shape[-1]
    eye = lax.broadcasted_iota(jnp.int32, (n, n), 0) == lax.broadcasted_iota(jnp.int32, (n, n), 1)
    return jnp.sum(jnp.where(eye, row, 0.0), axis=1, keepdims=True)


def sides(features, length_scale, width):
    n, own = features.shape
    scaled = features * column(math.sqrt(math.log2(math.e)) / length_scale)
    hi = scaled.astype(bf16)
    lo = (scaled - hi.astype(f32)).astype(bf16)
    col = lax.broadcasted_iota(jnp.int32, (n, width), 1)
    row = lax.broadcasted_iota(jnp.int32, (n, width), 0)
    first, second, third = (col == row + k * n for k in range(3))
    lane = lax.broadcasted_iota(jnp.int32, (own, width), 1)

    def place(x, where):
        spot = jnp.where(where, 1.0, 0.0).astype(bf16)
        return lax.dot_general(x, spot, (((0,), (0,)), ((), ())), preferred_element_type=f32)

    left = place(hi, first | second) + place(lo, third)
    right = place(hi, first | third) + place(lo, second)
    sq = -0.5 * jnp.sum(left * right, axis=1, keepdims=True)
    sq0 = sq.astype(bf16).astype(f32)
    sq1 = (sq - sq0).astype(bf16).astype(f32)
    sq2 = sq - sq0 - sq1

    def tail(x, squares, ones):
        for k, piece in enumerate((sq0, sq1, sq2)):
            x = jnp.where(lane == squares + k, piece, x)
        return jnp.where((lane >= ones) & (lane < ones + 3), 1.0, x).astype(bf16)

    return tail(left, 3 * n, 3 * n + 3), tail(right, 3 * n + 3, 3 * n)


def prepare(observed, lengths, features, length_scale, epoch_gain, copies):
    own, width = observed.shape

    def body(obs_ref, len_ref, feat_ref, scale_ref, gain_ref, v_ref, mask_ref, ek_ref, out_ref):
        lane = lax.broadcasted_iota(jnp.int32, (own, width), 1).astype(f32)
        mask = (lane < column(len_ref[...].astype(f32))).astype(f32)
        v = mask * obs_ref[...]
        ek = epoch_matrix(gain_ref[...])
        mask_ref[...] = mask
        v_ref[...] = v
        ek_ref[...] = ek
        w = jnp.dot(v, ek, precision=HIGHEST, preferred_element_type=f32).astype(bf16)
        right = sides(feat_ref[...], scale_ref[...], width)[1]
        for k in range(copies):
            out_ref[k, :own, :] = w
            out_ref[k, own:, :] = right

    return pl.pallas_call(
        body,
        out_shape=(
            jax.ShapeDtypeStruct((own, width), f32),
            jax.ShapeDtypeStruct((own, width), f32),
            jax.ShapeDtypeStruct((width, width), f32),
            jax.ShapeDtypeStruct((copies, 2 * own, width), bf16),
        ),
        in_specs=[VMEM] * 5,
        out_specs=(VMEM,) * 4,
        name="prepare",
    )(observed, lengths, features, length_scale, epoch_gain)


def left_side(features, length_scale, width):
    def body(feat_ref, scale_ref, left_ref):
        left_ref[...] = sides(feat_ref[...], scale_ref[...], width)[0]

    return pl.pallas_call(
        body,
        out_shape=jax.ShapeDtypeStruct((features.shape[1], width), bf16),
        in_specs=[VMEM] * 2,
        out_specs=VMEM,
        name="left_side",
    )(features, length_scale)


def arrange(blocks, here):
    ny = len(blocks)
    rows, width = blocks[0].shape
    nx = 4
    own = rows // nx

    def body(here_ref, *refs):
        out_ref = refs[-1]
        for j in range(ny):
            for i in range(nx):
                slot = lax.rem(here_ref[0] + j, ny) * nx + lax.rem(here_ref[1] + i, nx)
                out_ref[slot] = refs[j][i * own : (i + 1) * own, :]

    return pl.pallas_call(
        body,
        out_shape=jax.ShapeDtypeStruct((ny * nx, own, width), bf16),
        in_specs=[pl.BlockSpec(memory_space=pltpu.SMEM)] + [VMEM] * ny,
        out_specs=VMEM,
        name="arrange",
    )(here, *blocks).reshape(-1, width)


def measure(got, mask, v0, v1):
    def body(got_ref, mask_ref, v0_ref, v1_ref, v2_ref, m_ref):
        v0, v1 = v0_ref[...], v1_ref[...]
        v2 = mask_ref[...] * jnp.sum(got_ref[...], axis=0) + noise_level * v1
        v2_ref[...] = v2
        lane = lax.broadcasted_iota(jnp.int32, m_ref.shape, 1)
        m = jnp.zeros(m_ref.shape, f32)
        for k, (a, b) in enumerate(((v0, v0), (v0, v1), (v1, v1), (v1, v2))):
            total = jnp.sum(jnp.sum(a * b, axis=0, keepdims=True), axis=1, keepdims=True)
            m = jnp.where(lane == k, total, m)
        m_ref[...] = m

    own, width = v0.shape
    return pl.pallas_call(
        body,
        out_shape=(jax.ShapeDtypeStruct((own, width), f32), jax.ShapeDtypeStruct((1, width), f32)),
        in_specs=[VMEM] * 4,
        out_specs=(VMEM,) * 2,
        name="measure",
    )(got, mask, v0, v1)


def finish(moments, v0, v1, v2):
    def body(m_ref, v0_ref, v1_ref, v2_ref, x_ref, r_ref):
        m = jnp.sum(m_ref[...], axis=0, keepdims=True)
        lane = lax.broadcasted_iota(jnp.int32, m.shape, 1)

        def moment(k):
            return jnp.sum(jnp.where(lane == k, m, 0.0), axis=1, keepdims=True)

        m0, m1, m2, m3 = (moment(k) for k in range(4))
        alpha = m0 / m1
        norm = m0 + alpha * (alpha * m2 - 2.0 * m1)
        keep = 1.0 + norm / m0
        curve = keep * (keep * m1 - 2.0 * alpha * m2) + alpha * alpha * m3
        again = norm / curve
        on0 = alpha + again * keep
        on1 = again * alpha
        v0, v1 = v0_ref[...], v1_ref[...]
        x_ref[...] = on0 * v0 - on1 * v1
        r_ref[...] = v0 - on0 * v1 + on1 * v2_ref[...]

    out = jax.ShapeDtypeStruct(v0.shape, f32)
    return pl.pallas_call(
        body,
        out_shape=(out, out),
        in_specs=[VMEM] * 4,
        out_specs=(VMEM,) * 2,
        name="finish",
    )(moments, v0, v1, v2)


def block_kernel(left, right):
    e = lax.dot_general(left, right, (((1,), (1,)), ((), ())), preferred_element_type=f32)
    return jnp.exp2(jnp.minimum(e, 0.0)).astype(bf16)


def per_device(observed, lengths, features, length_scale, epoch_gain):
    own, width = observed.shape
    features, length_scale = features.T, length_scale[None, :]
    v0, mask, ek, outgoing = prepare(
        observed, lengths[None, :], features, length_scale, epoch_gain[None, :], lax.axis_size(Z)
    )
    here = lax.all_to_all(outgoing, Z, split_axis=0, concat_axis=0, tiled=True)
    left = left_side(features, length_scale, width)
    line = jnp.concatenate(around(left, X))
    lefts = arrange(around(line, Y), jnp.stack([lax.axis_index(Y), lax.axis_index(X)]))
    there = ahead(here, C, 1)
    k_here = block_kernel(lefts, here[:, own:].reshape(-1, width))
    k_there = block_kernel(lefts, there[:, own:].reshape(-1, width))

    def product(w_here, w_there):
        part = jnp.dot(k_here, w_here, preferred_element_type=f32)
        part = part + jnp.dot(k_there, w_there, preferred_element_type=f32)
        return lax.all_to_all(
            part.reshape(-1, own, width), (Y, X), split_axis=0, concat_axis=0, tiled=True
        )

    got = product(here[:, :own].reshape(-1, width), there[:, :own].reshape(-1, width))
    v1 = mask * jnp.sum(got, axis=0) + noise_level * v0
    w = jnp.dot(mask * v1, ek, precision=HIGHEST, preferred_element_type=f32).astype(bf16)
    w_here = to_all(w, Z).reshape(-1, width)
    v2, m = measure(product(w_here, ahead(w_here, C, 1)), mask, v0, v1)
    m = to_all(m + ahead(m, C, 1), (Y, Z, X))
    return finish(m.reshape(-1, width), v0, v1, v2)


def solution(mesh):
    torus = Mesh(mesh.devices.reshape(4, 2, 8, 4), ALL)
    in_specs = (P(ALL, None), P(ALL), P(ALL, None), P(), P())
    out_specs = (P(ALL, None), P(ALL, None))
    return jax.shard_map(
        per_device, mesh=torus, in_specs=in_specs, out_specs=out_specs, check_vma=False
    )
```

time: 112 us -> 112 us (level)
  Pallas kernels: 3.38 us -> 8.58 us
  local copies, waits for them, and re-layouts: 4.5 us -> 0.73 us
  waiting for transfers between devices: 9.61 us -> 5.92 us
  starting transfers between devices: 25.5 us -> 27.3 us
  blocking collectives: 63.6 us -> 62.3 us
  other arithmetic: 0.74 us -> 2.01 us
    pallas_call x0 -> x3, Pallas kernels: none -> 5.07 us  [the longest x1 1.71 us: measure(): pl.pallas_call(body, out_shape=(jax.ShapeDtypeStruct((own, width), f32),...]
    all_to_all x3 -> x2, blocking collectives: 36 us -> 31.6 us  [to_all(): return lax.all_to_all(copies, axes, split_axis=0, concat_axis=0, tiled=True)]
    all_to_all x1, waiting for transfers between devices: 4.28 us -> 0.01 us  [per_device(): here = lax.all_to_all(outgoing, Z, split_axis=0, concat_axis=0, tiled=True)]
    all_to_all x2, blocking collectives: 27.5 us -> 30.6 us  [product(): lax.all_to_all(part.reshape(-1, own, width), (Y, X), split_axis=0, concat...]
    unnamed x23 -> x18, local copies, waits for them, and re-layouts: 3.05 us -> 0.64 us
    broadcast_in_dim x1 -> x0, local copies, waits for them, and re-layouts: 1.36 us -> none  [prepare(): lengths[:, None]]
    ppermute x8 -> x9, starting transfers between devices: 17.3 us -> 18.3 us  [ahead(): return lax.ppermute(x, axis, [((i + k) % n, i) for i in range(n)])]
    ppermute x8 -> x9, waiting for transfers between devices: 5.33 us -> 5.92 us  [ahead(): return lax.ppermute(x, axis, [((i + k) % n, i) for i in range(n)])]
  transfers between devices with their start and end apart: 9 -> 10, of which waited for: 6 -> 7; matrix products, arithmetic and copies ran while one was open for 2% -> 2% of each run, Pallas kernels for 0% -> 3%
where the time goes in v2:
time: 112 us; the launch traced here: 111 us
  blocking collectives  62.3 us (56%)
  starting transfers between devices  27.3 us (24%)
  Pallas kernels  8.58 us (8%)
  waiting for transfers between devices  5.92 us (5%)
  matrix products  3.84 us (3%)
  other arithmetic  2.01 us (2%)
    all_to_all x2, blocking collectives, to_all(): return lax.all_to_all(copies, axes, split_axis=0, concat_axis=0, tiled=True)  31.6 us
    all_to_all x2, blocking collectives, product(): lax.all_to_all(part.reshape(-1, own, width), (Y, X), split_axis=0, concat...  30.6 us
    ppermute x9, starting transfers between devices, ahead(): return lax.ppermute(x, axis, [((i + k) % n, i) for i in range(n)])  18.3 us
    all_to_all x1, starting transfers between devices, per_device(): here = lax.all_to_all(outgoing, Z, split_axis=0, concat_axis=0, tiled=True)  9.01 us
    ppermute x9, waiting for transfers between devices, ahead(): return lax.ppermute(x, axis, [((i + k) % n, i) for i in range(n)])  5.92 us
  transfers between devices with their start and end apart: 10, of which 7 were waited for; matrix products, arithmetic and copies ran while one was open for 2% of the time, Pallas kernels for 3%

profile of v2, /device:TPU:1, one launch (start us, length us, event | category | flops | bytes accessed | tf_op | source)
XLA Modules:
  0.0 111.4 jit_solution(9171029360396568085)
XLA Ops:
  0.6 1.9 %prepare.1 = (f32[64,128]{1,0:T(8,128)}, f32[64,128]{1,0:T(8,128)}, f32[128,128]{1,0:T(8,128)}, bf16[8,128,128]{2,1,0:T(8,128)(2,1)}) custom-call(f32[64,128]{1,0:T(8,128)} %obs_ref.1, s32[1,64]{1,0:T(1,128)} %bitcast.45, f32[32,64]{1,0:T(8,128)} %bitcast.41, f32[1,32]{1,0:T(1,128)} %bitcast.43, f32[1,128]{1,0:T(1,128)} %bitcast.46), custom_call_target="tpu_custom_call" | custom-call | tf_op jit(solution)/shard_map/prepare/pallas_call | solution.py:96
  2.5 9.0 %all-to-all-start = ((bf16[8,128,128]{2,1,0:T(8,128)(2,1)}), bf16[8,128,128]{2,1,0:T(8,128)(2,1)S(1)}, u32[]{:S(2)}, u32[]{:S(2)}) async-start(bf16[8,128,128]{2,1,0:T(8,128)(2,1)} %get-tuple-element.8), calls=%async_computation | async-start | bytes 524288 | tf_op jit(solution)/shard_map/all_to_all | solution.py:208
  11.5 1.7 %left_side.1 = bf16[64,128]{1,0:T(8,128)(2,1)} custom-call(f32[32,64]{1,0:T(8,128)} %bitcast.42, f32[1,32]{1,0:T(1,128)} %bitcast.44), custom_call_target="tpu_custom_call" | custom-call | tf_op jit(solution)/shard_map/left_side/pallas_call | solution.py:114
  13.2 1.2 %collective-permute-start.2 = (bf16[64,128]{1,0:T(8,128)(2,1)}, bf16[64,128]{1,0:T(8,128)(2,1)S(1)}, u32[]{:S(2)}, u32[]{:S(2)}) collective-permute-start(bf16[64,128]{1,0:T(8,128)(2,1)} %left_side.1), channel_id=1, source_target_pairs={{3,0},{0,1},{1,2},{2,3},{7,4},{4,5},{5,6},{6,7},{11,8},{8,9},{9,10... | collective-permute-start | bytes 49160 | tf_op jit(solution)/shard_map/ppermute | solution.py:24
  14.4 2.5 %collective-permute-start.1 = (bf16[64,128]{1,0:T(8,128)(2,1)}, bf16[64,128]{1,0:T(8,128)(2,1)S(1)}, u32[]{:S(2)}, u32[]{:S(2)}) collective-permute-start(bf16[64,128]{1,0:T(8,128)(2,1)} %left_side.1), channel_id=1, source_target_pairs={{2,0},{3,1},{0,2},{1,3},{6,4},{7,5},{4,6},{5,7},{10,8},{11,9},{8,1... | collective-permute-start | bytes 49160 | tf_op jit(solution)/shard_map/ppermute | solution.py:24
  16.9 1.2 %collective-permute-start = (bf16[64,128]{1,0:T(8,128)(2,1)}, bf16[64,128]{1,0:T(8,128)(2,1)S(1)}, u32[]{:S(2)}, u32[]{:S(2)}) collective-permute-start(bf16[64,128]{1,0:T(8,128)(2,1)} %left_side.1), channel_id=1, source_target_pairs={{1,0},{2,1},{3,2},{0,3},{5,4},{6,5},{7,6},{4,7},{9,8},{10,9},{11,1... | collective-permute-start | bytes 49160 | tf_op jit(solution)/shard_map/ppermute | solution.py:24
  18.1 1.0 collective-permute-done.1
  19.0 0.9 collective-permute-done
  20.7 1.3 %collective-permute-start.5 = (bf16[256,128]{1,0:T(8,128)(2,1)S(1)}, bf16[256,128]{1,0:T(8,128)(2,1)S(1)}, u32[]{:S(2)}, u32[]{:S(2)}) collective-permute-start(bf16[256,128]{1,0:T(8,128)(2,1)S(1)} %pad_maximum_fusion.refs_0_), channel_id=1, source_target_pairs={{192,0},{0,64},{64,128},{128,192},{193,1},{1,65},{65,129},{129,193... | collective-permute-start | bytes 196616 | tf_op jit(solution)/shard_map/ppermute | solution.py:24
  22.0 2.6 %collective-permute-start.4 = (bf16[256,128]{1,0:T(8,128)(2,1)S(1)}, bf16[256,128]{1,0:T(8,128)(2,1)S(1)}, u32[]{:S(2)}, u32[]{:S(2)}) collective-permute-start(bf16[256,128]{1,0:T(8,128)(2,1)S(1)} %pad_maximum_fusion.refs_0_), channel_id=1, source_target_pairs={{128,0},{192,64},{0,128},{64,192},{129,1},{193,65},{1,129},{65,193... | collective-permute-start | bytes 196616 | tf_op jit(solution)/shard_map/ppermute | solution.py:24
  24.6 1.1 collective-permute-start.3
  27.0 1.1 collective-permute-done.3.refs_1_
  28.7 1.7 %arrange.1 = bf16[16,64,128]{2,1,0:T(8,128)(2,1)} custom-call(s32[2]{0:T(128)} %pad_add_fusion.here_ref, bf16[256,128]{1,0:T(8,128)(2,1)} %copy-done.4, bf16[256,128]{1,0:T(8,128)(2,1)} %copy-done.7, bf16[256,128]{1,0:T(8,128)(2,1)} %copy-done.6, bf16[256,128]{1,0:T(8,128)(2,1)} %copy-done.5), custom_call_target="tpu_custom_call" | custom-call | tf_op jit(solution)/shard_map/arrange/pallas_call | solution.py:136
  30.4 1.4 %exponential_convert_fusion.1 = bf16[1024,512]{1,0:T(8,128)(2,1)S(1)} fusion(bf16[1024,128]{1,0:T(8,128)(2,1)} %bitcast.36, bf16[512,128]{1,0:T(8,128)(2,1)S(1)} %bitcast.40), kind=kOutput, calls=%fused_computation.1 | convolution fusion | flops 135790592 | bytes 1441792 | tf_op jit(solution)/shard_map/dot_general | solution.py:198
  31.8 3.9 %collective-permute-start.6 = (bf16[8,128,128]{2,1,0:T(8,128)(2,1)S(1)}, bf16[8,128,128]{2,1,0:T(8,128)(2,1)S(1)}, u32[]{:S(2)}, u32[]{:S(2)}) collective-permute-start(bf16[8,128,128]{2,1,0:T(8,128)(2,1)S(1)} %all-to-all-done), channel_id=1, source_target_pairs={{32,0},{0,32},{33,1},{1,33},{34,2},{2,34},{35,3},{3,35},{36,4},{4,... | collective-permute-start | bytes 786440 | tf_op jit(solution)/shard_map/ppermute | solution.py:24
  37.8 16.4 %all_to_all.25 = f32[16,64,128]{2,1,0:T(8,128)S(1)} all-to-all(f32[16,64,128]{2,1,0:T(8,128)S(1)} %bitcast.31), channel_id=1, replica_groups=mesh['y'=4,'c'=2,'z'=8,'x'=4] {'y','x'}, dimensions={0} | all-to-all | bytes 1048576 | tf_op jit(solution)/shard_map/all_to_all | solution.py:219
  54.5 14.8 %all_to_all.26 = bf16[8,64,128]{2,1,0:T(8,128)(2,1)S(1)} all-to-all(bf16[8,64,128]{2,1,0:T(8,128)(2,1)S(1)} %broadcast_in_dim.18), channel_id=1, replica_groups=mesh['y'=4,'c'=2,'z'=8,'x'=4] {'z'}, dimensions={0} | all-to-all | bytes 262144 | tf_op jit(solution)/shard_map/all_to_all | solution.py:33
  69.3 3.1 %collective-permute-start.7 = (bf16[512,128]{1,0:T(8,128)(2,1)S(1)}, bf16[512,128]{1,0:T(8,128)(2,1)S(1)}, u32[]{:S(2)}, u32[]{:S(2)}) collective-permute-start(bf16[512,128]{1,0:T(8,128)(2,1)S(1)} %bitcast.33), channel_id=1, source_target_pairs={{32,0},{0,32},{33,1},{1,33},{34,2},{2,34},{35,3},{3,35},{36,4},{4,... | collective-permute-start | bytes 393224 | tf_op jit(solution)/shard_map/ppermute | solution.py:24
  73.8 14.3 %all_to_all.27.got_ref = f32[16,64,128]{2,1,0:T(8,128)} all-to-all(f32[16,64,128]{2,1,0:T(8,128)S(1)} %bitcast.30), channel_id=1, replica_groups=mesh['y'=4,'c'=2,'z'=8,'x'=4] {'y','x'}, dimensions={0} | all-to-all | bytes 1048576 | tf_op jit(solution)/shard_map/all_to_all | solution.py:219
  88.1 1.7 %measure.1 = (f32[64,128]{1,0:T(8,128)}, f32[1,128]{1,0:T(1,128)}) custom-call(f32[16,64,128]{2,1,0:T(8,128)} %all_to_all.27.got_ref, f32[64,128]{1,0:T(8,128)} %get-tuple-element.9.mask_ref, f32[64,128]{1,0:T(8,128)} %get-tuple-element.10.v0_ref, f32[64,128]{1,0:T(8,128)} %copy-done), custom_call_target="tpu_custom_call" | custom-call | tf_op jit(solution)/shard_map/measure/pallas_call | solution.py:158
  89.8 1.5 %collective-permute-start.8 = (f32[1,128]{1,0:T(1,128)}, f32[1,128]{1,0:T(1,128)S(1)}, u32[]{:S(2)}, u32[]{:S(2)}) collective-permute-start(f32[1,128]{1,0:T(1,128)} %get-tuple-element.12), channel_id=1, source_target_pairs={{32,0},{0,32},{33,1},{1,33},{34,2},{2,34},{35,3},{3,35},{36,4},{4,... | collective-permute-start | bytes 1544 | tf_op jit(solution)/shard_map/ppermute | solution.py:24
  91.3 1.0 collective-permute-done.8
  92.9 16.9 %all_to_all.28 = f32[128,1,128]{2,1,0:T(1,128)} all-to-all(f32[128,1,128]{2,1,0:T(1,128)S(1)} %broadcast_in_dim.19), channel_id=1, replica_groups=mesh['y'=4,'c'=2,'z'=8,'x'=4] {'y','z','x'}, dimensions={0} | all-to-all | bytes 131072 | tf_op jit(solution)/shard_map/all_to_all | solution.py:33
  109.8 1.6 %finish.1 = (f32[64,128]{1,0:T(8,128)}, f32[64,128]{1,0:T(8,128)}) custom-call(f32[128,128]{1,0:T(8,128)} %bitcast.38, f32[64,128]{1,0:T(8,128)} %get-tuple-element.10.v0_ref, f32[64,128]{1,0:T(8,128)} %copy-done, f32[64,128]{1,0:T(8,128)} %get-tuple-element.13.v2_ref), custom_call_target="tpu_custom_call" | custom-call | tf_op jit(solution)/shard_map/finish/pallas_call | solution.py:188
  (39 shorter events, 7.1 us)
Async XLA Ops:
  2.5 27.8 %all-to-all-start = ((bf16[8,128,128]{2,1,0:T(8,128)(2,1)}), bf16[8,128,128]{2,1,0:T(8,128)(2,1)S(1)}, u32[]{:S(2)}, u32[]{:S(2)}) async-start(bf16[8,128,128]{2,1,0:T(8,128)(2,1)} %get-tuple-element.8), calls=%async_computation | async-start | bytes 524288 | tf_op jit(solution)/shard_map/all_to_all | solution.py:208
  13.2 4.8 %collective-permute-start.2 = (bf16[64,128]{1,0:T(8,128)(2,1)}, bf16[64,128]{1,0:T(8,128)(2,1)S(1)}, u32[]{:S(2)}, u32[]{:S(2)}) collective-permute-start(bf16[64,128]{1,0:T(8,128)(2,1)} %left_side.1), channel_id=1, source_target_pairs={{3,0},{0,1},{1,2},{2,3},{7,4},{4,5},{5,6},{6,7},{11,8},{8,9},{9,10... | collective-permute-start | bytes 49160 | tf_op jit(solution)/shard_map/ppermute | solution.py:24
  14.4 4.6 %collective-permute-start.1 = (bf16[64,128]{1,0:T(8,128)(2,1)}, bf16[64,128]{1,0:T(8,128)(2,1)S(1)}, u32[]{:S(2)}, u32[]{:S(2)}) collective-permute-start(bf16[64,128]{1,0:T(8,128)(2,1)} %left_side.1), channel_id=1, source_target_pairs={{2,0},{3,1},{0,2},{1,3},{6,4},{7,5},{4,6},{5,7},{10,8},{11,9},{8,1... | collective-permute-start | bytes 49160 | tf_op jit(solution)/shard_map/ppermute | solution.py:24
  16.9 3.1 %collective-permute-start = (bf16[64,128]{1,0:T(8,128)(2,1)}, bf16[64,128]{1,0:T(8,128)(2,1)S(1)}, u32[]{:S(2)}, u32[]{:S(2)}) collective-permute-start(bf16[64,128]{1,0:T(8,128)(2,1)} %left_side.1), channel_id=1, source_target_pairs={{1,0},{2,1},{3,2},{0,3},{5,4},{6,5},{7,6},{4,7},{9,8},{10,9},{11,1... | collective-permute-start | bytes 49160 | tf_op jit(solution)/shard_map/ppermute | solution.py:24
  20.7 7.3 %copy-start.4 = (bf16[256,128]{1,0:T(8,128)(2,1)}, bf16[256,128]{1,0:T(8,128)(2,1)S(1)}, u32[]{:S(2)}) copy-start(bf16[256,128]{1,0:T(8,128)(2,1)S(1)} %pad_maximum_fusion.refs_0_) | copy-start | bytes 196612
  20.7 5.6 %collective-permute-start.5 = (bf16[256,128]{1,0:T(8,128)(2,1)S(1)}, bf16[256,128]{1,0:T(8,128)(2,1)S(1)}, u32[]{:S(2)}, u32[]{:S(2)}) collective-permute-start(bf16[256,128]{1,0:T(8,128)(2,1)S(1)} %pad_maximum_fusion.refs_0_), channel_id=1, source_target_pairs={{192,0},{0,64},{64,128},{128,192},{193,1},{1,65},{65,129},{129,193... | collective-permute-start | bytes 196616 | tf_op jit(solution)/shard_map/ppermute | solution.py:24
  22.0 5.0 %collective-permute-start.4 = (bf16[256,128]{1,0:T(8,128)(2,1)S(1)}, bf16[256,128]{1,0:T(8,128)(2,1)S(1)}, u32[]{:S(2)}, u32[]{:S(2)}) collective-permute-start(bf16[256,128]{1,0:T(8,128)(2,1)S(1)} %pad_maximum_fusion.refs_0_), channel_id=1, source_target_pairs={{128,0},{192,64},{0,128},{64,192},{129,1},{193,65},{1,129},{65,193... | collective-permute-start | bytes 196616 | tf_op jit(solution)/shard_map/ppermute | solution.py:24
  24.6 3.4 %collective-permute-start.3 = (bf16[256,128]{1,0:T(8,128)(2,1)S(1)}, bf16[256,128]{1,0:T(8,128)(2,1)S(1)}, u32[]{:S(2)}, u32[]{:S(2)}) collective-permute-start(bf16[256,128]{1,0:T(8,128)(2,1)S(1)} %pad_maximum_fusion.refs_0_), channel_id=1, source_target_pairs={{64,0},{128,64},{192,128},{0,192},{65,1},{129,65},{193,129},{1,193... | collective-permute-start | bytes 196616 | tf_op jit(solution)/shard_map/ppermute | solution.py:24
  26.3 1.8 %copy-start.5 = (bf16[256,128]{1,0:T(8,128)(2,1)}, bf16[256,128]{1,0:T(8,128)(2,1)S(1)}, u32[]{:S(2)}) copy-start(bf16[256,128]{1,0:T(8,128)(2,1)S(1)} %collective-permute-done.5.refs_3_) | copy-start | bytes 196612
  27.0 1.1 copy-start.6
  28.1 0.6 copy-start.7
  31.8 5.0 %collective-permute-start.6 = (bf16[8,128,128]{2,1,0:T(8,128)(2,1)S(1)}, bf16[8,128,128]{2,1,0:T(8,128)(2,1)S(1)}, u32[]{:S(2)}, u32[]{:S(2)}) collective-permute-start(bf16[8,128,128]{2,1,0:T(8,128)(2,1)S(1)} %all-to-all-done), channel_id=1, source_target_pairs={{32,0},{0,32},{33,1},{1,33},{34,2},{2,34},{35,3},{3,35},{36,4},{4,... | collective-permute-start | bytes 786440 | tf_op jit(solution)/shard_map/ppermute | solution.py:24
  35.7 1.2 %copy-start.3 = (bf16[16,64,128]{2,1,0:T(8,128)(2,1)S(1)}, bf16[16,64,128]{2,1,0:T(8,128)(2,1)}, u32[]{:S(2)}) copy-start(bf16[16,64,128]{2,1,0:T(8,128)(2,1)} %arrange.1) | copy-start | bytes 786436
  37.8 16.4 %copy-start.1 = (f32[64,128]{1,0:T(8,128)S(1)}, f32[64,128]{1,0:T(8,128)}, u32[]{:S(2)}) copy-start(f32[64,128]{1,0:T(8,128)} %get-tuple-element.10.v0_ref) | copy-start | bytes 98308
  37.8 16.4 %copy-start.2 = (f32[64,128]{1,0:T(8,128)S(1)}, f32[64,128]{1,0:T(8,128)}, u32[]{:S(2)}) copy-start(f32[64,128]{1,0:T(8,128)} %get-tuple-element.9.mask_ref) | copy-start | bytes 98308
  37.8 16.5 %copy-start.8 = (f32[128,128]{1,0:T(8,128)S(1)}, f32[128,128]{1,0:T(8,128)}, u32[]{:S(2)}) copy-start(f32[128,128]{1,0:T(8,128)} %get-tuple-element.11) | copy-start | bytes 196612
  54.3 18.6 %copy-start = (f32[64,128]{1,0:T(8,128)}, f32[64,128]{1,0:T(8,128)S(1)}, u32[]{:S(2)}) copy-start(f32[64,128]{1,0:T(8,128)S(1)} %multiply_add_fusion.v1_ref) | copy-start | bytes 98308
  69.3 4.1 %collective-permute-start.7 = (bf16[512,128]{1,0:T(8,128)(2,1)S(1)}, bf16[512,128]{1,0:T(8,128)(2,1)S(1)}, u32[]{:S(2)}, u32[]{:S(2)}) collective-permute-start(bf16[512,128]{1,0:T(8,128)(2,1)S(1)} %bitcast.33), channel_id=1, source_target_pairs={{32,0},{0,32},{33,1},{1,33},{34,2},{2,34},{35,3},{3,35},{36,4},{4,... | collective-permute-start | bytes 393224 | tf_op jit(solution)/shard_map/ppermute | solution.py:24
  89.8 2.4 %collective-permute-start.8 = (f32[1,128]{1,0:T(1,128)}, f32[1,128]{1,0:T(1,128)S(1)}, u32[]{:S(2)}, u32[]{:S(2)}) collective-permute-start(f32[1,128]{1,0:T(1,128)} %get-tuple-element.12), channel_id=1, source_target_pairs={{32,0},{0,32},{33,1},{1,33},{34,2},{2,34},{35,3},{3,35},{36,4},{4,... | collective-permute-start | bytes 1544 | tf_op jit(solution)/shard_map/ppermute | solution.py:24

commit v3 on v2

--- a/solution.py
+++ b/solution.py
@@ -17,6 +17,7 @@
 f32 = jnp.float32
 HIGHEST = lax.Precision.HIGHEST
 VMEM = pl.BlockSpec(memory_space=pltpu.VMEM)
+ANY = pl.BlockSpec(memory_space=pl.ANY)
 
 
 def ahead(x, axis, k):
@@ -25,7 +26,10 @@
 
 
 def around(x, axis):
-    return [x] + [ahead(x, axis, k) for k in range(1, lax.axis_size(axis))]
+    n = lax.axis_size(axis)
+    blocks = [x] + [ahead(x, axis, k) for k in range(1, n)]
+    start = (n - lax.axis_index(axis)) % n * x.shape[0]
+    return lax.dynamic_slice_in_dim(jnp.concatenate(blocks + blocks), start, n * x.shape[0], 0)
 
 
 def to_all(x, axes):
@@ -76,17 +80,18 @@
     return tail(left, 3 * n, 3 * n + 3), tail(right, 3 * n + 3, 3 * n)
 
 
-def prepare(observed, lengths, features, length_scale, epoch_gain, copies):
+def seen(lengths, own, width):
+    lane = lax.broadcasted_iota(jnp.int32, (own, width), 1).astype(f32)
+    return (lane < column(lengths.astype(f32))).astype(f32)
+
+
+def prepare(observed, lengths, features, length_scale, epoch_gain, left, copies):
     own, width = observed.shape
 
-    def body(obs_ref, len_ref, feat_ref, scale_ref, gain_ref, v_ref, mask_ref, ek_ref, out_ref):
-        lane = lax.broadcasted_iota(jnp.int32, (own, width), 1).astype(f32)
-        mask = (lane < column(len_ref[...].astype(f32))).astype(f32)
-        v = mask * obs_ref[...]
+    def body(obs_ref, len_ref, feat_ref, scale_ref, gain_ref, _, v_ref, out_ref):
+        v = seen(len_ref[...], own, width) * obs_ref[...]
         ek = epoch_matrix(gain_ref[...])
-        mask_ref[...] = mask
         v_ref[...] = v
-        ek_ref[...] = ek
         w = jnp.dot(v, ek, precision=HIGHEST, preferred_element_type=f32).astype(bf16)
         right = sides(feat_ref[...], scale_ref[...], width)[1]
         for k in range(copies):
@@ -97,14 +102,50 @@
         body,
         out_shape=(
             jax.ShapeDtypeStruct((own, width), f32),
+            jax.ShapeDtypeStruct((copies, 2 * own, width), bf16),
+        ),
+        in_specs=[VMEM] * 5 + [ANY],
+        out_specs=(VMEM,) * 2,
+        name="prepare",
+    )(observed, lengths, features, length_scale, epoch_gain, left)
+
+
+def meanwhile(lengths, epoch_gain, v0, after):
+    own, width = v0.shape
+
+    def body(len_ref, gain_ref, v_ref, _, mask_ref, ek_ref, m_ref):
+        mask_ref[...] = seen(len_ref[...], own, width)
+        ek_ref[...] = epoch_matrix(gain_ref[...])
+        v = v_ref[...]
+        m_ref[...] = jnp.sum(v * v, axis=0, keepdims=True)
+
+    return pl.pallas_call(
+        body,
+        out_shape=(
             jax.ShapeDtypeStruct((own, width), f32),
             jax.ShapeDtypeStruct((width, width), f32),
-            jax.ShapeDtypeStruct((copies, 2 * own, width), bf16),
+            jax.ShapeDtypeStruct((1, width), f32),
         ),
-        in_specs=[VMEM] * 5,
-        out_specs=(VMEM,) * 4,
-        name="prepare",
-    )(observed, lengths, features, length_scale, epoch_gain)
+        in_specs=[VMEM] * 3 + [ANY],
+        out_specs=(VMEM,) * 3,
+        name="meanwhile",
+    )(lengths, epoch_gain, v0, after)
+
+
+def moments(m0, v0, v1, after):
+    def body(m_ref, v0_ref, v1_ref, _, out_ref):
+        v0, v1 = v0_ref[...], v1_ref[...]
+        out_ref[0:1, :] = m_ref[...]
+        out_ref[1:2, :] = jnp.sum(v0 * v1, axis=0, keepdims=True)
+        out_ref[2:3, :] = jnp.sum(v1 * v1, axis=0, keepdims=True)
+
+    return pl.pallas_call(
+        body,
+        out_shape=jax.ShapeDtypeStruct((3, v0.shape[1]), f32),
+        in_specs=[VMEM] * 3 + [ANY],
+        out_specs=VMEM,
+        name="moments",
+    )(m0, v0, v1, after)
 
 
 def left_side(features, length_scale, width):
@@ -120,59 +161,10 @@
     )(features, length_scale)
 
 
-def arrange(blocks, here):
-    ny = len(blocks)
-    rows, width = blocks[0].shape
-    nx = 4
-    own = rows // nx
-
-    def body(here_ref, *refs):
-        out_ref = refs[-1]
-        for j in range(ny):
-            for i in range(nx):
-                slot = lax.rem(here_ref[0] + j, ny) * nx + lax.rem(here_ref[1] + i, nx)
-                out_ref[slot] = refs[j][i * own : (i + 1) * own, :]
-
-    return pl.pallas_call(
-        body,
-        out_shape=jax.ShapeDtypeStruct((ny * nx, own, width), bf16),
-        in_specs=[pl.BlockSpec(memory_space=pltpu.SMEM)] + [VMEM] * ny,
-        out_specs=VMEM,
-        name="arrange",
-    )(here, *blocks).reshape(-1, width)
-
-
-def measure(got, mask, v0, v1):
-    def body(got_ref, mask_ref, v0_ref, v1_ref, v2_ref, m_ref):
-        v0, v1 = v0_ref[...], v1_ref[...]
-        v2 = mask_ref[...] * jnp.sum(got_ref[...], axis=0) + noise_level * v1
-        v2_ref[...] = v2
-        lane = lax.broadcasted_iota(jnp.int32, m_ref.shape, 1)
-        m = jnp.zeros(m_ref.shape, f32)
-        for k, (a, b) in enumerate(((v0, v0), (v0, v1), (v1, v1), (v1, v2))):
-            total = jnp.sum(jnp.sum(a * b, axis=0, keepdims=True), axis=1, keepdims=True)
-            m = jnp.where(lane == k, total, m)
-        m_ref[...] = m
-
-    own, width = v0.shape
-    return pl.pallas_call(
-        body,
-        out_shape=(jax.ShapeDtypeStruct((own, width), f32), jax.ShapeDtypeStruct((1, width), f32)),
-        in_specs=[VMEM] * 4,
-        out_specs=(VMEM,) * 2,
-        name="measure",
-    )(got, mask, v0, v1)
-
-
 def finish(moments, v0, v1, v2):
     def body(m_ref, v0_ref, v1_ref, v2_ref, x_ref, r_ref):
-        m = jnp.sum(m_ref[...], axis=0, keepdims=True)
-        lane = lax.broadcasted_iota(jnp.int32, m.shape, 1)
-
-        def moment(k):
-            return jnp.sum(jnp.where(lane == k, m, 0.0), axis=1, keepdims=True)
-
-        m0, m1, m2, m3 = (moment(k) for k in range(4))
+        m = jnp.sum(jnp.sum(m_ref[...], axis=0), axis=1, keepdims=True)
+        m0, m1, m2, m3 = (m[k : k + 1, :] for k in range(4))
         alpha = m0 / m1
         norm = m0 + alpha * (alpha * m2 - 2.0 * m1)
         keep = 1.0 + norm / m0
@@ -202,13 +194,14 @@
 def per_device(observed, lengths, features, length_scale, epoch_gain):
     own, width = observed.shape
     features, length_scale = features.T, length_scale[None, :]
-    v0, mask, ek, outgoing = prepare(
-        observed, lengths[None, :], features, length_scale, epoch_gain[None, :], lax.axis_size(Z)
+    lengths, epoch_gain = lengths[None, :], epoch_gain[None, :]
+    left = left_side(features, length_scale, width)
+    line = around(left, X)
+    v0, outgoing = prepare(
+        observed, lengths, features, length_scale, epoch_gain, left, lax.axis_size(Z)
     )
     here = lax.all_to_all(outgoing, Z, split_axis=0, concat_axis=0, tiled=True)
-    left = left_side(features, length_scale, width)
-    line = jnp.concatenate(around(left, X))
-    lefts = arrange(around(line, Y), jnp.stack([lax.axis_index(Y), lax.axis_index(X)]))
+    lefts = around(line.reshape(-1, own, width), Y).reshape(-1, width)
     there = ahead(here, C, 1)
     k_here = block_kernel(lefts, here[:, own:].reshape(-1, width))
     k_there = block_kernel(lefts, there[:, own:].reshape(-1, width))
@@ -216,17 +209,21 @@
     def product(w_here, w_there):
         part = jnp.dot(k_here, w_here, preferred_element_type=f32)
         part = part + jnp.dot(k_there, w_there, preferred_element_type=f32)
-        return lax.all_to_all(
+        got = lax.all_to_all(
             part.reshape(-1, own, width), (Y, X), split_axis=0, concat_axis=0, tiled=True
         )
-
-    got = product(here[:, :own].reshape(-1, width), there[:, :own].reshape(-1, width))
-    v1 = mask * jnp.sum(got, axis=0) + noise_level * v0
+        return jnp.sum(got, axis=0), part[:8]
+
+    p, part = product(here[:, :own].reshape(-1, width), there[:, :own].reshape(-1, width))
+    mask, ek, m = meanwhile(lengths, epoch_gain, v0, part)
+    v1 = mask * p + noise_level * v0
     w = jnp.dot(mask * v1, ek, precision=HIGHEST, preferred_element_type=f32).astype(bf16)
     w_here = to_all(w, Z).reshape(-1, width)
-    v2, m = measure(product(w_here, ahead(w_here, C, 1)), mask, v0, v1)
-    m = to_all(m + ahead(m, C, 1), (Y, Z, X))
-    return finish(m.reshape(-1, width), v0, v1, v2)
+    p, part = product(w_here, ahead(w_here, C, 1))
+    m = moments(m, v0, v1, part)
+    v2 = mask * p + noise_level * v1
+    m = jnp.concatenate([m, jnp.sum(v1 * v2, axis=0, keepdims=True)])
+    return finish(to_all(m + ahead(m, C, 1), (Y, Z, X)), v0, v1, v2)
 
 
 def solution(mesh):

time: 112 us -> 112 us (level)
  blocking collectives: 62.3 us -> 33.2 us
  waiting for transfers between devices: 5.92 us -> 21.1 us
  starting transfers between devices: 27.3 us -> 35 us
  local copies, waits for them, and re-layouts: 0.73 us -> 4.29 us
  matrix products: 3.84 us -> 5.36 us
    all_to_all x2 -> x0, blocking collectives: 30.6 us -> none  [product(): lax.all_to_all(part.reshape(-1, own, width), (Y, X), split_axis=0, concat...]
    all_to_all x0 -> x2, waiting for transfers between devices: none -> 16.3 us  [product(): lax.all_to_all(part.reshape(-1, own, width), (Y, X), split_axis=0, concat...]
    all_to_all x0 -> x2, starting transfers between devices: none -> 8.16 us  [product(): lax.all_to_all(part.reshape(-1, own, width), (Y, X), split_axis=0, concat...]
    slice x0 -> x2, local copies, waits for them, and re-layouts: none -> 2.54 us  [product(): return (jnp.sum(got, axis=0), part[:8])]
    dot_general x2, matrix products: 0.87 us -> 2.46 us  [product(): part = part + jnp.dot(k_there, w_there, preferred_element_type=f32)]
    all_to_all x2, blocking collectives: 31.6 us -> 33.2 us  [to_all(): return lax.all_to_all(copies, axes, split_axis=0, concat_axis=0, tiled=True)]
  transfers between devices with their start and end apart: 10 -> 12, of which waited for: 7 -> 6; matrix products, arithmetic and copies ran while one was open for 2% -> 5% of each run, Pallas kernels for 3% -> 4%
where the time goes in v3:
time: 112 us; the launch traced here: 111 us
  starting transfers between devices  35 us (31%)
  blocking collectives  33.2 us (30%)
  waiting for transfers between devices  21.1 us (19%)
  Pallas kernels  8.35 us (7%)
  matrix products  5.36 us (5%)
  local copies, waits for them, and re-layouts  4.29 us (4%)
  other arithmetic  2.82 us (3%)
    all_to_all x2, blocking collectives, to_all(): return lax.all_to_all(copies, axes, split_axis=0, concat_axis=0, tiled=True)  33.2 us
    ppermute x9, starting transfers between devices, ahead(): return lax.ppermute(x, axis, [((i + k) % n, i) for i in range(n)])  18.7 us
    all_to_all x2, waiting for transfers between devices, product(): lax.all_to_all(part.reshape(-1, own, width), (Y, X), split_axis=0, concat...  16.3 us
    all_to_all x1, starting transfers between devices, per_device(): here = lax.all_to_all(outgoing, Z, split_axis=0, concat_axis=0, tiled=True)  8.18 us
    all_to_all x2, starting transfers between devices, product(): lax.all_to_all(part.reshape(-1, own, width), (Y, X), split_axis=0, concat...  8.16 us
    ppermute x9, waiting for transfers between devices, ahead(): return lax.ppermute(x, axis, [((i + k) % n, i) for i in range(n)])  4.82 us
    slice x2, local copies, waits for them, and re-layouts, product(): return (jnp.sum(got, axis=0), part[:8])  2.54 us
    dot_general x2, matrix products, product(): part = part + jnp.dot(k_there, w_there, preferred_element_type=f32)  2.46 us
  transfers between devices with their start and end apart: 12, of which 6 were waited for; matrix products, arithmetic and copies ran while one was open for 5% of the time, Pallas kernels for 4%

profile of v3, /device:TPU:1, one launch (start us, length us, event | category | flops | bytes accessed | tf_op | source)
XLA Modules:
  0.0 110.9 jit_solution(2303361545919756208)
XLA Ops:
  0.6 1.7 %left_side.1._ = bf16[64,128]{1,0:T(8,128)(2,1)} custom-call(f32[32,64]{1,0:T(8,128)} %bitcast.40, f32[1,32]{1,0:T(1,128)} %bitcast.44), custom_call_target="tpu_custom_call" | custom-call | tf_op jit(solution)/shard_map/left_side/pallas_call | solution.py:155
  2.3 2.0 %collective-permute-start.2 = (bf16[64,128]{1,0:T(8,128)(2,1)}, bf16[64,128]{1,0:T(8,128)(2,1)S(1)}, u32[]{:S(2)}, u32[]{:S(2)}) collective-permute-start(bf16[64,128]{1,0:T(8,128)(2,1)} %left_side.1._), channel_id=1, source_target_pairs={{3,0},{0,1},{1,2},{2,3},{7,4},{4,5},{5,6},{6,7},{11,8},{8,9},{9,10... | collective-permute-start | bytes 49160 | tf_op jit(solution)/shard_map/ppermute | solution.py:25
  4.4 2.5 %collective-permute-start.1 = (bf16[64,128]{1,0:T(8,128)(2,1)}, bf16[64,128]{1,0:T(8,128)(2,1)S(1)}, u32[]{:S(2)}, u32[]{:S(2)}) collective-permute-start(bf16[64,128]{1,0:T(8,128)(2,1)} %left_side.1._), channel_id=1, source_target_pairs={{2,0},{3,1},{0,2},{1,3},{6,4},{7,5},{4,6},{5,7},{10,8},{11,9},{8,1... | collective-permute-start | bytes 49160 | tf_op jit(solution)/shard_map/ppermute | solution.py:25
  8.0 1.9 %prepare.1 = (f32[64,128]{1,0:T(8,128)}, bf16[8,128,128]{2,1,0:T(8,128)(2,1)}) custom-call(f32[64,128]{1,0:T(8,128)} %obs_ref.1, s32[1,64]{1,0:T(1,128)} %bitcast.46, f32[32,64]{1,0:T(8,128)} %bitcast.41, f32[1,32]{1,0:T(1,128)} %bitcast.45, f32[1,128]{1,0:T(1,128)} %bitcast.48, bf16[64,128]{1,0:T(8,128)(2,1)} %left_side.1._), custom_call_target="tpu_custom_call" | custom-call | tf_op jit(solution)/shard_map/prepare/pallas_call | solution.py:101
  9.9 8.2 %all-to-all-start = ((bf16[8,128,128]{2,1,0:T(8,128)(2,1)}), bf16[8,128,128]{2,1,0:T(8,128)(2,1)S(1)}, u32[]{:S(2)}, u32[]{:S(2)}) async-start(bf16[8,128,128]{2,1,0:T(8,128)(2,1)} %get-tuple-element.8), calls=%async_computation | async-start | bytes 524288 | tf_op jit(solution)/shard_map/all_to_all | solution.py:203
  19.6 1.4 %collective-permute-start.5 = (bf16[4,64,128]{2,1,0:T(8,128)(2,1)S(1)}, bf16[4,64,128]{2,1,0:T(8,128)(2,1)S(1)}, u32[]{:S(2)}, u32[]{:S(2)}) collective-permute-start(bf16[4,64,128]{2,1,0:T(8,128)(2,1)S(1)} %bitcast.27), channel_id=1, source_target_pairs={{192,0},{0,64},{64,128},{128,192},{193,1},{1,65},{65,129},{129,193... | collective-permute-start | bytes 196616 | tf_op jit(solution)/shard_map/ppermute | solution.py:25
  21.0 2.6 %collective-permute-start.4 = (bf16[4,64,128]{2,1,0:T(8,128)(2,1)S(1)}, bf16[4,64,128]{2,1,0:T(8,128)(2,1)S(1)}, u32[]{:S(2)}, u32[]{:S(2)}) collective-permute-start(bf16[4,64,128]{2,1,0:T(8,128)(2,1)S(1)} %bitcast.28), channel_id=1, source_target_pairs={{128,0},{192,64},{0,128},{64,192},{129,1},{193,65},{1,129},{65,193... | collective-permute-start | bytes 196616 | tf_op jit(solution)/shard_map/ppermute | solution.py:25
  24.7 2.7 %collective-permute-done.3 = bf16[4,64,128]{2,1,0:T(8,128)(2,1)S(1)} collective-permute-done((bf16[4,64,128]{2,1,0:T(8,128)(2,1)S(1)}, bf16[4,64,128]{2,1,0:T(8,128)(2,1)S(1)}, u32[]{:S(2)}, u32[]{:S(2)}) %collective-permute-start.3) | collective-permute-done | bytes 65568 | tf_op jit(solution)/shard_map/ppermute | solution.py:25
  28.1 3.4 %collective-permute-start.6 = (bf16[8,128,128]{2,1,0:T(8,128)(2,1)S(1)}, bf16[8,128,128]{2,1,0:T(8,128)(2,1)S(1)}, u32[]{:S(2)}, u32[]{:S(2)}) collective-permute-start(bf16[8,128,128]{2,1,0:T(8,128)(2,1)S(1)} %all-to-all-done), channel_id=1, source_target_pairs={{32,0},{0,32},{33,1},{1,33},{34,2},{2,34},{35,3},{3,35},{36,4},{4,... | collective-permute-start | bytes 786440 | tf_op jit(solution)/shard_map/ppermute | solution.py:25
  33.2 1.2 %convolution_add_fusion.1 = f32[1024,128]{1,0:T(8,128)} fusion(f32[1024,128]{1,0:T(8,128)S(1)} %fusion.3, bf16[1024,512]{1,0:T(8,128)(2,1)S(1)} %exponential_convert_fusion, bf16[512,128]{1,0:T(8,128)(2,1)S(1)} %bitcast.32), kind=kOutput, calls=%fused_computation.3 | convolution fusion | flops 134348800 | bytes 2228224 | tf_op jit(solution)/shard_map/dot_general | solution.py:211
  34.4 4.5 %all-to-all-start.1 = ((f32[16,64,128]{2,1,0:T(8,128)}), f32[16,64,128]{2,1,0:T(8,128)S(1)}, u32[]{:S(2)}, u32[]{:S(2)}) async-start(f32[16,64,128]{2,1,0:T(8,128)} %bitcast.10), calls=%async_computation.1 | async-start | bytes 1048576 | tf_op jit(solution)/shard_map/all_to_all | solution.py:212
  38.9 1.3 %slice.28._ = f32[8,128]{1,0:T(8,128)} slice(f32[1024,128]{1,0:T(8,128)} %convolution_add_fusion.1), slice={[0:8], [0:128]} | slice | bytes 8192 | tf_op jit(solution)/shard_map/slice | solution.py:215
  40.1 1.5 %meanwhile.1 = (f32[64,128]{1,0:T(8,128)}, f32[128,128]{1,0:T(8,128)}, f32[1,128]{1,0:T(1,128)}) custom-call(s32[1,64]{1,0:T(1,128)} %bitcast.47, f32[1,128]{1,0:T(1,128)} %bitcast.49, f32[64,128]{1,0:T(8,128)} %get-tuple-element.7.v_ref.v0_ref, f32[8,128]{1,0:T(8,128)} %slice.28._), custom_call_target="tpu_custom_call" | custom-call | tf_op jit(solution)/shard_map/meanwhile/pallas_call | solution.py:122
  41.6 8.0 %all-to-all-done.1 = f32[16,64,128]{2,1,0:T(8,128)S(1)} async-done(((f32[16,64,128]{2,1,0:T(8,128)}), f32[16,64,128]{2,1,0:T(8,128)S(1)}, u32[]{:S(2)}, u32[]{:S(2)}) %all-to-all-start.1) | async-done | bytes 524320 | tf_op jit(solution)/shard_map/all_to_all | solution.py:212
  51.5 13.7 %all_to_all.25 = bf16[8,64,128]{2,1,0:T(8,128)(2,1)S(1)} all-to-all(bf16[8,64,128]{2,1,0:T(8,128)(2,1)S(1)} %broadcast_in_dim.21), channel_id=1, replica_groups=mesh['y'=4,'c'=2,'z'=8,'x'=4] {'z'}, dimensions={0} | all-to-all | bytes 262144 | tf_op jit(solution)/shard_map/all_to_all | solution.py:37
  65.1 3.1 %collective-permute-start.7 = (bf16[512,128]{1,0:T(8,128)(2,1)S(1)}, bf16[512,128]{1,0:T(8,128)(2,1)S(1)}, u32[]{:S(2)}, u32[]{:S(2)}) collective-permute-start(bf16[512,128]{1,0:T(8,128)(2,1)S(1)} %bitcast.33), channel_id=1, source_target_pairs={{32,0},{0,32},{33,1},{1,33},{34,2},{2,34},{35,3},{3,35},{36,4},{4,... | collective-permute-start | bytes 393224 | tf_op jit(solution)/shard_map/ppermute | solution.py:25
  69.2 1.2 %convolution_add_fusion = f32[1024,128]{1,0:T(8,128)} fusion(f32[1024,128]{1,0:T(8,128)S(1)} %fusion.4, bf16[1024,512]{1,0:T(8,128)(2,1)S(1)} %exponential_convert_fusion, bf16[512,128]{1,0:T(8,128)(2,1)S(1)} %collective-permute-done.7), kind=kOutput, calls=%fused_computation.2 | convolution fusion | flops 134348800 | bytes 2228224 | tf_op jit(solution)/shard_map/dot_general | solution.py:211
  70.5 3.7 %all-to-all-start.3 = ((f32[16,64,128]{2,1,0:T(8,128)}), f32[16,64,128]{2,1,0:T(8,128)S(1)}, u32[]{:S(2)}, u32[]{:S(2)}) async-start(f32[16,64,128]{2,1,0:T(8,128)} %bitcast.12), calls=%async_computation.3 | async-start | bytes 1048576 | tf_op jit(solution)/shard_map/all_to_all | solution.py:212
  74.2 1.3 %slice.29._ = f32[8,128]{1,0:T(8,128)} slice(f32[1024,128]{1,0:T(8,128)} %convolution_add_fusion), slice={[0:8], [0:128]} | slice | bytes 8192 | tf_op jit(solution)/shard_map/slice | solution.py:215
  75.5 1.4 %moments.1 = f32[3,128]{1,0:T(4,128)} custom-call(f32[1,128]{1,0:T(1,128)} %get-tuple-element.9.m_ref, f32[64,128]{1,0:T(8,128)} %get-tuple-element.7.v_ref.v0_ref, f32[64,128]{1,0:T(8,128)} %copy-done, f32[8,128]{1,0:T(8,128)} %slice.29._), custom_call_target="tpu_custom_call" | custom-call | tf_op jit(solution)/shard_map/moments/pallas_call | solution.py:142
  76.8 8.3 %all-to-all-done.3 = f32[16,64,128]{2,1,0:T(8,128)S(1)} async-done(((f32[16,64,128]{2,1,0:T(8,128)}), f32[16,64,128]{2,1,0:T(8,128)S(1)}, u32[]{:S(2)}, u32[]{:S(2)}) %all-to-all-start.3) | async-done | bytes 524320 | tf_op jit(solution)/shard_map/all_to_all | solution.py:212
  86.5 1.5 %collective-permute-start.8 = (f32[4,128]{1,0:T(4,128)S(1)}, f32[4,128]{1,0:T(4,128)S(1)}, u32[]{:S(2)}, u32[]{:S(2)}) collective-permute-start(f32[4,128]{1,0:T(4,128)S(1)} %pad_maximum_fusion), channel_id=1, source_target_pairs={{32,0},{0,32},{33,1},{1,33},{34,2},{2,34},{35,3},{3,35},{36,4},{4,... | collective-permute-start | bytes 6152 | tf_op jit(solution)/shard_map/ppermute | solution.py:25
  89.5 19.5 %all_to_all.26.m_ref = f32[128,4,128]{2,1,0:T(4,128)} all-to-all(f32[128,4,128]{2,1,0:T(4,128)S(1)} %broadcast_in_dim.23), channel_id=1, replica_groups=mesh['y'=4,'c'=2,'z'=8,'x'=4] {'y','z','x'}, dimensions={0} | all-to-all | bytes 524288 | tf_op jit(solution)/shard_map/all_to_all | solution.py:37
  109.1 1.9 %finish.1 = (f32[64,128]{1,0:T(8,128)}, f32[64,128]{1,0:T(8,128)}) custom-call(f32[128,4,128]{2,1,0:T(4,128)} %all_to_all.26.m_ref, f32[64,128]{1,0:T(8,128)} %get-tuple-element.7.v_ref.v0_ref, f32[64,128]{1,0:T(8,128)} %copy-done, f32[64,128]{1,0:T(8,128)} %get-tuple-element.13.v2_ref), custom_call_target="tpu_custom_call" | custom-call | tf_op jit(solution)/shard_map/finish/pallas_call | solution.py:180
  (52 shorter events, 11.8 us)
Async XLA Ops:
  2.3 16.5 %collective-permute-start.2 = (bf16[64,128]{1,0:T(8,128)(2,1)}, bf16[64,128]{1,0:T(8,128)(2,1)S(1)}, u32[]{:S(2)}, u32[]{:S(2)}) collective-permute-start(bf16[64,128]{1,0:T(8,128)(2,1)} %left_side.1._), channel_id=1, source_target_pairs={{3,0},{0,1},{1,2},{2,3},{7,4},{4,5},{5,6},{6,7},{11,8},{8,9},{9,10... | collective-permute-start | bytes 49160 | tf_op jit(solution)/shard_map/ppermute | solution.py:25
  4.4 14.4 %collective-permute-start.1 = (bf16[64,128]{1,0:T(8,128)(2,1)}, bf16[64,128]{1,0:T(8,128)(2,1)S(1)}, u32[]{:S(2)}, u32[]{:S(2)}) collective-permute-start(bf16[64,128]{1,0:T(8,128)(2,1)} %left_side.1._), channel_id=1, source_target_pairs={{2,0},{3,1},{0,2},{1,3},{6,4},{7,5},{4,6},{5,7},{10,8},{11,9},{8,1... | collective-permute-start | bytes 49160 | tf_op jit(solution)/shard_map/ppermute | solution.py:25
  6.8 12.0 %collective-permute-start = (bf16[64,128]{1,0:T(8,128)(2,1)}, bf16[64,128]{1,0:T(8,128)(2,1)S(1)}, u32[]{:S(2)}, u32[]{:S(2)}) collective-permute-start(bf16[64,128]{1,0:T(8,128)(2,1)} %left_side.1._), channel_id=1, source_target_pairs={{1,0},{2,1},{3,2},{0,3},{5,4},{6,5},{7,6},{4,7},{9,8},{10,9},{11,1... | collective-permute-start | bytes 49160 | tf_op jit(solution)/shard_map/ppermute | solution.py:25
  9.9 17.7 %all-to-all-start = ((bf16[8,128,128]{2,1,0:T(8,128)(2,1)}), bf16[8,128,128]{2,1,0:T(8,128)(2,1)S(1)}, u32[]{:S(2)}, u32[]{:S(2)}) async-start(bf16[8,128,128]{2,1,0:T(8,128)(2,1)} %get-tuple-element.8), calls=%async_computation | async-start | bytes 524288 | tf_op jit(solution)/shard_map/all_to_all | solution.py:203
  19.6 7.8 %collective-permute-start.5 = (bf16[4,64,128]{2,1,0:T(8,128)(2,1)S(1)}, bf16[4,64,128]{2,1,0:T(8,128)(2,1)S(1)}, u32[]{:S(2)}, u32[]{:S(2)}) collective-permute-start(bf16[4,64,128]{2,1,0:T(8,128)(2,1)S(1)} %bitcast.27), channel_id=1, source_target_pairs={{192,0},{0,64},{64,128},{128,192},{193,1},{1,65},{65,129},{129,193... | collective-permute-start | bytes 196616 | tf_op jit(solution)/shard_map/ppermute | solution.py:25
  21.0 6.4 %collective-permute-start.4 = (bf16[4,64,128]{2,1,0:T(8,128)(2,1)S(1)}, bf16[4,64,128]{2,1,0:T(8,128)(2,1)S(1)}, u32[]{:S(2)}, u32[]{:S(2)}) collective-permute-start(bf16[4,64,128]{2,1,0:T(8,128)(2,1)S(1)} %bitcast.28), channel_id=1, source_target_pairs={{128,0},{192,64},{0,128},{64,192},{129,1},{193,65},{1,129},{65,193... | collective-permute-start | bytes 196616 | tf_op jit(solution)/shard_map/ppermute | solution.py:25
  23.6 3.8 %collective-permute-start.3 = (bf16[4,64,128]{2,1,0:T(8,128)(2,1)S(1)}, bf16[4,64,128]{2,1,0:T(8,128)(2,1)S(1)}, u32[]{:S(2)}, u32[]{:S(2)}) collective-permute-start(bf16[4,64,128]{2,1,0:T(8,128)(2,1)S(1)} %bitcast.29), channel_id=1, source_target_pairs={{64,0},{128,64},{192,128},{0,192},{65,1},{129,65},{193,129},{1,193... | collective-permute-start | bytes 196616 | tf_op jit(solution)/shard_map/ppermute | solution.py:25
  28.1 4.5 %collective-permute-start.6 = (bf16[8,128,128]{2,1,0:T(8,128)(2,1)S(1)}, bf16[8,128,128]{2,1,0:T(8,128)(2,1)S(1)}, u32[]{:S(2)}, u32[]{:S(2)}) collective-permute-start(bf16[8,128,128]{2,1,0:T(8,128)(2,1)S(1)} %all-to-all-done), channel_id=1, source_target_pairs={{32,0},{0,32},{33,1},{1,33},{34,2},{2,34},{35,3},{3,35},{36,4},{4,... | collective-permute-start | bytes 786440 | tf_op jit(solution)/shard_map/ppermute | solution.py:25
  34.4 15.2 %copy-start.2 = (f32[64,128]{1,0:T(8,128)S(1)}, f32[64,128]{1,0:T(8,128)}, u32[]{:S(2)}) copy-start(f32[64,128]{1,0:T(8,128)} %get-tuple-element.7.v_ref.v0_ref) | copy-start | bytes 98308
  34.4 15.2 %all-to-all-start.1 = ((f32[16,64,128]{2,1,0:T(8,128)}), f32[16,64,128]{2,1,0:T(8,128)S(1)}, u32[]{:S(2)}, u32[]{:S(2)}) async-start(f32[16,64,128]{2,1,0:T(8,128)} %bitcast.10), calls=%async_computation.1 | async-start | bytes 1048576 | tf_op jit(solution)/shard_map/all_to_all | solution.py:212
  50.4 18.3 %copy-start = (f32[64,128]{1,0:T(8,128)}, f32[64,128]{1,0:T(8,128)S(1)}, u32[]{:S(2)}) copy-start(f32[64,128]{1,0:T(8,128)S(1)} %multiply_add_fusion.1.v1_ref) | copy-start | bytes 98308
  65.1 4.1 %collective-permute-start.7 = (bf16[512,128]{1,0:T(8,128)(2,1)S(1)}, bf16[512,128]{1,0:T(8,128)(2,1)S(1)}, u32[]{:S(2)}, u32[]{:S(2)}) collective-permute-start(bf16[512,128]{1,0:T(8,128)(2,1)S(1)} %bitcast.33), channel_id=1, source_target_pairs={{32,0},{0,32},{33,1},{1,33},{34,2},{2,34},{35,3},{3,35},{36,4},{4,... | collective-permute-start | bytes 393224 | tf_op jit(solution)/shard_map/ppermute | solution.py:25
  70.5 14.7 %copy-start.1 = (f32[64,128]{1,0:T(8,128)S(1)}, f32[64,128]{1,0:T(8,128)}, u32[]{:S(2)}) copy-start(f32[64,128]{1,0:T(8,128)} %copy-done) | copy-start | bytes 98308
  70.5 14.7 %copy-start.3 = (f32[64,128]{1,0:T(8,128)S(1)}, f32[64,128]{1,0:T(8,128)}, u32[]{:S(2)}) copy-start(f32[64,128]{1,0:T(8,128)} %get-tuple-element.10) | copy-start | bytes 98308
  70.5 14.7 %all-to-all-start.3 = ((f32[16,64,128]{2,1,0:T(8,128)}), f32[16,64,128]{2,1,0:T(8,128)S(1)}, u32[]{:S(2)}, u32[]{:S(2)}) async-start(f32[16,64,128]{2,1,0:T(8,128)} %bitcast.12), calls=%async_computation.3 | async-start | bytes 1048576 | tf_op jit(solution)/shard_map/all_to_all | solution.py:212
  86.5 2.3 %collective-permute-start.8 = (f32[4,128]{1,0:T(4,128)S(1)}, f32[4,128]{1,0:T(4,128)S(1)}, u32[]{:S(2)}, u32[]{:S(2)}) collective-permute-start(f32[4,128]{1,0:T(4,128)S(1)} %pad_maximum_fusion), channel_id=1, source_target_pairs={{32,0},{0,32},{33,1},{1,33},{34,2},{2,34},{35,3},{3,35},{36,4},{4,... | collective-permute-start | bytes 6152 | tf_op jit(solution)/shard_map/ppermute | solution.py:25

commit v4 on v2

--- a/solution.py
+++ b/solution.py
@@ -15,8 +15,10 @@
 epoch_offset = 16.0
 bf16 = jnp.bfloat16
 f32 = jnp.float32
+f16 = jnp.float16
 HIGHEST = lax.Precision.HIGHEST
 VMEM = pl.BlockSpec(memory_space=pltpu.VMEM)
+ANY = pl.BlockSpec(memory_space=pl.ANY)
 
 
 def ahead(x, axis, k):
@@ -25,7 +27,10 @@
 
 
 def around(x, axis):
-    return [x] + [ahead(x, axis, k) for k in range(1, lax.axis_size(axis))]
+    n = lax.axis_size(axis)
+    blocks = [x] + [ahead(x, axis, k) for k in range(1, n)]
+    start = (n - lax.axis_index(axis)) % n * x.shape[0]
+    return lax.dynamic_slice_in_dim(jnp.concatenate(blocks + blocks), start, n * x.shape[0], 0)
 
 
 def to_all(x, axes):
@@ -76,10 +81,15 @@
     return tail(left, 3 * n, 3 * n + 3), tail(right, 3 * n + 3, 3 * n)
 
 
-def prepare(observed, lengths, features, length_scale, epoch_gain, copies):
+def seen(lengths, own, width):
+    lane = lax.broadcasted_iota(jnp.int32, (own, width), 1).astype(f32)
+    return (lane < column(lengths.astype(f32))).astype(f32)
+
+
+def prepare(observed, lengths, features, length_scale, epoch_gain, left, copies):
     own, width = observed.shape
 
-    def body(obs_ref, len_ref, feat_ref, scale_ref, gain_ref, v_ref, mask_ref, ek_ref, out_ref):
+    def body(obs_ref, len_ref, feat_ref, scale_ref, gain_ref, _, v_ref, mask_ref, ek_ref, out_ref):
         lane = lax.broadcasted_iota(jnp.int32, (own, width), 1).astype(f32)
         mask = (lane < column(len_ref[...].astype(f32))).astype(f32)
         v = mask * obs_ref[...]
@@ -101,10 +111,10 @@
             jax.ShapeDtypeStruct((width, width), f32),
             jax.ShapeDtypeStruct((copies, 2 * own, width), bf16),
         ),
-        in_specs=[VMEM] * 5,
+        in_specs=[VMEM] * 5 + [ANY],
         out_specs=(VMEM,) * 4,
         name="prepare",
-    )(observed, lengths, features, length_scale, epoch_gain)
+    )(observed, lengths, features, length_scale, epoch_gain, left)
 
 
 def left_side(features, length_scale, width):
@@ -120,33 +130,9 @@
     )(features, length_scale)
 
 
-def arrange(blocks, here):
-    ny = len(blocks)
-    rows, width = blocks[0].shape
-    nx = 4
-    own = rows // nx
-
-    def body(here_ref, *refs):
-        out_ref = refs[-1]
-        for j in range(ny):
-            for i in range(nx):
-                slot = lax.rem(here_ref[0] + j, ny) * nx + lax.rem(here_ref[1] + i, nx)
-                out_ref[slot] = refs[j][i * own : (i + 1) * own, :]
-
-    return pl.pallas_call(
-        body,
-        out_shape=jax.ShapeDtypeStruct((ny * nx, own, width), bf16),
-        in_specs=[pl.BlockSpec(memory_space=pltpu.SMEM)] + [VMEM] * ny,
-        out_specs=VMEM,
-        name="arrange",
-    )(here, *blocks).reshape(-1, width)
-
-
-def measure(got, mask, v0, v1):
-    def body(got_ref, mask_ref, v0_ref, v1_ref, v2_ref, m_ref):
-        v0, v1 = v0_ref[...], v1_ref[...]
-        v2 = mask_ref[...] * jnp.sum(got_ref[...], axis=0) + noise_level * v1
-        v2_ref[...] = v2
+def measure(v0, v1, v2):
+    def body(v0_ref, v1_ref, v2_ref, m_ref):
+        v0, v1, v2 = v0_ref[...], v1_ref[...], v2_ref[...]
         lane = lax.broadcasted_iota(jnp.int32, m_ref.shape, 1)
         m = jnp.zeros(m_ref.shape, f32)
         for k, (a, b) in enumerate(((v0, v0), (v0, v1), (v1, v1), (v1, v2))):
@@ -154,14 +140,13 @@
             m = jnp.where(lane == k, total, m)
         m_ref[...] = m
 
-    own, width = v0.shape
-    return pl.pallas_call(
-        body,
-        out_shape=(jax.ShapeDtypeStruct((own, width), f32), jax.ShapeDtypeStruct((1, width), f32)),
-        in_specs=[VMEM] * 4,
-        out_specs=(VMEM,) * 2,
+    return pl.pallas_call(
+        body,
+        out_shape=jax.ShapeDtypeStruct((1, v0.shape[1]), f32),
+        in_specs=[VMEM] * 3,
+        out_specs=VMEM,
         name="measure",
-    )(got, mask, v0, v1)
+    )(v0, v1, v2)
 
 
 def finish(moments, v0, v1, v2):
@@ -202,13 +187,14 @@
 def per_device(observed, lengths, features, length_scale, epoch_gain):
     own, width = observed.shape
     features, length_scale = features.T, length_scale[None, :]
+    lengths, epoch_gain = lengths[None, :], epoch_gain[None, :]
+    left = left_side(features, length_scale, width)
+    line = around(left, X)
     v0, mask, ek, outgoing = prepare(
-        observed, lengths[None, :], features, length_scale, epoch_gain[None, :], lax.axis_size(Z)
+        observed, lengths, features, length_scale, epoch_gain, left, lax.axis_size(Z)
     )
     here = lax.all_to_all(outgoing, Z, split_axis=0, concat_axis=0, tiled=True)
-    left = left_side(features, length_scale, width)
-    line = jnp.concatenate(around(left, X))
-    lefts = arrange(around(line, Y), jnp.stack([lax.axis_index(Y), lax.axis_index(X)]))
+    lefts = around(line.reshape(-1, own, width), Y).reshape(-1, width)
     there = ahead(here, C, 1)
     k_here = block_kernel(lefts, here[:, own:].reshape(-1, width))
     k_there = block_kernel(lefts, there[:, own:].reshape(-1, width))
@@ -216,17 +202,25 @@
     def product(w_here, w_there):
         part = jnp.dot(k_here, w_here, preferred_element_type=f32)
         part = part + jnp.dot(k_there, w_there, preferred_element_type=f32)
-        return lax.all_to_all(
-            part.reshape(-1, own, width), (Y, X), split_axis=0, concat_axis=0, tiled=True
+        top = jnp.maximum(*(jnp.max(jnp.abs(w.astype(f32)), axis=0) for w in (w_here, w_there)))
+        power = jnp.ceil(jnp.log2(jnp.maximum(top, 1e-30) * (2 * w_here.shape[0])))
+        part = (part * jnp.exp2(15.0 - power)).astype(f16).reshape(-1, own, width)
+        tail = jnp.broadcast_to(power.astype(f16), (part.shape[0], 16, width))
+        got = lax.all_to_all(
+            jnp.concatenate([part, tail], axis=1), (Y, X), split_axis=0, concat_axis=0, tiled=True
         )
-
-    got = product(here[:, :own].reshape(-1, width), there[:, :own].reshape(-1, width))
-    v1 = mask * jnp.sum(got, axis=0) + noise_level * v0
+        scale = jnp.exp2(got[:, own : own + 1].astype(f32) - 15.0)
+        return jnp.sum(got[:, :own].astype(f32) * scale, axis=0)
+
+    p = product(here[:, :own].reshape(-1, width), there[:, :own].reshape(-1, width))
+    v1 = mask * p + noise_level * v0
     w = jnp.dot(mask * v1, ek, precision=HIGHEST, preferred_element_type=f32).astype(bf16)
     w_here = to_all(w, Z).reshape(-1, width)
-    v2, m = measure(product(w_here, ahead(w_here, C, 1)), mask, v0, v1)
-    m = to_all(m + ahead(m, C, 1), (Y, Z, X))
-    return finish(m.reshape(-1, width), v0, v1, v2)
+    p = product(w_here, ahead(w_here, C, 1))
+    v2 = mask * p + noise_level * v1
+    m = measure(v0, v1, v2)
+    m = to_all(m + ahead(m, C, 1), (Y, Z, X)).reshape(-1, width)
+    return finish(m, v0, v1, v2)
 
 
 def solution(mesh):

time: 112 us -> 101 us (0.902)
  blocking collectives: 62.3 us -> 54.9 us
  Pallas kernels: 8.58 us -> 6.59 us
    all_to_all x2, blocking collectives: 30.6 us -> 24.4 us  [product(): lax.all_to_all(jnp.concatenate([part, tail], axis=1), (Y, X), split_axis=...]
    pallas_call x2 -> x1, Pallas kernels: 3.37 us -> 1.39 us  [measure(): pl.pallas_call(body, out_shape=jax.ShapeDtypeStruct((1, v0.shape[1]), f32...]
    all_to_all x2, blocking collectives: 31.6 us -> 30.5 us  [to_all(): return lax.all_to_all(copies, axes, split_axis=0, concat_axis=0, tiled=True)]
  transfers between devices with their start and end apart: 10 -> 10, of which waited for: 7 -> 4; matrix products, arithmetic and copies ran while one was open for 2% -> 3% of each run, Pallas kernels for 3% -> 2%
where the time goes in v4:
time: 101 us
  blocking collectives  54.9 us (54%)
  starting transfers between devices  26.7 us (26%)
  Pallas kernels  6.59 us (7%)
  waiting for transfers between devices  4.93 us (5%)
  matrix products  2.92 us (3%)
  local copies, waits for them, and re-layouts  1.81 us (2%)
  other arithmetic  1.8 us (2%)
    all_to_all x2, blocking collectives, to_all(): return lax.all_to_all(copies, axes, split_axis=0, concat_axis=0, tiled=True)  30.5 us
    all_to_all x2, blocking collectives, product(): lax.all_to_all(jnp.concatenate([part, tail], axis=1), (Y, X), split_axis=...  24.4 us
    ppermute x9, starting transfers between devices, ahead(): return lax.ppermute(x, axis, [((i + k) % n, i) for i in range(n)])  18.5 us
    all_to_all x1, starting transfers between devices, per_device(): here = lax.all_to_all(outgoing, Z, split_axis=0, concat_axis=0, tiled=True)  8.18 us
    ppermute x9, waiting for transfers between devices, ahead(): return lax.ppermute(x, axis, [((i + k) % n, i) for i in range(n)])  4.93 us
  transfers between devices with their start and end apart: 10, of which 4 were waited for; matrix products, arithmetic and copies ran while one was open for 3% of the time, Pallas kernels for 2%

profile of v4, /device:TPU:1, one launch (start us, length us, event | category | flops | bytes accessed | tf_op | source)
XLA Modules:
  0.0 100.5 jit_solution(1079228708246614553)
XLA Ops:
  0.6 1.7 %left_side.1._ = bf16[64,128]{1,0:T(8,128)(2,1)} custom-call(f32[32,64]{1,0:T(8,128)} %bitcast.49, f32[1,32]{1,0:T(1,128)} %bitcast.51), custom_call_target="tpu_custom_call" | custom-call | tf_op jit(solution)/shard_map/left_side/pallas_call | solution.py:124
  2.3 2.0 %collective-permute-start.2 = (bf16[64,128]{1,0:T(8,128)(2,1)}, bf16[64,128]{1,0:T(8,128)(2,1)S(1)}, u32[]{:S(2)}, u32[]{:S(2)}) collective-permute-start(bf16[64,128]{1,0:T(8,128)(2,1)} %left_side.1._), channel_id=1, source_target_pairs={{3,0},{0,1},{1,2},{2,3},{7,4},{4,5},{5,6},{6,7},{11,8},{8,9},{9,10... | collective-permute-start | bytes 49160 | tf_op jit(solution)/shard_map/ppermute | solution.py:26
  4.4 2.5 %collective-permute-start.1 = (bf16[64,128]{1,0:T(8,128)(2,1)}, bf16[64,128]{1,0:T(8,128)(2,1)S(1)}, u32[]{:S(2)}, u32[]{:S(2)}) collective-permute-start(bf16[64,128]{1,0:T(8,128)(2,1)} %left_side.1._), channel_id=1, source_target_pairs={{2,0},{3,1},{0,2},{1,3},{6,4},{7,5},{4,6},{5,7},{10,8},{11,9},{8,1... | collective-permute-start | bytes 49160 | tf_op jit(solution)/shard_map/ppermute | solution.py:26
  6.8 1.2 %collective-permute-start = (bf16[64,128]{1,0:T(8,128)(2,1)}, bf16[64,128]{1,0:T(8,128)(2,1)S(1)}, u32[]{:S(2)}, u32[]{:S(2)}) collective-permute-start(bf16[64,128]{1,0:T(8,128)(2,1)} %left_side.1._), channel_id=1, source_target_pairs={{1,0},{2,1},{3,2},{0,3},{5,4},{6,5},{7,6},{4,7},{9,8},{10,9},{11,1... | collective-permute-start | bytes 49160 | tf_op jit(solution)/shard_map/ppermute | solution.py:26
  8.0 1.9 %prepare.1 = (f32[64,128]{1,0:T(8,128)}, f32[64,128]{1,0:T(8,128)}, f32[128,128]{1,0:T(8,128)}, bf16[8,128,128]{2,1,0:T(8,128)(2,1)}) custom-call(f32[64,128]{1,0:T(8,128)} %obs_ref.1, s32[1,64]{1,0:T(1,128)} %bitcast.53, f32[32,64]{1,0:T(8,128)} %bitcast.50, f32[1,32]{1,0:T(1,128)} %bitcast.52, f32[1,128]{1,0:T(1,128)} %bitcast.54, bf16[64,128]{1,0:T(8,128)(2,1)} %left_side.1._), custom_call_target="tpu_custom_call" | custom-call | tf_op jit(solution)/shard_map/prepare/pallas_call | solution.py:106
  9.9 8.2 %all-to-all-start = ((bf16[8,128,128]{2,1,0:T(8,128)(2,1)}), bf16[8,128,128]{2,1,0:T(8,128)(2,1)S(1)}, u32[]{:S(2)}, u32[]{:S(2)}) async-start(bf16[8,128,128]{2,1,0:T(8,128)(2,1)} %get-tuple-element.8), calls=%async_computation | async-start | bytes 524288 | tf_op jit(solution)/shard_map/all_to_all | solution.py:196
  18.0 0.7 constant_dynamic-update-slice_fusion.7
  18.8 0.7 constant_dynamic-update-slice_fusion.3
  19.6 1.4 %collective-permute-start.5 = (bf16[4,64,128]{2,1,0:T(8,128)(2,1)S(1)}, bf16[4,64,128]{2,1,0:T(8,128)(2,1)S(1)}, u32[]{:S(2)}, u32[]{:S(2)}) collective-permute-start(bf16[4,64,128]{2,1,0:T(8,128)(2,1)S(1)} %bitcast.37), channel_id=1, source_target_pairs={{192,0},{0,64},{64,128},{128,192},{193,1},{1,65},{65,129},{129,193... | collective-permute-start | bytes 196616 | tf_op jit(solution)/shard_map/ppermute | solution.py:26
  21.0 2.6 %collective-permute-start.4 = (bf16[4,64,128]{2,1,0:T(8,128)(2,1)S(1)}, bf16[4,64,128]{2,1,0:T(8,128)(2,1)S(1)}, u32[]{:S(2)}, u32[]{:S(2)}) collective-permute-start(bf16[4,64,128]{2,1,0:T(8,128)(2,1)S(1)} %bitcast.38), channel_id=1, source_target_pairs={{128,0},{192,64},{0,128},{64,192},{129,1},{193,65},{1,129},{65,193... | collective-permute-start | bytes 196616 | tf_op jit(solution)/shard_map/ppermute | solution.py:26
  23.6 1.1 %collective-permute-start.3 = (bf16[4,64,128]{2,1,0:T(8,128)(2,1)S(1)}, bf16[4,64,128]{2,1,0:T(8,128)(2,1)S(1)}, u32[]{:S(2)}, u32[]{:S(2)}) collective-permute-start(bf16[4,64,128]{2,1,0:T(8,128)(2,1)S(1)} %bitcast.39), channel_id=1, source_target_pairs={{64,0},{128,64},{192,128},{0,192},{65,1},{129,65},{193,129},{1,193... | collective-permute-start | bytes 196616 | tf_op jit(solution)/shard_map/ppermute | solution.py:26
  24.7 2.7 %collective-permute-done.3 = bf16[4,64,128]{2,1,0:T(8,128)(2,1)S(1)} collective-permute-done((bf16[4,64,128]{2,1,0:T(8,128)(2,1)S(1)}, bf16[4,64,128]{2,1,0:T(8,128)(2,1)S(1)}, u32[]{:S(2)}, u32[]{:S(2)}) %collective-permute-start.3) | collective-permute-done | bytes 65568 | tf_op jit(solution)/shard_map/ppermute | solution.py:26
  28.1 3.4 %collective-permute-start.6 = (bf16[8,128,128]{2,1,0:T(8,128)(2,1)S(1)}, bf16[8,128,128]{2,1,0:T(8,128)(2,1)S(1)}, u32[]{:S(2)}, u32[]{:S(2)}) collective-permute-start(bf16[8,128,128]{2,1,0:T(8,128)(2,1)S(1)} %all-to-all-done), channel_id=1, source_target_pairs={{32,0},{0,32},{33,1},{1,33},{34,2},{2,34},{35,3},{3,35},{36,4},{4,... | collective-permute-start | bytes 786440 | tf_op jit(solution)/shard_map/ppermute | solution.py:26
  31.9 0.7 collective-permute-done.6
  33.9 12.9 %all_to_all.25 = f16[16,80,128]{2,1,0:T(8,128)(2,1)S(1)} all-to-all(f16[16,80,128]{2,1,0:T(8,128)(2,1)S(1)} %pad_maximum_fusion), channel_id=1, replica_groups=mesh['y'=4,'c'=2,'z'=8,'x'=4] {'y','x'}, dimensions={0} | all-to-all | bytes 655360 | tf_op jit(solution)/shard_map/all_to_all | solution.py:209
  47.2 13.6 %all_to_all.26 = bf16[8,64,128]{2,1,0:T(8,128)(2,1)S(1)} all-to-all(bf16[8,64,128]{2,1,0:T(8,128)(2,1)S(1)} %broadcast_in_dim.27), channel_id=1, replica_groups=mesh['y'=4,'c'=2,'z'=8,'x'=4] {'z'}, dimensions={0} | all-to-all | bytes 262144 | tf_op jit(solution)/shard_map/all_to_all | solution.py:38
  60.7 2.9 %collective-permute-start.7 = (bf16[512,128]{1,0:T(8,128)(2,1)S(1)}, bf16[512,128]{1,0:T(8,128)(2,1)S(1)}, u32[]{:S(2)}, u32[]{:S(2)}) collective-permute-start(bf16[512,128]{1,0:T(8,128)(2,1)S(1)} %bitcast.33), channel_id=1, source_target_pairs={{32,0},{0,32},{33,1},{1,33},{34,2},{2,34},{35,3},{3,35},{36,4},{4,... | collective-permute-start | bytes 393224 | tf_op jit(solution)/shard_map/ppermute | solution.py:26
  65.3 11.4 %all_to_all.27 = f16[16,80,128]{2,1,0:T(8,128)(2,1)S(1)} all-to-all(f16[16,80,128]{2,1,0:T(8,128)(2,1)S(1)} %pad_maximum_fusion.1), channel_id=1, replica_groups=mesh['y'=4,'c'=2,'z'=8,'x'=4] {'y','x'}, dimensions={0} | all-to-all | bytes 655360 | tf_op jit(solution)/shard_map/all_to_all | solution.py:209
  77.5 1.4 %measure.1 = f32[1,128]{1,0:T(1,128)} custom-call(f32[64,128]{1,0:T(8,128)} %get-tuple-element.6.v0_ref, f32[64,128]{1,0:T(8,128)} %copy-done, f32[64,128]{1,0:T(8,128)} %multiply_add_fusion.v2_ref), custom_call_target="tpu_custom_call" | custom-call | tf_op jit(solution)/shard_map/measure/pallas_call | solution.py:143
  78.9 1.5 %collective-permute-start.8 = (f32[1,128]{1,0:T(1,128)}, f32[1,128]{1,0:T(1,128)S(1)}, u32[]{:S(2)}, u32[]{:S(2)}) collective-permute-start(f32[1,128]{1,0:T(1,128)} %measure.1), channel_id=1, source_target_pairs={{32,0},{0,32},{33,1},{1,33},{34,2},{2,34},{35,3},{3,35},{36,4},{4,... | collective-permute-start | bytes 1544 | tf_op jit(solution)/shard_map/ppermute | solution.py:26
  80.4 1.0 collective-permute-done.8
  81.3 0.7 add_bitcast_fusion
  82.0 16.9 %all_to_all.28 = f32[128,1,128]{2,1,0:T(1,128)} all-to-all(f32[128,1,128]{2,1,0:T(1,128)S(1)} %broadcast_in_dim.29), channel_id=1, replica_groups=mesh['y'=4,'c'=2,'z'=8,'x'=4] {'y','z','x'}, dimensions={0} | all-to-all | bytes 131072 | tf_op jit(solution)/shard_map/all_to_all | solution.py:38
  98.9 1.6 %finish.1 = (f32[64,128]{1,0:T(8,128)}, f32[64,128]{1,0:T(8,128)}) custom-call(f32[128,128]{1,0:T(8,128)} %bitcast.46, f32[64,128]{1,0:T(8,128)} %get-tuple-element.6.v0_ref, f32[64,128]{1,0:T(8,128)} %copy-done, f32[64,128]{1,0:T(8,128)} %multiply_add_fusion.v2_ref), custom_call_target="tpu_custom_call" | custom-call | tf_op jit(solution)/shard_map/finish/pallas_call | solution.py:173
  (62 shorter events, 4.9 us)
Async XLA Ops:
  2.3 16.5 %collective-permute-start.2 = (bf16[64,128]{1,0:T(8,128)(2,1)}, bf16[64,128]{1,0:T(8,128)(2,1)S(1)}, u32[]{:S(2)}, u32[]{:S(2)}) collective-permute-start(bf16[64,128]{1,0:T(8,128)(2,1)} %left_side.1._), channel_id=1, source_target_pairs={{3,0},{0,1},{1,2},{2,3},{7,4},{4,5},{5,6},{6,7},{11,8},{8,9},{9,10... | collective-permute-start | bytes 49160 | tf_op jit(solution)/shard_map/ppermute | solution.py:26
  4.4 14.4 %collective-permute-start.1 = (bf16[64,128]{1,0:T(8,128)(2,1)}, bf16[64,128]{1,0:T(8,128)(2,1)S(1)}, u32[]{:S(2)}, u32[]{:S(2)}) collective-permute-start(bf16[64,128]{1,0:T(8,128)(2,1)} %left_side.1._), channel_id=1, source_target_pairs={{2,0},{3,1},{0,2},{1,3},{6,4},{7,5},{4,6},{5,7},{10,8},{11,9},{8,1... | collective-permute-start | bytes 49160 | tf_op jit(solution)/shard_map/ppermute | solution.py:26
  6.8 11.9 %collective-permute-start = (bf16[64,128]{1,0:T(8,128)(2,1)}, bf16[64,128]{1,0:T(8,128)(2,1)S(1)}, u32[]{:S(2)}, u32[]{:S(2)}) collective-permute-start(bf16[64,128]{1,0:T(8,128)(2,1)} %left_side.1._), channel_id=1, source_target_pairs={{1,0},{2,1},{3,2},{0,3},{5,4},{6,5},{7,6},{4,7},{9,8},{10,9},{11,1... | collective-permute-start | bytes 49160 | tf_op jit(solution)/shard_map/ppermute | solution.py:26
  9.9 17.7 %all-to-all-start = ((bf16[8,128,128]{2,1,0:T(8,128)(2,1)}), bf16[8,128,128]{2,1,0:T(8,128)(2,1)S(1)}, u32[]{:S(2)}, u32[]{:S(2)}) async-start(bf16[8,128,128]{2,1,0:T(8,128)(2,1)} %get-tuple-element.8), calls=%async_computation | async-start | bytes 524288 | tf_op jit(solution)/shard_map/all_to_all | solution.py:196
  19.6 7.8 %collective-permute-start.5 = (bf16[4,64,128]{2,1,0:T(8,128)(2,1)S(1)}, bf16[4,64,128]{2,1,0:T(8,128)(2,1)S(1)}, u32[]{:S(2)}, u32[]{:S(2)}) collective-permute-start(bf16[4,64,128]{2,1,0:T(8,128)(2,1)S(1)} %bitcast.37), channel_id=1, source_target_pairs={{192,0},{0,64},{64,128},{128,192},{193,1},{1,65},{65,129},{129,193... | collective-permute-start | bytes 196616 | tf_op jit(solution)/shard_map/ppermute | solution.py:26
  21.0 6.4 %collective-permute-start.4 = (bf16[4,64,128]{2,1,0:T(8,128)(2,1)S(1)}, bf16[4,64,128]{2,1,0:T(8,128)(2,1)S(1)}, u32[]{:S(2)}, u32[]{:S(2)}) collective-permute-start(bf16[4,64,128]{2,1,0:T(8,128)(2,1)S(1)} %bitcast.38), channel_id=1, source_target_pairs={{128,0},{192,64},{0,128},{64,192},{129,1},{193,65},{1,129},{65,193... | collective-permute-start | bytes 196616 | tf_op jit(solution)/shard_map/ppermute | solution.py:26
  23.6 3.8 %collective-permute-start.3 = (bf16[4,64,128]{2,1,0:T(8,128)(2,1)S(1)}, bf16[4,64,128]{2,1,0:T(8,128)(2,1)S(1)}, u32[]{:S(2)}, u32[]{:S(2)}) collective-permute-start(bf16[4,64,128]{2,1,0:T(8,128)(2,1)S(1)} %bitcast.39), channel_id=1, source_target_pairs={{64,0},{128,64},{192,128},{0,192},{65,1},{129,65},{193,129},{1,193... | collective-permute-start | bytes 196616 | tf_op jit(solution)/shard_map/ppermute | solution.py:26
  28.1 4.5 %collective-permute-start.6 = (bf16[8,128,128]{2,1,0:T(8,128)(2,1)S(1)}, bf16[8,128,128]{2,1,0:T(8,128)(2,1)S(1)}, u32[]{:S(2)}, u32[]{:S(2)}) collective-permute-start(bf16[8,128,128]{2,1,0:T(8,128)(2,1)S(1)} %all-to-all-done), channel_id=1, source_target_pairs={{32,0},{0,32},{33,1},{1,33},{34,2},{2,34},{35,3},{3,35},{36,4},{4,... | collective-permute-start | bytes 786440 | tf_op jit(solution)/shard_map/ppermute | solution.py:26
  33.7 13.2 %copy-start.1 = (f32[64,128]{1,0:T(8,128)S(1)}, f32[64,128]{1,0:T(8,128)}, u32[]{:S(2)}) copy-start(f32[64,128]{1,0:T(8,128)} %get-tuple-element.6.v0_ref) | copy-start | bytes 98308
  33.7 13.2 %copy-start.2 = (f32[64,128]{1,0:T(8,128)S(1)}, f32[64,128]{1,0:T(8,128)}, u32[]{:S(2)}) copy-start(f32[64,128]{1,0:T(8,128)} %get-tuple-element.7) | copy-start | bytes 98308
  33.7 13.2 %copy-start.3 = (f32[128,128]{1,0:T(8,128)S(1)}, f32[128,128]{1,0:T(8,128)}, u32[]{:S(2)}) copy-start(f32[128,128]{1,0:T(8,128)} %get-tuple-element.9) | copy-start | bytes 196612
  46.9 29.9 %copy-start = (f32[64,128]{1,0:T(8,128)}, f32[64,128]{1,0:T(8,128)S(1)}, u32[]{:S(2)}) copy-start(f32[64,128]{1,0:T(8,128)S(1)} %multiply_add_fusion.1.v1_ref) | copy-start | bytes 98308
  60.7 3.9 %collective-permute-start.7 = (bf16[512,128]{1,0:T(8,128)(2,1)S(1)}, bf16[512,128]{1,0:T(8,128)(2,1)S(1)}, u32[]{:S(2)}, u32[]{:S(2)}) collective-permute-start(bf16[512,128]{1,0:T(8,128)(2,1)S(1)} %bitcast.33), channel_id=1, source_target_pairs={{32,0},{0,32},{33,1},{1,33},{34,2},{2,34},{35,3},{3,35},{36,4},{4,... | collective-permute-start | bytes 393224 | tf_op jit(solution)/shard_map/ppermute | solution.py:26
  78.9 2.4 %collective-permute-start.8 = (f32[1,128]{1,0:T(1,128)}, f32[1,128]{1,0:T(1,128)S(1)}, u32[]{:S(2)}, u32[]{:S(2)}) collective-permute-start(f32[1,128]{1,0:T(1,128)} %measure.1), channel_id=1, source_target_pairs={{32,0},{0,32},{33,1},{1,33},{34,2},{2,34},{35,3},{3,35},{36,4},{4,... | collective-permute-start | bytes 1544 | tf_op jit(solution)/shard_map/ppermute | solution.py:26

commit v5 on v4

--- a/solution.py
+++ b/solution.py
@@ -26,11 +26,12 @@
     return lax.ppermute(x, axis, [((i + k) % n, i) for i in range(n)])
 
 
-def around(x, axis):
-    n = lax.axis_size(axis)
-    blocks = [x] + [ahead(x, axis, k) for k in range(1, n)]
-    start = (n - lax.axis_index(axis)) % n * x.shape[0]
-    return lax.dynamic_slice_in_dim(jnp.concatenate(blocks + blocks), start, n * x.shape[0], 0)
+def around(x, axis, base):
+    n, me = lax.axis_size(axis), lax.axis_index(axis)
+    for k in range(n):
+        block = ahead(x, axis, k) if k else x
+        base = lax.dynamic_update_slice_in_dim(base, block, (me + k) % n * x.shape[0], 0)
+    return base
 
 
 def to_all(x, axes):
@@ -86,10 +87,12 @@
     return (lane < column(lengths.astype(f32))).astype(f32)
 
 
-def prepare(observed, lengths, features, length_scale, epoch_gain, left, copies):
+def prepare(observed, lengths, features, length_scale, epoch_gain):
     own, width = observed.shape
 
-    def body(obs_ref, len_ref, feat_ref, scale_ref, gain_ref, _, v_ref, mask_ref, ek_ref, out_ref):
+    def body(obs_ref, len_ref, feat_ref, scale_ref, gain_ref, v_ref, mask_ref, ek_ref, out_ref, left_ref):
+        left, right = sides(feat_ref[...], scale_ref[...], width)
+        left_ref[...] = left
         lane = lax.broadcasted_iota(jnp.int32, (own, width), 1).astype(f32)
         mask = (lane < column(len_ref[...].astype(f32))).astype(f32)
         v = mask * obs_ref[...]
@@ -97,11 +100,9 @@
         mask_ref[...] = mask
         v_ref[...] = v
         ek_ref[...] = ek
-        w = jnp.dot(v, ek, precision=HIGHEST, preferred_element_type=f32).astype(bf16)
-        right = sides(feat_ref[...], scale_ref[...], width)[1]
-        for k in range(copies):
-            out_ref[k, :own, :] = w
-            out_ref[k, own:, :] = right
+        w = jnp.dot(v, ek, precision=HIGHEST, preferred_element_type=f32)
+        out_ref[:own, :] = w.astype(bf16)
+        out_ref[own:, :] = right
 
     return pl.pallas_call(
         body,
@@ -109,30 +110,20 @@
             jax.ShapeDtypeStruct((own, width), f32),
             jax.ShapeDtypeStruct((own, width), f32),
             jax.ShapeDtypeStruct((width, width), f32),
-            jax.ShapeDtypeStruct((copies, 2 * own, width), bf16),
+            jax.ShapeDtypeStruct((2 * own, width), bf16),
+            jax.ShapeDtypeStruct((own, width), bf16),
         ),
-        in_specs=[VMEM] * 5 + [ANY],
-        out_specs=(VMEM,) * 4,
+        in_specs=[VMEM] * 5,
+        out_specs=(VMEM,) * 5,
         name="prepare",
-    )(observed, lengths, features, length_scale, epoch_gain, left)
-
-
-def left_side(features, length_scale, width):
-    def body(feat_ref, scale_ref, left_ref):
-        left_ref[...] = sides(feat_ref[...], scale_ref[...], width)[0]
-
-    return pl.pallas_call(
-        body,
-        out_shape=jax.ShapeDtypeStruct((features.shape[1], width), bf16),
-        in_specs=[VMEM] * 2,
-        out_specs=VMEM,
-        name="left_side",
-    )(features, length_scale)
-
-
-def measure(v0, v1, v2):
-    def body(v0_ref, v1_ref, v2_ref, m_ref):
-        v0, v1, v2 = v0_ref[...], v1_ref[...], v2_ref[...]
+    )(observed, lengths, features, length_scale, epoch_gain)
+
+
+def measure(p, mask, v0, v1):
+    def body(p_ref, mask_ref, v0_ref, v1_ref, v2_ref, m_ref):
+        v0, v1 = v0_ref[...], v1_ref[...]
+        v2 = mask_ref[...] * p_ref[...] + noise_level * v1
+        v2_ref[...] = v2
         lane = lax.broadcasted_iota(jnp.int32, m_ref.shape, 1)
         m = jnp.zeros(m_ref.shape, f32)
         for k, (a, b) in enumerate(((v0, v0), (v0, v1), (v1, v1), (v1, v2))):
@@ -140,18 +131,22 @@
             m = jnp.where(lane == k, total, m)
         m_ref[...] = m
 
+    own, width = v0.shape
     return pl.pallas_call(
         body,
-        out_shape=jax.ShapeDtypeStruct((1, v0.shape[1]), f32),
-        in_specs=[VMEM] * 3,
-        out_specs=VMEM,
+        out_shape=(jax.ShapeDtypeStruct((own, width), f32), jax.ShapeDtypeStruct((1, width), f32)),
+        in_specs=[VMEM] * 4,
+        out_specs=(VMEM,) * 2,
         name="measure",
-    )(v0, v1, v2)
+    )(p, mask, v0, v1)
 
 
 def finish(moments, v0, v1, v2):
-    def body(m_ref, v0_ref, v1_ref, v2_ref, x_ref, r_ref):
-        m = jnp.sum(m_ref[...], axis=0, keepdims=True)
+    n = len(moments)
+
+    def body(*refs):
+        v0_ref, v1_ref, v2_ref, x_ref, r_ref = refs[n:]
+        m = sum(ref[...] for ref in refs[1:n]) + refs[0][...]
         lane = lax.broadcasted_iota(jnp.int32, m.shape, 1)
 
         def moment(k):
@@ -173,10 +168,10 @@
     return pl.pallas_call(
         body,
         out_shape=(out, out),
-        in_specs=[VMEM] * 4,
+        in_specs=[VMEM] * (n + 3),
         out_specs=(VMEM,) * 2,
         name="finish",
-    )(moments, v0, v1, v2)
+    )(*moments, v0, v1, v2)
 
 
 def block_kernel(left, right):
@@ -188,14 +183,11 @@
     own, width = observed.shape
     features, length_scale = features.T, length_scale[None, :]
     lengths, epoch_gain = lengths[None, :], epoch_gain[None, :]
-    left = left_side(features, length_scale, width)
-    line = around(left, X)
-    v0, mask, ek, outgoing = prepare(
-        observed, lengths, features, length_scale, epoch_gain, left, lax.axis_size(Z)
-    )
-    here = lax.all_to_all(outgoing, Z, split_axis=0, concat_axis=0, tiled=True)
-    lefts = around(line.reshape(-1, own, width), Y).reshape(-1, width)
+    v0, mask, ek, outgoing, left = prepare(observed, lengths, features, length_scale, epoch_gain)
+    here = to_all(outgoing, Z)
+    line = around(left, X, jnp.zeros((lax.axis_size(X) * own, width), bf16))
     there = ahead(here, C, 1)
+    lefts = around(line, Y, here.reshape(-1, width))
     k_here = block_kernel(lefts, here[:, own:].reshape(-1, width))
     k_there = block_kernel(lefts, there[:, own:].reshape(-1, width))
 
@@ -205,7 +197,7 @@
         top = jnp.maximum(*(jnp.max(jnp.abs(w.astype(f32)), axis=0) for w in (w_here, w_there)))
         power = jnp.ceil(jnp.log2(jnp.maximum(top, 1e-30) * (2 * w_here.shape[0])))
         part = (part * jnp.exp2(15.0 - power)).astype(f16).reshape(-1, own, width)
-        tail = jnp.broadcast_to(power.astype(f16), (part.shape[0], 16, width))
+        tail = jnp.broadcast_to(power.astype(f16), (part.shape[0], 8, width))
         got = lax.all_to_all(
             jnp.concatenate([part, tail], axis=1), (Y, X), split_axis=0, concat_axis=0, tiled=True
         )
@@ -217,10 +209,9 @@
     w = jnp.dot(mask * v1, ek, precision=HIGHEST, preferred_element_type=f32).astype(bf16)
     w_here = to_all(w, Z).reshape(-1, width)
     p = product(w_here, ahead(w_here, C, 1))
-    v2 = mask * p + noise_level * v1
-    m = measure(v0, v1, v2)
-    m = to_all(m + ahead(m, C, 1), (Y, Z, X)).reshape(-1, width)
-    return finish(m, v0, v1, v2)
+    v2, m = measure(p, mask, v0, v1)
+    m = jnp.sum(to_all(m, (C, Z, X)), axis=0)
+    return finish([m] + [ahead(m, Y, k) for k in range(1, lax.axis_size(Y))], v0, v1, v2)
 
 
 def solution(mesh):

time: 101 us -> 102 us (level); the launches traced: 101 us -> 100 us
  starting transfers between devices: 26.7 us -> 31.2 us
  blocking collectives: 54.9 us -> 51.2 us
  local copies, waits for them, and re-layouts: 1.81 us -> 3.69 us
  Pallas kernels: 6.59 us -> 4.78 us
    ppermute x9 -> x11, starting transfers between devices: 18.5 us -> 22.2 us  [ahead(): return lax.ppermute(x, axis, [((i + k) % n, i) for i in range(n)])]
    all_to_all x2, blocking collectives: 30.5 us -> 28.1 us  [to_all(): return lax.all_to_all(copies, axes, split_axis=0, concat_axis=0, tiled=True)]
    broadcast_in_dim x2 -> x3, local copies, waits for them, and re-layouts: 0.06 us -> 2.15 us  [to_all(): copies = jnp.broadcast_to(x, (lax.axis_size(axes), *x.shape))]
    pallas_call x3 -> x2, Pallas kernels: 4.71 us -> 2.99 us  [the longest x1 1.54 us: finish(): pl.pallas_call(body, out_shape=(out, out), in_specs=[VMEM] * (n + 3), out...]
    add x2 -> x0, other arithmetic: 1.27 us -> none  [the longest x1 0.66 us: per_device(): m = to_all(m + ahead(m, C, 1), (Y, Z, X)).reshape(-1, width)]
    all_to_all x2, blocking collectives: 24.4 us -> 23.1 us  [product(): lax.all_to_all(jnp.concatenate([part, tail], axis=1), (Y, X), split_axis=...]
    ppermute x9 -> x11, waiting for transfers between devices: 4.93 us -> 4.3 us  [ahead(): return lax.ppermute(x, axis, [((i + k) % n, i) for i in range(n)])]
  transfers between devices with their start and end apart: 10 -> 12, of which waited for: 4 -> 6; matrix products, arithmetic and copies ran while one was open for 3% -> 1% of each run, Pallas kernels for 2% -> 0%
where the time goes in v5:
time: 102 us; the launch traced here: 100 us
  blocking collectives  51.2 us (50%)
  starting transfers between devices  31.2 us (31%)
  Pallas kernels  4.78 us (5%)
  waiting for transfers between devices  4.3 us (4%)
  local copies, waits for them, and re-layouts  3.69 us (4%)
  matrix products  2.93 us (3%)
  other arithmetic  1.15 us (1%)
    all_to_all x2, blocking collectives, to_all(): return lax.all_to_all(copies, axes, split_axis=0, concat_axis=0, tiled=True)  28.1 us
    all_to_all x2, blocking collectives, product(): lax.all_to_all(jnp.concatenate([part, tail], axis=1), (Y, X), split_axis=...  23.1 us
    ppermute x11, starting transfers between devices, ahead(): return lax.ppermute(x, axis, [((i + k) % n, i) for i in range(n)])  22.2 us
    all_to_all x1, starting transfers between devices, to_all(): return lax.all_to_all(copies, axes, split_axis=0, concat_axis=0, tiled=True)  9.01 us
    ppermute x11, waiting for transfers between devices, ahead(): return lax.ppermute(x, axis, [((i + k) % n, i) for i in range(n)])  4.3 us
    broadcast_in_dim x3, local copies, waits for them, and re-layouts, to_all(): copies = jnp.broadcast_to(x, (lax.axis_size(axes), *x.shape))  2.15 us
  transfers between devices with their start and end apart: 12, of which 6 were waited for; matrix products, arithmetic and copies ran while one was open for 1% of the time, Pallas kernels for 0%

profile of v5, /device:TPU:1, one launch (start us, length us, event | category | flops | bytes accessed | tf_op | source)
XLA Modules:
  0.0 100.1 jit_solution(6633152146668952606)
XLA Ops:
  0.6 1.8 %prepare.1 = (f32[64,128]{1,0:T(8,128)}, f32[64,128]{1,0:T(8,128)}, f32[128,128]{1,0:T(8,128)}, bf16[128,128]{1,0:T(8,128)(2,1)}, bf16[64,128]{1,0:T(8,128)(2,1)}) custom-call(f32[64,128]{1,0:T(8,128)} %obs_ref.1, s32[1,64]{1,0:T(1,128)} %bitcast.47, f32[32,64]{1,0:T(8,128)} %bitcast.42, f32[1,32]{1,0:T(1,128)} %bitcast.48, f32[1,128]{1,0:T(1,128)} %bitcast.49), custom_call_target="tpu_custom_call" | custom-call | tf_op jit(solution)/shard_map/prepare/pallas_call | solution.py:107
  2.4 1.5 %broadcast_in_dim.32 = bf16[8,128,128]{2,1,0:T(8,128)(2,1)} broadcast(bf16[128,128]{1,0:T(8,128)(2,1)} %get-tuple-element.9), dimensions={1,2} | broadcast | bytes 294912 | tf_op jit(solution)/shard_map/broadcast_in_dim | solution.py:38
  3.9 9.0 %all-to-all-start = ((bf16[8,128,128]{2,1,0:T(8,128)(2,1)}), bf16[8,128,128]{2,1,0:T(8,128)(2,1)S(1)}, u32[]{:S(2)}, u32[]{:S(2)}) async-start(bf16[8,128,128]{2,1,0:T(8,128)(2,1)} %broadcast_in_dim.32), calls=%async_computation | async-start | bytes 524288 | tf_op jit(solution)/shard_map/all_to_all | solution.py:39
  12.9 1.2 %collective-permute-start.2 = (bf16[64,128]{1,0:T(8,128)(2,1)}, bf16[64,128]{1,0:T(8,128)(2,1)S(1)}, u32[]{:S(2)}, u32[]{:S(2)}) collective-permute-start(bf16[64,128]{1,0:T(8,128)(2,1)} %get-tuple-element.10), channel_id=1, source_target_pairs={{3,0},{0,1},{1,2},{2,3},{7,4},{4,5},{5,6},{6,7},{11,8},{8,9},{9,10... | collective-permute-start | bytes 49160 | tf_op jit(solution)/shard_map/ppermute | solution.py:26
  14.1 2.5 %collective-permute-start.1 = (bf16[64,128]{1,0:T(8,128)(2,1)}, bf16[64,128]{1,0:T(8,128)(2,1)S(1)}, u32[]{:S(2)}, u32[]{:S(2)}) collective-permute-start(bf16[64,128]{1,0:T(8,128)(2,1)} %get-tuple-element.10), channel_id=1, source_target_pairs={{2,0},{3,1},{0,2},{1,3},{6,4},{7,5},{4,6},{5,7},{10,8},{11,9},{8,1... | collective-permute-start | bytes 49160 | tf_op jit(solution)/shard_map/ppermute | solution.py:26
  16.6 1.2 %collective-permute-start = (bf16[64,128]{1,0:T(8,128)(2,1)}, bf16[64,128]{1,0:T(8,128)(2,1)S(1)}, u32[]{:S(2)}, u32[]{:S(2)}) collective-permute-start(bf16[64,128]{1,0:T(8,128)(2,1)} %get-tuple-element.10), channel_id=1, source_target_pairs={{1,0},{2,1},{3,2},{0,3},{5,4},{6,5},{7,6},{4,7},{9,8},{10,9},{11,1... | collective-permute-start | bytes 49160 | tf_op jit(solution)/shard_map/ppermute | solution.py:26
  17.8 0.7 constant_dynamic-update-slice_fusion.7
  18.5 1.2 %collective-permute-done = bf16[64,128]{1,0:T(8,128)(2,1)S(1)} collective-permute-done((bf16[64,128]{1,0:T(8,128)(2,1)}, bf16[64,128]{1,0:T(8,128)(2,1)S(1)}, u32[]{:S(2)}, u32[]{:S(2)}) %collective-permute-start) | collective-permute-done | bytes 16416 | tf_op jit(solution)/shard_map/ppermute | solution.py:26
  19.7 1.4 %collective-permute-start.5 = (bf16[256,128]{1,0:T(8,128)(2,1)S(1)}, bf16[256,128]{1,0:T(8,128)(2,1)S(1)}, u32[]{:S(2)}, u32[]{:S(2)}) collective-permute-start(bf16[256,128]{1,0:T(8,128)(2,1)S(1)} %constant_dynamic-update-slice_fusion.4), channel_id=1, source_target_pairs={{192,0},{0,64},{64,128},{128,192},{193,1},{1,65},{65,129},{129,193... | collective-permute-start | bytes 196616 | tf_op jit(solution)/shard_map/ppermute | solution.py:26
  21.1 2.6 %collective-permute-start.4 = (bf16[256,128]{1,0:T(8,128)(2,1)S(1)}, bf16[256,128]{1,0:T(8,128)(2,1)S(1)}, u32[]{:S(2)}, u32[]{:S(2)}) collective-permute-start(bf16[256,128]{1,0:T(8,128)(2,1)S(1)} %constant_dynamic-update-slice_fusion.4), channel_id=1, source_target_pairs={{128,0},{192,64},{0,128},{64,192},{129,1},{193,65},{1,129},{65,193... | collective-permute-start | bytes 196616 | tf_op jit(solution)/shard_map/ppermute | solution.py:26
  23.7 1.1 %collective-permute-start.3 = (bf16[256,128]{1,0:T(8,128)(2,1)S(1)}, bf16[256,128]{1,0:T(8,128)(2,1)S(1)}, u32[]{:S(2)}, u32[]{:S(2)}) collective-permute-start(bf16[256,128]{1,0:T(8,128)(2,1)S(1)} %constant_dynamic-update-slice_fusion.4), channel_id=1, source_target_pairs={{64,0},{128,64},{192,128},{0,192},{65,1},{129,65},{193,129},{1,193... | collective-permute-start | bytes 196616 | tf_op jit(solution)/shard_map/ppermute | solution.py:26
  24.8 3.2 %collective-permute-start.6 = (bf16[8,128,128]{2,1,0:T(8,128)(2,1)S(1)}, bf16[8,128,128]{2,1,0:T(8,128)(2,1)S(1)}, u32[]{:S(2)}, u32[]{:S(2)}) collective-permute-start(bf16[8,128,128]{2,1,0:T(8,128)(2,1)S(1)} %all-to-all-done), channel_id=1, source_target_pairs={{32,0},{0,32},{33,1},{1,33},{34,2},{2,34},{35,3},{3,35},{36,4},{4,... | collective-permute-start | bytes 786440 | tf_op jit(solution)/shard_map/ppermute | solution.py:26
  28.1 1.1 %collective-permute-done.6 = bf16[8,128,128]{2,1,0:T(8,128)(2,1)S(1)} collective-permute-done((bf16[8,128,128]{2,1,0:T(8,128)(2,1)S(1)}, bf16[8,128,128]{2,1,0:T(8,128)(2,1)S(1)}, u32[]{:S(2)}, u32[]{:S(2)}) %collective-permute-start.6) | collective-permute-done | bytes 262176 | tf_op jit(solution)/shard_map/ppermute | solution.py:26
  31.4 12.0 %all_to_all.25 = f16[16,72,128]{2,1,0:T(8,128)(2,1)S(1)} all-to-all(f16[16,72,128]{2,1,0:T(8,128)(2,1)S(1)} %pad_maximum_fusion), channel_id=1, replica_groups=mesh['y'=4,'c'=2,'z'=8,'x'=4] {'y','x'}, dimensions={0} | all-to-all | bytes 589824 | tf_op jit(solution)/shard_map/all_to_all | solution.py:201
  43.8 14.0 %all_to_all.26 = bf16[8,64,128]{2,1,0:T(8,128)(2,1)S(1)} all-to-all(bf16[8,64,128]{2,1,0:T(8,128)(2,1)S(1)} %broadcast_in_dim.35), channel_id=1, replica_groups=mesh['y'=4,'c'=2,'z'=8,'x'=4] {'z'}, dimensions={0} | all-to-all | bytes 262144 | tf_op jit(solution)/shard_map/all_to_all | solution.py:39
  57.8 6.4 %collective-permute-start.7 = (bf16[512,128]{1,0:T(8,128)(2,1)S(1)}, bf16[512,128]{1,0:T(8,128)(2,1)S(1)}, u32[]{:S(2)}, u32[]{:S(2)}) collective-permute-start(bf16[512,128]{1,0:T(8,128)(2,1)S(1)} %bitcast.33), channel_id=1, source_target_pairs={{32,0},{0,32},{33,1},{1,33},{34,2},{2,34},{35,3},{3,35},{36,4},{4,... | collective-permute-start | bytes 393224 | tf_op jit(solution)/shard_map/ppermute | solution.py:26
  65.8 11.1 %all_to_all.27 = f16[16,72,128]{2,1,0:T(8,128)(2,1)S(1)} all-to-all(f16[16,72,128]{2,1,0:T(8,128)(2,1)S(1)} %pad_maximum_fusion.1), channel_id=1, replica_groups=mesh['y'=4,'c'=2,'z'=8,'x'=4] {'y','x'}, dimensions={0} | all-to-all | bytes 589824 | tf_op jit(solution)/shard_map/all_to_all | solution.py:201
  76.9 0.7 multiply_reduce_fusion.p_ref
  77.6 1.4 %measure.1 = (f32[64,128]{1,0:T(8,128)}, f32[1,128]{1,0:T(1,128)}) custom-call(f32[64,128]{1,0:T(8,128)} %multiply_reduce_fusion.p_ref, f32[64,128]{1,0:T(8,128)} %get-tuple-element.11.mask_ref, f32[64,128]{1,0:T(8,128)} %get-tuple-element.12.v0_ref.refs_4_, f32[64,128]{1,0:T(8,128)} %copy-done), custom_call_target="tpu_custom_call" | custom-call | tf_op jit(solution)/shard_map/measure/pallas_call | solution.py:135
  79.7 14.0 %all_to_all.28 = f32[64,1,128]{2,1,0:T(1,128)S(1)} all-to-all(f32[64,1,128]{2,1,0:T(1,128)S(1)} %broadcast_in_dim.37), channel_id=1, replica_groups=mesh['y'=4,'c'=2,'z'=8,'x'=4] {'c','z','x'}, dimensions={0} | all-to-all | bytes 65536 | tf_op jit(solution)/shard_map/all_to_all | solution.py:39
  93.8 1.7 %collective-permute-start.9 = (f32[1,128]{1,0:T(1,128)S(1)}, f32[1,128]{1,0:T(1,128)S(1)}, u32[]{:S(2)}, u32[]{:S(2)}) collective-permute-start(f32[1,128]{1,0:T(1,128)S(1)} %bitcast.44), channel_id=1, source_target_pairs={{128,0},{192,64},{0,128},{64,192},{129,1},{193,65},{1,129},{65,193... | collective-permute-start | bytes 1544 | tf_op jit(solution)/shard_map/ppermute | solution.py:26
  95.6 0.9 collective-permute-start.8
  96.5 0.9 collective-permute-done.10.refs_3_
  98.6 1.5 %finish.1 = (f32[64,128]{1,0:T(8,128)}, f32[64,128]{1,0:T(8,128)}) custom-call(f32[1,128]{1,0:T(1,128)} %bitcast.46, f32[1,128]{1,0:T(1,128)} %copy-done.7, f32[1,128]{1,0:T(1,128)} %copy-done.6, f32[1,128]{1,0:T(1,128)} %copy-done.5, f32[64,128]{1,0:T(8,128)} %get-tuple-element.12.v0_ref.refs_4_, f32[64,128]{1,0:T(8,128)} %copy-done, ...), custom_call_target="tpu_custom_call" | custom-call | tf_op jit(solution)/shard_map/finish/pallas_call | solution.py:168
  (64 shorter events, 6.0 us)
Async XLA Ops:
  3.9 20.9 %all-to-all-start = ((bf16[8,128,128]{2,1,0:T(8,128)(2,1)}), bf16[8,128,128]{2,1,0:T(8,128)(2,1)S(1)}, u32[]{:S(2)}, u32[]{:S(2)}) async-start(bf16[8,128,128]{2,1,0:T(8,128)(2,1)} %broadcast_in_dim.32), calls=%async_computation | async-start | bytes 524288 | tf_op jit(solution)/shard_map/all_to_all | solution.py:39
  12.9 6.8 %collective-permute-start.2 = (bf16[64,128]{1,0:T(8,128)(2,1)}, bf16[64,128]{1,0:T(8,128)(2,1)S(1)}, u32[]{:S(2)}, u32[]{:S(2)}) collective-permute-start(bf16[64,128]{1,0:T(8,128)(2,1)} %get-tuple-element.10), channel_id=1, source_target_pairs={{3,0},{0,1},{1,2},{2,3},{7,4},{4,5},{5,6},{6,7},{11,8},{8,9},{9,10... | collective-permute-start | bytes 49160 | tf_op jit(solution)/shard_map/ppermute | solution.py:26
  14.1 5.6 %collective-permute-start.1 = (bf16[64,128]{1,0:T(8,128)(2,1)}, bf16[64,128]{1,0:T(8,128)(2,1)S(1)}, u32[]{:S(2)}, u32[]{:S(2)}) collective-permute-start(bf16[64,128]{1,0:T(8,128)(2,1)} %get-tuple-element.10), channel_id=1, source_target_pairs={{2,0},{3,1},{0,2},{1,3},{6,4},{7,5},{4,6},{5,7},{10,8},{11,9},{8,1... | collective-permute-start | bytes 49160 | tf_op jit(solution)/shard_map/ppermute | solution.py:26
  16.6 3.1 %collective-permute-start = (bf16[64,128]{1,0:T(8,128)(2,1)}, bf16[64,128]{1,0:T(8,128)(2,1)S(1)}, u32[]{:S(2)}, u32[]{:S(2)}) collective-permute-start(bf16[64,128]{1,0:T(8,128)(2,1)} %get-tuple-element.10), channel_id=1, source_target_pairs={{1,0},{2,1},{3,2},{0,3},{5,4},{6,5},{7,6},{4,7},{9,8},{10,9},{11,1... | collective-permute-start | bytes 49160 | tf_op jit(solution)/shard_map/ppermute | solution.py:26
  19.7 9.6 %collective-permute-start.5 = (bf16[256,128]{1,0:T(8,128)(2,1)S(1)}, bf16[256,128]{1,0:T(8,128)(2,1)S(1)}, u32[]{:S(2)}, u32[]{:S(2)}) collective-permute-start(bf16[256,128]{1,0:T(8,128)(2,1)S(1)} %constant_dynamic-update-slice_fusion.4), channel_id=1, source_target_pairs={{192,0},{0,64},{64,128},{128,192},{193,1},{1,65},{65,129},{129,193... | collective-permute-start | bytes 196616 | tf_op jit(solution)/shard_map/ppermute | solution.py:26
  21.1 8.2 %collective-permute-start.4 = (bf16[256,128]{1,0:T(8,128)(2,1)S(1)}, bf16[256,128]{1,0:T(8,128)(2,1)S(1)}, u32[]{:S(2)}, u32[]{:S(2)}) collective-permute-start(bf16[256,128]{1,0:T(8,128)(2,1)S(1)} %constant_dynamic-update-slice_fusion.4), channel_id=1, source_target_pairs={{128,0},{192,64},{0,128},{64,192},{129,1},{193,65},{1,129},{65,193... | collective-permute-start | bytes 196616 | tf_op jit(solution)/shard_map/ppermute | solution.py:26
  23.7 5.6 %collective-permute-start.3 = (bf16[256,128]{1,0:T(8,128)(2,1)S(1)}, bf16[256,128]{1,0:T(8,128)(2,1)S(1)}, u32[]{:S(2)}, u32[]{:S(2)}) collective-permute-start(bf16[256,128]{1,0:T(8,128)(2,1)S(1)} %constant_dynamic-update-slice_fusion.4), channel_id=1, source_target_pairs={{64,0},{128,64},{192,128},{0,192},{65,1},{129,65},{193,129},{1,193... | collective-permute-start | bytes 196616 | tf_op jit(solution)/shard_map/ppermute | solution.py:26
  24.8 4.4 %collective-permute-start.6 = (bf16[8,128,128]{2,1,0:T(8,128)(2,1)S(1)}, bf16[8,128,128]{2,1,0:T(8,128)(2,1)S(1)}, u32[]{:S(2)}, u32[]{:S(2)}) collective-permute-start(bf16[8,128,128]{2,1,0:T(8,128)(2,1)S(1)} %all-to-all-done), channel_id=1, source_target_pairs={{32,0},{0,32},{33,1},{1,33},{34,2},{2,34},{35,3},{3,35},{36,4},{4,... | collective-permute-start | bytes 786440 | tf_op jit(solution)/shard_map/ppermute | solution.py:26
  31.3 12.3 %copy-start.1 = (f32[64,128]{1,0:T(8,128)S(1)}, f32[64,128]{1,0:T(8,128)}, u32[]{:S(2)}) copy-start(f32[64,128]{1,0:T(8,128)} %get-tuple-element.12.v0_ref.refs_4_) | copy-start | bytes 98308
  31.3 12.3 %copy-start.2 = (f32[64,128]{1,0:T(8,128)S(1)}, f32[64,128]{1,0:T(8,128)}, u32[]{:S(2)}) copy-start(f32[64,128]{1,0:T(8,128)} %get-tuple-element.11.mask_ref) | copy-start | bytes 98308
  31.3 12.3 %copy-start.3 = (f32[128,128]{1,0:T(8,128)S(1)}, f32[128,128]{1,0:T(8,128)}, u32[]{:S(2)}) copy-start(f32[128,128]{1,0:T(8,128)} %get-tuple-element.13) | copy-start | bytes 196612
  43.6 21.0 %copy-start = (f32[64,128]{1,0:T(8,128)}, f32[64,128]{1,0:T(8,128)S(1)}, u32[]{:S(2)}) copy-start(f32[64,128]{1,0:T(8,128)S(1)} %multiply_add_fusion.v1_ref.refs_5_) | copy-start | bytes 98308
  57.8 7.3 %collective-permute-start.7 = (bf16[512,128]{1,0:T(8,128)(2,1)S(1)}, bf16[512,128]{1,0:T(8,128)(2,1)S(1)}, u32[]{:S(2)}, u32[]{:S(2)}) collective-permute-start(bf16[512,128]{1,0:T(8,128)(2,1)S(1)} %bitcast.33), channel_id=1, source_target_pairs={{32,0},{0,32},{33,1},{1,33},{34,2},{2,34},{35,3},{3,35},{36,4},{4,... | collective-permute-start | bytes 393224 | tf_op jit(solution)/shard_map/ppermute | solution.py:26
  93.8 4.3 %copy-start.4 = (f32[128]{0:T(128)}, f32[128]{0:T(128)S(1)}, u32[]{:S(2)}) copy-start(f32[128]{0:T(128)S(1)} %reduce_sum.31) | copy-start | bytes 1540
  93.8 3.7 %collective-permute-start.10 = (f32[1,128]{1,0:T(1,128)S(1)}, f32[1,128]{1,0:T(1,128)S(1)}, u32[]{:S(2)}, u32[]{:S(2)}) collective-permute-start(f32[1,128]{1,0:T(1,128)S(1)} %bitcast.43), channel_id=1, source_target_pairs={{192,0},{0,64},{64,128},{128,192},{193,1},{1,65},{65,129},{129,193... | collective-permute-start | bytes 1544 | tf_op jit(solution)/shard_map/ppermute | solution.py:26
  93.8 4.0 %collective-permute-start.9 = (f32[1,128]{1,0:T(1,128)S(1)}, f32[1,128]{1,0:T(1,128)S(1)}, u32[]{:S(2)}, u32[]{:S(2)}) collective-permute-start(f32[1,128]{1,0:T(1,128)S(1)} %bitcast.44), channel_id=1, source_target_pairs={{128,0},{192,64},{0,128},{64,192},{129,1},{193,65},{1,129},{65,193... | collective-permute-start | bytes 1544 | tf_op jit(solution)/shard_map/ppermute | solution.py:26
  95.6 2.5 %collective-permute-start.8 = (f32[1,128]{1,0:T(1,128)S(1)}, f32[1,128]{1,0:T(1,128)S(1)}, u32[]{:S(2)}, u32[]{:S(2)}) collective-permute-start(f32[1,128]{1,0:T(1,128)S(1)} %bitcast.45), channel_id=1, source_target_pairs={{64,0},{128,64},{192,128},{0,192},{65,1},{129,65},{193,129},{1,193... | collective-permute-start | bytes 1544 | tf_op jit(solution)/shard_map/ppermute | solution.py:26
  97.4 0.6 copy-start.5
  97.8 0.5 copy-start.6
  98.0 0.6 copy-start.7

commit v6 on v5

--- a/solution.py
+++ b/solution.py
@@ -119,59 +119,33 @@
     )(observed, lengths, features, length_scale, epoch_gain)
 
 
-def measure(p, mask, v0, v1):
-    def body(p_ref, mask_ref, v0_ref, v1_ref, v2_ref, m_ref):
-        v0, v1 = v0_ref[...], v1_ref[...]
-        v2 = mask_ref[...] * p_ref[...] + noise_level * v1
-        v2_ref[...] = v2
-        lane = lax.broadcasted_iota(jnp.int32, m_ref.shape, 1)
-        m = jnp.zeros(m_ref.shape, f32)
-        for k, (a, b) in enumerate(((v0, v0), (v0, v1), (v1, v1), (v1, v2))):
-            total = jnp.sum(jnp.sum(a * b, axis=0, keepdims=True), axis=1, keepdims=True)
-            m = jnp.where(lane == k, total, m)
-        m_ref[...] = m
+def across(x):
+    ones = jnp.ones((x.shape[1], x.shape[1]), f32)
+    return jnp.dot(x, ones, precision=HIGHEST, preferred_element_type=f32)
 
-    own, width = v0.shape
-    return pl.pallas_call(
-        body,
-        out_shape=(jax.ShapeDtypeStruct((own, width), f32), jax.ShapeDtypeStruct((1, width), f32)),
-        in_specs=[VMEM] * 4,
-        out_specs=(VMEM,) * 2,
-        name="measure",
-    )(p, mask, v0, v1)
+
+def pick(n, width):
+    return jnp.arange(width)[None, :] == jnp.arange(n)[:, None]
+
+
+def measure(v0, v1, v2):
+    m = [jnp.sum(a * b, axis=0) for a, b in ((v0, v0), (v0, v1), (v1, v1), (v1, v2))]
+    m = across(jnp.stack(m))
+    return jnp.sum(jnp.where(pick(*m.shape), m, 0.0), axis=0, keepdims=True)
 
 
 def finish(moments, v0, v1, v2):
-    n = len(moments)
-
-    def body(*refs):
-        v0_ref, v1_ref, v2_ref, x_ref, r_ref = refs[n:]
-        m = sum(ref[...] for ref in refs[1:n]) + refs[0][...]
-        lane = lax.broadcasted_iota(jnp.int32, m.shape, 1)
-
-        def moment(k):
-            return jnp.sum(jnp.where(lane == k, m, 0.0), axis=1, keepdims=True)
-
-        m0, m1, m2, m3 = (moment(k) for k in range(4))
-        alpha = m0 / m1
-        norm = m0 + alpha * (alpha * m2 - 2.0 * m1)
-        keep = 1.0 + norm / m0
-        curve = keep * (keep * m1 - 2.0 * alpha * m2) + alpha * alpha * m3
-        again = norm / curve
-        on0 = alpha + again * keep
-        on1 = again * alpha
-        v0, v1 = v0_ref[...], v1_ref[...]
-        x_ref[...] = on0 * v0 - on1 * v1
-        r_ref[...] = v0 - on0 * v1 + on1 * v2_ref[...]
-
-    out = jax.ShapeDtypeStruct(v0.shape, f32)
-    return pl.pallas_call(
-        body,
-        out_shape=(out, out),
-        in_specs=[VMEM] * (n + 3),
-        out_specs=(VMEM,) * 2,
-        name="finish",
-    )(*moments, v0, v1, v2)
+    m = jnp.sum(moments, axis=0, keepdims=True)
+    m = across(jnp.where(pick(4, m.shape[1]), m, 0.0))
+    m0, m1, m2, m3 = (m[k : k + 1] for k in range(4))
+    alpha = m0 / m1
+    norm = m0 + alpha * (alpha * m2 - 2.0 * m1)
+    keep = 1.0 + norm / m0
+    curve = keep * (keep * m1 - 2.0 * alpha * m2) + alpha * alpha * m3
+    again = norm / curve
+    on0 = alpha + again * keep
+    on1 = again * alpha
+    return on0 * v0 - on1 * v1, v0 - on0 * v1 + on1 * v2
 
 
 def block_kernel(left, right):
@@ -186,8 +160,8 @@
     v0, mask, ek, outgoing, left = prepare(observed, lengths, features, length_scale, epoch_gain)
     here = to_all(outgoing, Z)
     line = around(left, X, jnp.zeros((lax.axis_size(X) * own, width), bf16))
+    lefts = around(line, Y, jnp.zeros((lax.axis_size(Y) * line.shape[0], width), bf16))
     there = ahead(here, C, 1)
-    lefts = around(line, Y, here.reshape(-1, width))
     k_here = block_kernel(lefts, here[:, own:].reshape(-1, width))
     k_there = block_kernel(lefts, there[:, own:].reshape(-1, width))
 
@@ -209,9 +183,10 @@
     w = jnp.dot(mask * v1, ek, precision=HIGHEST, preferred_element_type=f32).astype(bf16)
     w_here = to_all(w, Z).reshape(-1, width)
     p = product(w_here, ahead(w_here, C, 1))
-    v2, m = measure(p, mask, v0, v1)
-    m = jnp.sum(to_all(m, (C, Z, X)), axis=0)
-    return finish([m] + [ahead(m, Y, k) for k in range(1, lax.axis_size(Y))], v0, v1, v2)
+    v2 = mask * p + noise_level * v1
+    m = measure(v0, v1, v2)
+    m = to_all(m + ahead(m, C, 1), (Y, Z, X)).reshape(-1, width)
+    return finish(m, v0, v1, v2)
 
 
 def solution(mesh):

time: 102 us -> 95.1 us (0.932); the launches traced: 100 us -> 94.6 us
  starting transfers between devices: 31.2 us -> 26.8 us
  Pallas kernels: 4.78 us -> 1.79 us
  blocking collectives: 51.2 us -> 52.5 us
  waiting for transfers between devices: 4.3 us -> 5.54 us
  local copies, waits for them, and re-layouts: 3.69 us -> 2.52 us
    ppermute x11 -> x9, starting transfers between devices: 22.2 us -> 18.7 us  [ahead(): return lax.ppermute(x, axis, [((i + k) % n, i) for i in range(n)])]
    pallas_call x2 -> x0, Pallas kernels: 2.99 us -> none  [the longest x1 1.54 us: finish(): pl.pallas_call(body, out_shape=(out, out), in_specs=[VMEM] * (n + 3), out...]
    ppermute x11 -> x9, waiting for transfers between devices: 4.3 us -> 4.74 us  [ahead(): return lax.ppermute(x, axis, [((i + k) % n, i) for i in range(n)])]
  transfers between devices with their start and end apart: 12 -> 10, of which waited for: 6 -> 5; matrix products, arithmetic and copies ran while one was open for 1% -> 3% of each run, Pallas kernels for 0% -> 0%
where the time goes in v6:
time: 95.1 us; the launch traced here: 94.6 us
  blocking collectives  52.5 us (55%)
  starting transfers between devices  26.8 us (28%)
  waiting for transfers between devices  5.54 us (6%)
  matrix products  3.2 us (3%)
  local copies, waits for them, and re-layouts  2.52 us (3%)
  Pallas kernels  1.79 us (2%)
  other arithmetic  1.27 us (1%)
    all_to_all x2, blocking collectives, to_all(): return lax.all_to_all(copies, axes, split_axis=0, concat_axis=0, tiled=True)  28.8 us
    all_to_all x2, blocking collectives, product(): lax.all_to_all(jnp.concatenate([part, tail], axis=1), (Y, X), split_axis=...  23.7 us
    ppermute x9, starting transfers between devices, ahead(): return lax.ppermute(x, axis, [((i + k) % n, i) for i in range(n)])  18.7 us
    all_to_all x1, starting transfers between devices, to_all(): return lax.all_to_all(copies, axes, split_axis=0, concat_axis=0, tiled=True)  8.18 us
    ppermute x9, waiting for transfers between devices, ahead(): return lax.ppermute(x, axis, [((i + k) % n, i) for i in range(n)])  4.74 us
  transfers between devices with their start and end apart: 10, of which 5 were waited for; matrix products, arithmetic and copies ran while one was open for 3% of the time, Pallas kernels for 0%

profile of v6, /device:TPU:1, one launch (start us, length us, event | category | flops | bytes accessed | tf_op | source)
XLA Modules:
  0.0 94.6 jit_solution(17660753967459171153)
XLA Ops:
  0.6 1.8 %prepare.1 = (f32[64,128]{1,0:T(8,128)}, f32[64,128]{1,0:T(8,128)}, f32[128,128]{1,0:T(8,128)}, bf16[128,128]{1,0:T(8,128)(2,1)}, bf16[64,128]{1,0:T(8,128)(2,1)}) custom-call(f32[64,128]{1,0:T(8,128)} %obs_ref.1, s32[1,64]{1,0:T(1,128)} %bitcast.51, f32[32,64]{1,0:T(8,128)} %bitcast.50, f32[1,32]{1,0:T(1,128)} %bitcast.52, f32[1,128]{1,0:T(1,128)} %bitcast.53), custom_call_target="tpu_custom_call" | custom-call | tf_op jit(solution)/shard_map/prepare/pallas_call | solution.py:107
  2.4 2.0 %collective-permute-start.2 = (bf16[64,128]{1,0:T(8,128)(2,1)}, bf16[64,128]{1,0:T(8,128)(2,1)S(1)}, u32[]{:S(2)}, u32[]{:S(2)}) collective-permute-start(bf16[64,128]{1,0:T(8,128)(2,1)} %get-tuple-element.9), channel_id=1, source_target_pairs={{3,0},{0,1},{1,2},{2,3},{7,4},{4,5},{5,6},{6,7},{11,8},{8,9},{9,10... | collective-permute-start | bytes 49160 | tf_op jit(solution)/shard_map/ppermute | solution.py:26
  4.5 2.4 %collective-permute-start.1 = (bf16[64,128]{1,0:T(8,128)(2,1)}, bf16[64,128]{1,0:T(8,128)(2,1)S(1)}, u32[]{:S(2)}, u32[]{:S(2)}) collective-permute-start(bf16[64,128]{1,0:T(8,128)(2,1)} %get-tuple-element.9), channel_id=1, source_target_pairs={{2,0},{3,1},{0,2},{1,3},{6,4},{7,5},{4,6},{5,7},{10,8},{11,9},{8,1... | collective-permute-start | bytes 49160 | tf_op jit(solution)/shard_map/ppermute | solution.py:26
  6.9 1.2 %collective-permute-start = (bf16[64,128]{1,0:T(8,128)(2,1)}, bf16[64,128]{1,0:T(8,128)(2,1)S(1)}, u32[]{:S(2)}, u32[]{:S(2)}) collective-permute-start(bf16[64,128]{1,0:T(8,128)(2,1)} %get-tuple-element.9), channel_id=1, source_target_pairs={{1,0},{2,1},{3,2},{0,3},{5,4},{6,5},{7,6},{4,7},{9,8},{10,9},{11,1... | collective-permute-start | bytes 49160 | tf_op jit(solution)/shard_map/ppermute | solution.py:26
  8.1 1.5 %broadcast_in_dim.59 = bf16[8,128,128]{2,1,0:T(8,128)(2,1)} broadcast(bf16[128,128]{1,0:T(8,128)(2,1)} %get-tuple-element.10), dimensions={1,2} | broadcast | bytes 294912 | tf_op jit(solution)/shard_map/broadcast_in_dim | solution.py:38
  9.6 8.2 %all-to-all-start = ((bf16[8,128,128]{2,1,0:T(8,128)(2,1)}), bf16[8,128,128]{2,1,0:T(8,128)(2,1)S(1)}, u32[]{:S(2)}, u32[]{:S(2)}) async-start(bf16[8,128,128]{2,1,0:T(8,128)(2,1)} %broadcast_in_dim.59), calls=%async_computation | async-start | bytes 524288 | tf_op jit(solution)/shard_map/all_to_all | solution.py:39
  17.8 0.7 constant_dynamic-update-slice_fusion.7
  18.6 1.4 %collective-permute-start.5 = (bf16[256,128]{1,0:T(8,128)(2,1)S(1)}, bf16[256,128]{1,0:T(8,128)(2,1)S(1)}, u32[]{:S(2)}, u32[]{:S(2)}) collective-permute-start(bf16[256,128]{1,0:T(8,128)(2,1)S(1)} %constant_dynamic-update-slice_fusion.4), channel_id=1, source_target_pairs={{192,0},{0,64},{64,128},{128,192},{193,1},{1,65},{65,129},{129,193... | collective-permute-start | bytes 196616 | tf_op jit(solution)/shard_map/ppermute | solution.py:26
  19.9 2.6 %collective-permute-start.4 = (bf16[256,128]{1,0:T(8,128)(2,1)S(1)}, bf16[256,128]{1,0:T(8,128)(2,1)S(1)}, u32[]{:S(2)}, u32[]{:S(2)}) collective-permute-start(bf16[256,128]{1,0:T(8,128)(2,1)S(1)} %constant_dynamic-update-slice_fusion.4), channel_id=1, source_target_pairs={{128,0},{192,64},{0,128},{64,192},{129,1},{193,65},{1,129},{65,193... | collective-permute-start | bytes 196616 | tf_op jit(solution)/shard_map/ppermute | solution.py:26
  22.5 1.1 %collective-permute-start.3 = (bf16[256,128]{1,0:T(8,128)(2,1)S(1)}, bf16[256,128]{1,0:T(8,128)(2,1)S(1)}, u32[]{:S(2)}, u32[]{:S(2)}) collective-permute-start(bf16[256,128]{1,0:T(8,128)(2,1)S(1)} %constant_dynamic-update-slice_fusion.4), channel_id=1, source_target_pairs={{64,0},{128,64},{192,128},{0,192},{65,1},{129,65},{193,129},{1,193... | collective-permute-start | bytes 196616 | tf_op jit(solution)/shard_map/ppermute | solution.py:26
  23.7 2.7 %collective-permute-done.3 = bf16[256,128]{1,0:T(8,128)(2,1)S(1)} collective-permute-done((bf16[256,128]{1,0:T(8,128)(2,1)S(1)}, bf16[256,128]{1,0:T(8,128)(2,1)S(1)}, u32[]{:S(2)}, u32[]{:S(2)}) %collective-permute-start.3) | collective-permute-done | bytes 65568 | tf_op jit(solution)/shard_map/ppermute | solution.py:26
  26.4 0.8 all-to-all-done
  27.2 0.5 exponential_convert_fusion.1
  27.8 3.4 %collective-permute-start.6 = (bf16[8,128,128]{2,1,0:T(8,128)(2,1)S(1)}, bf16[8,128,128]{2,1,0:T(8,128)(2,1)S(1)}, u32[]{:S(2)}, u32[]{:S(2)}) collective-permute-start(bf16[8,128,128]{2,1,0:T(8,128)(2,1)S(1)} %all-to-all-done), channel_id=1, source_target_pairs={{32,0},{0,32},{33,1},{1,33},{34,2},{2,34},{35,3},{3,35},{36,4},{4,... | collective-permute-start | bytes 786440 | tf_op jit(solution)/shard_map/ppermute | solution.py:26
  31.6 0.7 collective-permute-done.6
  33.5 12.6 %all_to_all.25 = f16[16,72,128]{2,1,0:T(8,128)(2,1)S(1)} all-to-all(f16[16,72,128]{2,1,0:T(8,128)(2,1)S(1)} %pad_maximum_fusion), channel_id=1, replica_groups=mesh['y'=4,'c'=2,'z'=8,'x'=4] {'y','x'}, dimensions={0} | all-to-all | bytes 589824 | tf_op jit(solution)/shard_map/all_to_all | solution.py:175
  46.5 12.7 %all_to_all.26 = bf16[8,64,128]{2,1,0:T(8,128)(2,1)S(1)} all-to-all(bf16[8,64,128]{2,1,0:T(8,128)(2,1)S(1)} %broadcast_in_dim.61), channel_id=1, replica_groups=mesh['y'=4,'c'=2,'z'=8,'x'=4] {'z'}, dimensions={0} | all-to-all | bytes 262144 | tf_op jit(solution)/shard_map/all_to_all | solution.py:39
  59.2 3.0 %collective-permute-start.7 = (bf16[512,128]{1,0:T(8,128)(2,1)S(1)}, bf16[512,128]{1,0:T(8,128)(2,1)S(1)}, u32[]{:S(2)}, u32[]{:S(2)}) collective-permute-start(bf16[512,128]{1,0:T(8,128)(2,1)S(1)} %bitcast.41), channel_id=1, source_target_pairs={{32,0},{0,32},{33,1},{1,33},{34,2},{2,34},{35,3},{3,35},{36,4},{4,... | collective-permute-start | bytes 393224 | tf_op jit(solution)/shard_map/ppermute | solution.py:26
  62.6 0.5 collective-permute-done.7
  63.8 11.1 %all_to_all.27 = f16[16,72,128]{2,1,0:T(8,128)(2,1)S(1)} all-to-all(f16[16,72,128]{2,1,0:T(8,128)(2,1)S(1)} %pad_maximum_fusion.1), channel_id=1, replica_groups=mesh['y'=4,'c'=2,'z'=8,'x'=4] {'y','x'}, dimensions={0} | all-to-all | bytes 589824 | tf_op jit(solution)/shard_map/all_to_all | solution.py:175
  75.2 1.6 %collective-permute-start.8 = (f32[1,128]{1,0:T(1,128)S(1)}, f32[1,128]{1,0:T(1,128)S(1)}, u32[]{:S(2)}, u32[]{:S(2)}) collective-permute-start(f32[1,128]{1,0:T(1,128)S(1)} %bitcast.58), channel_id=1, source_target_pairs={{32,0},{0,32},{33,1},{1,33},{34,2},{2,34},{35,3},{3,35},{36,4},{4,... | collective-permute-start | bytes 1544 | tf_op jit(solution)/shard_map/ppermute | solution.py:26
  76.7 0.8 collective-permute-done.8
  77.6 16.1 %all_to_all.28 = f32[128,1,128]{2,1,0:T(1,128)S(1)} all-to-all(f32[128,1,128]{2,1,0:T(1,128)S(1)} %broadcast_in_dim.65), channel_id=1, replica_groups=mesh['y'=4,'c'=2,'z'=8,'x'=4] {'y','z','x'}, dimensions={0} | all-to-all | bytes 131072 | tf_op jit(solution)/shard_map/all_to_all | solution.py:39
  93.9 0.6 multiply_add_fusion
  (57 shorter events, 3.7 us)
Async XLA Ops:
  2.4 16.1 %collective-permute-start.2 = (bf16[64,128]{1,0:T(8,128)(2,1)}, bf16[64,128]{1,0:T(8,128)(2,1)S(1)}, u32[]{:S(2)}, u32[]{:S(2)}) collective-permute-start(bf16[64,128]{1,0:T(8,128)(2,1)} %get-tuple-element.9), channel_id=1, source_target_pairs={{3,0},{0,1},{1,2},{2,3},{7,4},{4,5},{5,6},{6,7},{11,8},{8,9},{9,10... | collective-permute-start | bytes 49160 | tf_op jit(solution)/shard_map/ppermute | solution.py:26
  4.5 14.0 %collective-permute-start.1 = (bf16[64,128]{1,0:T(8,128)(2,1)}, bf16[64,128]{1,0:T(8,128)(2,1)S(1)}, u32[]{:S(2)}, u32[]{:S(2)}) collective-permute-start(bf16[64,128]{1,0:T(8,128)(2,1)} %get-tuple-element.9), channel_id=1, source_target_pairs={{2,0},{3,1},{0,2},{1,3},{6,4},{7,5},{4,6},{5,7},{10,8},{11,9},{8,1... | collective-permute-start | bytes 49160 | tf_op jit(solution)/shard_map/ppermute | solution.py:26
  6.9 11.6 %collective-permute-start = (bf16[64,128]{1,0:T(8,128)(2,1)}, bf16[64,128]{1,0:T(8,128)(2,1)S(1)}, u32[]{:S(2)}, u32[]{:S(2)}) collective-permute-start(bf16[64,128]{1,0:T(8,128)(2,1)} %get-tuple-element.9), channel_id=1, source_target_pairs={{1,0},{2,1},{3,2},{0,3},{5,4},{6,5},{7,6},{4,7},{9,8},{10,9},{11,1... | collective-permute-start | bytes 49160 | tf_op jit(solution)/shard_map/ppermute | solution.py:26
  9.6 17.7 %all-to-all-start = ((bf16[8,128,128]{2,1,0:T(8,128)(2,1)}), bf16[8,128,128]{2,1,0:T(8,128)(2,1)S(1)}, u32[]{:S(2)}, u32[]{:S(2)}) async-start(bf16[8,128,128]{2,1,0:T(8,128)(2,1)} %broadcast_in_dim.59), calls=%async_computation | async-start | bytes 524288 | tf_op jit(solution)/shard_map/all_to_all | solution.py:39
  18.6 7.8 %collective-permute-start.5 = (bf16[256,128]{1,0:T(8,128)(2,1)S(1)}, bf16[256,128]{1,0:T(8,128)(2,1)S(1)}, u32[]{:S(2)}, u32[]{:S(2)}) collective-permute-start(bf16[256,128]{1,0:T(8,128)(2,1)S(1)} %constant_dynamic-update-slice_fusion.4), channel_id=1, source_target_pairs={{192,0},{0,64},{64,128},{128,192},{193,1},{1,65},{65,129},{129,193... | collective-permute-start | bytes 196616 | tf_op jit(solution)/shard_map/ppermute | solution.py:26
  19.9 6.4 %collective-permute-start.4 = (bf16[256,128]{1,0:T(8,128)(2,1)S(1)}, bf16[256,128]{1,0:T(8,128)(2,1)S(1)}, u32[]{:S(2)}, u32[]{:S(2)}) collective-permute-start(bf16[256,128]{1,0:T(8,128)(2,1)S(1)} %constant_dynamic-update-slice_fusion.4), channel_id=1, source_target_pairs={{128,0},{192,64},{0,128},{64,192},{129,1},{193,65},{1,129},{65,193... | collective-permute-start | bytes 196616 | tf_op jit(solution)/shard_map/ppermute | solution.py:26
  22.5 3.8 %collective-permute-start.3 = (bf16[256,128]{1,0:T(8,128)(2,1)S(1)}, bf16[256,128]{1,0:T(8,128)(2,1)S(1)}, u32[]{:S(2)}, u32[]{:S(2)}) collective-permute-start(bf16[256,128]{1,0:T(8,128)(2,1)S(1)} %constant_dynamic-update-slice_fusion.4), channel_id=1, source_target_pairs={{64,0},{128,64},{192,128},{0,192},{65,1},{129,65},{193,129},{1,193... | collective-permute-start | bytes 196616 | tf_op jit(solution)/shard_map/ppermute | solution.py:26
  27.8 4.6 %collective-permute-start.6 = (bf16[8,128,128]{2,1,0:T(8,128)(2,1)S(1)}, bf16[8,128,128]{2,1,0:T(8,128)(2,1)S(1)}, u32[]{:S(2)}, u32[]{:S(2)}) collective-permute-start(bf16[8,128,128]{2,1,0:T(8,128)(2,1)S(1)} %all-to-all-done), channel_id=1, source_target_pairs={{32,0},{0,32},{33,1},{1,33},{34,2},{2,34},{35,3},{3,35},{36,4},{4,... | collective-permute-start | bytes 786440 | tf_op jit(solution)/shard_map/ppermute | solution.py:26
  33.4 12.8 %copy-start = (f32[64,128]{1,0:T(8,128)S(1)}, f32[64,128]{1,0:T(8,128)}, u32[]{:S(2)}) copy-start(f32[64,128]{1,0:T(8,128)} %get-tuple-element.8) | copy-start | bytes 98308
  33.4 12.8 %copy-start.1 = (f32[64,128]{1,0:T(8,128)S(1)}, f32[64,128]{1,0:T(8,128)}, u32[]{:S(2)}) copy-start(f32[64,128]{1,0:T(8,128)} %get-tuple-element.7) | copy-start | bytes 98308
  33.4 12.8 %copy-start.2 = (f32[128,128]{1,0:T(8,128)S(1)}, f32[128,128]{1,0:T(8,128)}, u32[]{:S(2)}) copy-start(f32[128,128]{1,0:T(8,128)} %get-tuple-element.11) | copy-start | bytes 196612
  59.2 3.9 %collective-permute-start.7 = (bf16[512,128]{1,0:T(8,128)(2,1)S(1)}, bf16[512,128]{1,0:T(8,128)(2,1)S(1)}, u32[]{:S(2)}, u32[]{:S(2)}) collective-permute-start(bf16[512,128]{1,0:T(8,128)(2,1)S(1)} %bitcast.41), channel_id=1, source_target_pairs={{32,0},{0,32},{33,1},{1,33},{34,2},{2,34},{35,3},{3,35},{36,4},{4,... | collective-permute-start | bytes 393224 | tf_op jit(solution)/shard_map/ppermute | solution.py:26
  75.2 2.4 %collective-permute-start.8 = (f32[1,128]{1,0:T(1,128)S(1)}, f32[1,128]{1,0:T(1,128)S(1)}, u32[]{:S(2)}, u32[]{:S(2)}) collective-permute-start(f32[1,128]{1,0:T(1,128)S(1)} %bitcast.58), channel_id=1, source_target_pairs={{32,0},{0,32},{33,1},{1,33},{34,2},{2,34},{35,3},{3,35},{36,4},{4,... | collective-permute-start | bytes 1544 | tf_op jit(solution)/shard_map/ppermute | solution.py:26

commit v7 on v6

--- a/solution.py
+++ b/solution.py
@@ -26,10 +26,13 @@
     return lax.ppermute(x, axis, [((i + k) % n, i) for i in range(n)])
 
 
-def around(x, axis, base):
+def shifted(x, axis):
+    return [ahead(x, axis, k) for k in range(1, lax.axis_size(axis))]
+
+
+def in_order(x, others, axis, base):
     n, me = lax.axis_size(axis), lax.axis_index(axis)
-    for k in range(n):
-        block = ahead(x, axis, k) if k else x
+    for k, block in enumerate([x, *others]):
         base = lax.dynamic_update_slice_in_dim(base, block, (me + k) % n * x.shape[0], 0)
     return base
 
@@ -87,7 +90,7 @@
     return (lane < column(lengths.astype(f32))).astype(f32)
 
 
-def prepare(observed, lengths, features, length_scale, epoch_gain):
+def prepare(observed, lengths, features, length_scale, epoch_gain, copies):
     own, width = observed.shape
 
     def body(obs_ref, len_ref, feat_ref, scale_ref, gain_ref, v_ref, mask_ref, ek_ref, out_ref, left_ref):
@@ -101,8 +104,10 @@
         v_ref[...] = v
         ek_ref[...] = ek
         w = jnp.dot(v, ek, precision=HIGHEST, preferred_element_type=f32)
-        out_ref[:own, :] = w.astype(bf16)
-        out_ref[own:, :] = right
+        w = w.astype(bf16)
+        for k in range(copies):
+            out_ref[k, :own, :] = w
+            out_ref[k, own:, :] = right
 
     return pl.pallas_call(
         body,
@@ -110,7 +115,7 @@
             jax.ShapeDtypeStruct((own, width), f32),
             jax.ShapeDtypeStruct((own, width), f32),
             jax.ShapeDtypeStruct((width, width), f32),
-            jax.ShapeDtypeStruct((2 * own, width), bf16),
+            jax.ShapeDtypeStruct((copies, 2 * own, width), bf16),
             jax.ShapeDtypeStruct((own, width), bf16),
         ),
         in_specs=[VMEM] * 5,
@@ -157,11 +162,15 @@
     own, width = observed.shape
     features, length_scale = features.T, length_scale[None, :]
     lengths, epoch_gain = lengths[None, :], epoch_gain[None, :]
-    v0, mask, ek, outgoing, left = prepare(observed, lengths, features, length_scale, epoch_gain)
-    here = to_all(outgoing, Z)
-    line = around(left, X, jnp.zeros((lax.axis_size(X) * own, width), bf16))
-    lefts = around(line, Y, jnp.zeros((lax.axis_size(Y) * line.shape[0], width), bf16))
+    v0, mask, ek, outgoing, left = prepare(
+        observed, lengths, features, length_scale, epoch_gain, lax.axis_size(Z)
+    )
+    others = shifted(left, X)
+    outgoing, others = lax.optimization_barrier((outgoing, others))
+    here = lax.all_to_all(outgoing, Z, split_axis=0, concat_axis=0, tiled=True)
     there = ahead(here, C, 1)
+    line = in_order(left, others, X, jnp.zeros((lax.axis_size(X) * own, width), bf16))
+    lefts = in_order(line, shifted(line, Y), Y, here.reshape(-1, width))
     k_here = block_kernel(lefts, here[:, own:].reshape(-1, width))
     k_there = block_kernel(lefts, there[:, own:].reshape(-1, width))
 

time: 95.1 us -> 96.4 us (1.014)
  waiting for transfers between devices: 5.54 us -> 7.98 us
  local copies, waits for them, and re-layouts: 2.52 us -> 1 us
    all_to_all x1, waiting for transfers between devices: 0.8 us -> 3.6 us  [per_device(): here = lax.all_to_all(outgoing, Z, split_axis=0, concat_axis=0, tiled=True)]
    all_to_all x2, blocking collectives: 28.8 us -> 26.5 us  [to_all(): return lax.all_to_all(copies, axes, split_axis=0, concat_axis=0, tiled=True)]
    all_to_all x2, blocking collectives: 23.7 us -> 25.7 us  [product(): lax.all_to_all(jnp.concatenate([part, tail], axis=1), (Y, X), split_axis=...]
    broadcast_in_dim x3 -> x2, local copies, waits for them, and re-layouts: 1.54 us -> 0.06 us  [to_all(): copies = jnp.broadcast_to(x, (lax.axis_size(axes), *x.shape))]
  transfers between devices with their start and end apart: 10 -> 10, of which waited for: 5 -> 6; matrix products, arithmetic and copies ran while one was open for 3% -> 1% of each run, Pallas kernels for 0% -> 0%
where the time goes in v7:
time: 96.4 us; the launch traced here: 95.9 us
  blocking collectives  52.2 us (54%)
  starting transfers between devices  27.4 us (28%)
  waiting for transfers between devices  7.98 us (8%)
  matrix products  3.22 us (3%)
  Pallas kernels  1.88 us (2%)
  other arithmetic  1.27 us (1%)
  local copies, waits for them, and re-layouts  1 us (1%)
    all_to_all x2, blocking collectives, to_all(): return lax.all_to_all(copies, axes, split_axis=0, concat_axis=0, tiled=True)  26.5 us
    all_to_all x2, blocking collectives, product(): lax.all_to_all(jnp.concatenate([part, tail], axis=1), (Y, X), split_axis=...  25.7 us
    ppermute x9, starting transfers between devices, ahead(): return lax.ppermute(x, axis, [((i + k) % n, i) for i in range(n)])  19.2 us
    all_to_all x1, starting transfers between devices, per_device(): here = lax.all_to_all(outgoing, Z, split_axis=0, concat_axis=0, tiled=True)  8.19 us
    ppermute x9, waiting for transfers between devices, ahead(): return lax.ppermute(x, axis, [((i + k) % n, i) for i in range(n)])  4.38 us
    all_to_all x1, waiting for transfers between devices, per_device(): here = lax.all_to_all(outgoing, Z, split_axis=0, concat_axis=0, tiled=True)  3.6 us
  transfers between devices with their start and end apart: 10, of which 6 were waited for; matrix products, arithmetic and copies ran while one was open for 1% of the time, Pallas kernels for 0%

profile of v7, /device:TPU:1, one launch (start us, length us, event | category | flops | bytes accessed | tf_op | source)
XLA Modules:
  0.0 95.9 jit_solution(296434384630096033)
XLA Ops:
  0.6 1.9 %prepare.1 = (f32[64,128]{1,0:T(8,128)}, f32[64,128]{1,0:T(8,128)}, f32[128,128]{1,0:T(8,128)}, bf16[8,128,128]{2,1,0:T(8,128)(2,1)}, bf16[64,128]{1,0:T(8,128)(2,1)}) custom-call(f32[64,128]{1,0:T(8,128)} %obs_ref.1, s32[1,64]{1,0:T(1,128)} %bitcast.53, f32[32,64]{1,0:T(8,128)} %bitcast.52, f32[1,32]{1,0:T(1,128)} %bitcast.54, f32[1,128]{1,0:T(1,128)} %bitcast.55), custom_call_target="tpu_custom_call" | custom-call | tf_op jit(solution)/shard_map/prepare/pallas_call | solution.py:112
  2.5 2.0 %collective-permute-start.2 = (bf16[64,128]{1,0:T(8,128)(2,1)}, bf16[64,128]{1,0:T(8,128)(2,1)S(1)}, u32[]{:S(2)}, u32[]{:S(2)}) collective-permute-start(bf16[64,128]{1,0:T(8,128)(2,1)} %get-tuple-element.14), channel_id=1, source_target_pairs={{3,0},{0,1},{1,2},{2,3},{7,4},{4,5},{5,6},{6,7},{11,8},{8,9},{9,10... | collective-permute-start | bytes 49160 | tf_op jit(solution)/shard_map/ppermute | solution.py:26
  4.5 2.4 %collective-permute-start.1 = (bf16[64,128]{1,0:T(8,128)(2,1)}, bf16[64,128]{1,0:T(8,128)(2,1)S(1)}, u32[]{:S(2)}, u32[]{:S(2)}) collective-permute-start(bf16[64,128]{1,0:T(8,128)(2,1)} %get-tuple-element.14), channel_id=1, source_target_pairs={{2,0},{3,1},{0,2},{1,3},{6,4},{7,5},{4,6},{5,7},{10,8},{11,9},{8,1... | collective-permute-start | bytes 49160 | tf_op jit(solution)/shard_map/ppermute | solution.py:26
  7.0 1.2 %collective-permute-start = (bf16[64,128]{1,0:T(8,128)(2,1)}, bf16[64,128]{1,0:T(8,128)(2,1)S(1)}, u32[]{:S(2)}, u32[]{:S(2)}) collective-permute-start(bf16[64,128]{1,0:T(8,128)(2,1)} %get-tuple-element.14), channel_id=1, source_target_pairs={{1,0},{2,1},{3,2},{0,3},{5,4},{6,5},{7,6},{4,7},{9,8},{10,9},{11,1... | collective-permute-start | bytes 49160 | tf_op jit(solution)/shard_map/ppermute | solution.py:26
  8.2 0.7 collective-permute-done.1
  8.9 1.2 %collective-permute-done = bf16[64,128]{1,0:T(8,128)(2,1)S(1)} collective-permute-done((bf16[64,128]{1,0:T(8,128)(2,1)}, bf16[64,128]{1,0:T(8,128)(2,1)S(1)}, u32[]{:S(2)}, u32[]{:S(2)}) %collective-permute-start) | collective-permute-done | bytes 16416 | tf_op jit(solution)/shard_map/ppermute | solution.py:26
  10.1 8.2 %all-to-all-start = ((bf16[8,128,128]{2,1,0:T(8,128)(2,1)}), bf16[8,128,128]{2,1,0:T(8,128)(2,1)S(1)}, u32[]{:S(2)}, u32[]{:S(2)}) async-start(bf16[8,128,128]{2,1,0:T(8,128)(2,1)} %get-tuple-element.15), calls=%async_computation | async-start | bytes 524288 | tf_op jit(solution)/shard_map/all_to_all | solution.py:170
  18.3 0.7 constant_dynamic-update-slice_fusion.7
  19.1 1.4 %collective-permute-start.5 = (bf16[256,128]{1,0:T(8,128)(2,1)S(1)}, bf16[256,128]{1,0:T(8,128)(2,1)S(1)}, u32[]{:S(2)}, u32[]{:S(2)}) collective-permute-start(bf16[256,128]{1,0:T(8,128)(2,1)S(1)} %constant_dynamic-update-slice_fusion.4), channel_id=1, source_target_pairs={{192,0},{0,64},{64,128},{128,192},{193,1},{1,65},{65,129},{129,193... | collective-permute-start | bytes 196616 | tf_op jit(solution)/shard_map/ppermute | solution.py:26
  20.4 2.6 %collective-permute-start.4 = (bf16[256,128]{1,0:T(8,128)(2,1)S(1)}, bf16[256,128]{1,0:T(8,128)(2,1)S(1)}, u32[]{:S(2)}, u32[]{:S(2)}) collective-permute-start(bf16[256,128]{1,0:T(8,128)(2,1)S(1)} %constant_dynamic-update-slice_fusion.4), channel_id=1, source_target_pairs={{128,0},{192,64},{0,128},{64,192},{129,1},{193,65},{1,129},{65,193... | collective-permute-start | bytes 196616 | tf_op jit(solution)/shard_map/ppermute | solution.py:26
  23.0 1.1 %collective-permute-start.3 = (bf16[256,128]{1,0:T(8,128)(2,1)S(1)}, bf16[256,128]{1,0:T(8,128)(2,1)S(1)}, u32[]{:S(2)}, u32[]{:S(2)}) collective-permute-start(bf16[256,128]{1,0:T(8,128)(2,1)S(1)} %constant_dynamic-update-slice_fusion.4), channel_id=1, source_target_pairs={{64,0},{128,64},{192,128},{0,192},{65,1},{129,65},{193,129},{1,193... | collective-permute-start | bytes 196616 | tf_op jit(solution)/shard_map/ppermute | solution.py:26
  24.1 3.6 %all-to-all-done = bf16[8,128,128]{2,1,0:T(8,128)(2,1)S(1)} async-done(((bf16[8,128,128]{2,1,0:T(8,128)(2,1)}), bf16[8,128,128]{2,1,0:T(8,128)(2,1)S(1)}, u32[]{:S(2)}, u32[]{:S(2)}) %all-to-all-start) | async-done | bytes 262176 | tf_op jit(solution)/shard_map/all_to_all | solution.py:170
  27.7 3.4 %collective-permute-start.6 = (bf16[8,128,128]{2,1,0:T(8,128)(2,1)S(1)}, bf16[8,128,128]{2,1,0:T(8,128)(2,1)S(1)}, u32[]{:S(2)}, u32[]{:S(2)}) collective-permute-start(bf16[8,128,128]{2,1,0:T(8,128)(2,1)S(1)} %all-to-all-done), channel_id=1, source_target_pairs={{32,0},{0,32},{33,1},{1,33},{34,2},{2,34},{35,3},{3,35},{36,4},{4,... | collective-permute-start | bytes 786440 | tf_op jit(solution)/shard_map/ppermute | solution.py:26
  31.2 1.1 %collective-permute-done.6 = bf16[8,128,128]{2,1,0:T(8,128)(2,1)S(1)} collective-permute-done((bf16[8,128,128]{2,1,0:T(8,128)(2,1)S(1)}, bf16[8,128,128]{2,1,0:T(8,128)(2,1)S(1)}, u32[]{:S(2)}, u32[]{:S(2)}) %collective-permute-start.6) | collective-permute-done | bytes 262176 | tf_op jit(solution)/shard_map/ppermute | solution.py:26
  33.0 0.5 exponential_convert_fusion.1
  34.5 14.6 %all_to_all.25 = f16[16,72,128]{2,1,0:T(8,128)(2,1)S(1)} all-to-all(f16[16,72,128]{2,1,0:T(8,128)(2,1)S(1)} %pad_maximum_fusion), channel_id=1, replica_groups=mesh['y'=4,'c'=2,'z'=8,'x'=4] {'y','x'}, dimensions={0} | all-to-all | bytes 589824 | tf_op jit(solution)/shard_map/all_to_all | solution.py:184
  49.5 10.4 %all_to_all.26 = bf16[8,64,128]{2,1,0:T(8,128)(2,1)S(1)} all-to-all(bf16[8,64,128]{2,1,0:T(8,128)(2,1)S(1)} %broadcast_in_dim.53), channel_id=1, replica_groups=mesh['y'=4,'c'=2,'z'=8,'x'=4] {'z'}, dimensions={0} | all-to-all | bytes 262144 | tf_op jit(solution)/shard_map/all_to_all | solution.py:42
  59.9 3.6 %collective-permute-start.7 = (bf16[512,128]{1,0:T(8,128)(2,1)S(1)}, bf16[512,128]{1,0:T(8,128)(2,1)S(1)}, u32[]{:S(2)}, u32[]{:S(2)}) collective-permute-start(bf16[512,128]{1,0:T(8,128)(2,1)S(1)} %bitcast.43), channel_id=1, source_target_pairs={{32,0},{0,32},{33,1},{1,33},{34,2},{2,34},{35,3},{3,35},{36,4},{4,... | collective-permute-start | bytes 393224 | tf_op jit(solution)/shard_map/ppermute | solution.py:26
  64.0 0.5 collective-permute-done.7
  65.1 11.1 %all_to_all.27 = f16[16,72,128]{2,1,0:T(8,128)(2,1)S(1)} all-to-all(f16[16,72,128]{2,1,0:T(8,128)(2,1)S(1)} %pad_maximum_fusion.1), channel_id=1, replica_groups=mesh['y'=4,'c'=2,'z'=8,'x'=4] {'y','x'}, dimensions={0} | all-to-all | bytes 589824 | tf_op jit(solution)/shard_map/all_to_all | solution.py:184
  76.5 1.6 %collective-permute-start.8 = (f32[1,128]{1,0:T(1,128)S(1)}, f32[1,128]{1,0:T(1,128)S(1)}, u32[]{:S(2)}, u32[]{:S(2)}) collective-permute-start(f32[1,128]{1,0:T(1,128)S(1)} %bitcast.60), channel_id=1, source_target_pairs={{32,0},{0,32},{33,1},{1,33},{34,2},{2,34},{35,3},{3,35},{36,4},{4,... | collective-permute-start | bytes 1544 | tf_op jit(solution)/shard_map/ppermute | solution.py:26
  78.1 0.8 collective-permute-done.8
  78.9 16.1 %all_to_all.28 = f32[128,1,128]{2,1,0:T(1,128)S(1)} all-to-all(f32[128,1,128]{2,1,0:T(1,128)S(1)} %broadcast_in_dim.57), channel_id=1, replica_groups=mesh['y'=4,'c'=2,'z'=8,'x'=4] {'y','z','x'}, dimensions={0} | all-to-all | bytes 131072 | tf_op jit(solution)/shard_map/all_to_all | solution.py:42
  95.3 0.6 multiply_add_fusion
  (55 shorter events, 3.6 us)
Async XLA Ops:
  2.5 5.6 %collective-permute-start.2 = (bf16[64,128]{1,0:T(8,128)(2,1)}, bf16[64,128]{1,0:T(8,128)(2,1)S(1)}, u32[]{:S(2)}, u32[]{:S(2)}) collective-permute-start(bf16[64,128]{1,0:T(8,128)(2,1)} %get-tuple-element.14), channel_id=1, source_target_pairs={{3,0},{0,1},{1,2},{2,3},{7,4},{4,5},{5,6},{6,7},{11,8},{8,9},{9,10... | collective-permute-start | bytes 49160 | tf_op jit(solution)/shard_map/ppermute | solution.py:26
  4.5 4.3 %collective-permute-start.1 = (bf16[64,128]{1,0:T(8,128)(2,1)}, bf16[64,128]{1,0:T(8,128)(2,1)S(1)}, u32[]{:S(2)}, u32[]{:S(2)}) collective-permute-start(bf16[64,128]{1,0:T(8,128)(2,1)} %get-tuple-element.14), channel_id=1, source_target_pairs={{2,0},{3,1},{0,2},{1,3},{6,4},{7,5},{4,6},{5,7},{10,8},{11,9},{8,1... | collective-permute-start | bytes 49160 | tf_op jit(solution)/shard_map/ppermute | solution.py:26
  7.0 3.1 %collective-permute-start = (bf16[64,128]{1,0:T(8,128)(2,1)}, bf16[64,128]{1,0:T(8,128)(2,1)S(1)}, u32[]{:S(2)}, u32[]{:S(2)}) collective-permute-start(bf16[64,128]{1,0:T(8,128)(2,1)} %get-tuple-element.14), channel_id=1, source_target_pairs={{1,0},{2,1},{3,2},{0,3},{5,4},{6,5},{7,6},{4,7},{9,8},{10,9},{11,1... | collective-permute-start | bytes 49160 | tf_op jit(solution)/shard_map/ppermute | solution.py:26
  10.1 17.6 %all-to-all-start = ((bf16[8,128,128]{2,1,0:T(8,128)(2,1)}), bf16[8,128,128]{2,1,0:T(8,128)(2,1)S(1)}, u32[]{:S(2)}, u32[]{:S(2)}) async-start(bf16[8,128,128]{2,1,0:T(8,128)(2,1)} %get-tuple-element.15), calls=%async_computation | async-start | bytes 524288 | tf_op jit(solution)/shard_map/all_to_all | solution.py:170
  19.1 13.4 %collective-permute-start.5 = (bf16[256,128]{1,0:T(8,128)(2,1)S(1)}, bf16[256,128]{1,0:T(8,128)(2,1)S(1)}, u32[]{:S(2)}, u32[]{:S(2)}) collective-permute-start(bf16[256,128]{1,0:T(8,128)(2,1)S(1)} %constant_dynamic-update-slice_fusion.4), channel_id=1, source_target_pairs={{192,0},{0,64},{64,128},{128,192},{193,1},{1,65},{65,129},{129,193... | collective-permute-start | bytes 196616 | tf_op jit(solution)/shard_map/ppermute | solution.py:26
  20.4 12.0 %collective-permute-start.4 = (bf16[256,128]{1,0:T(8,128)(2,1)S(1)}, bf16[256,128]{1,0:T(8,128)(2,1)S(1)}, u32[]{:S(2)}, u32[]{:S(2)}) collective-permute-start(bf16[256,128]{1,0:T(8,128)(2,1)S(1)} %constant_dynamic-update-slice_fusion.4), channel_id=1, source_target_pairs={{128,0},{192,64},{0,128},{64,192},{129,1},{193,65},{1,129},{65,193... | collective-permute-start | bytes 196616 | tf_op jit(solution)/shard_map/ppermute | solution.py:26
  23.0 9.4 %collective-permute-start.3 = (bf16[256,128]{1,0:T(8,128)(2,1)S(1)}, bf16[256,128]{1,0:T(8,128)(2,1)S(1)}, u32[]{:S(2)}, u32[]{:S(2)}) collective-permute-start(bf16[256,128]{1,0:T(8,128)(2,1)S(1)} %constant_dynamic-update-slice_fusion.4), channel_id=1, source_target_pairs={{64,0},{128,64},{192,128},{0,192},{65,1},{129,65},{193,129},{1,193... | collective-permute-start | bytes 196616 | tf_op jit(solution)/shard_map/ppermute | solution.py:26
  27.7 4.6 %collective-permute-start.6 = (bf16[8,128,128]{2,1,0:T(8,128)(2,1)S(1)}, bf16[8,128,128]{2,1,0:T(8,128)(2,1)S(1)}, u32[]{:S(2)}, u32[]{:S(2)}) collective-permute-start(bf16[8,128,128]{2,1,0:T(8,128)(2,1)S(1)} %all-to-all-done), channel_id=1, source_target_pairs={{32,0},{0,32},{33,1},{1,33},{34,2},{2,34},{35,3},{3,35},{36,4},{4,... | collective-permute-start | bytes 786440 | tf_op jit(solution)/shard_map/ppermute | solution.py:26
  34.4 14.9 %copy-start = (f32[64,128]{1,0:T(8,128)S(1)}, f32[64,128]{1,0:T(8,128)}, u32[]{:S(2)}) copy-start(f32[64,128]{1,0:T(8,128)} %get-tuple-element.12) | copy-start | bytes 98308
  34.4 14.9 %copy-start.1 = (f32[64,128]{1,0:T(8,128)S(1)}, f32[64,128]{1,0:T(8,128)}, u32[]{:S(2)}) copy-start(f32[64,128]{1,0:T(8,128)} %get-tuple-element.11) | copy-start | bytes 98308
  34.4 14.9 %copy-start.2 = (f32[128,128]{1,0:T(8,128)S(1)}, f32[128,128]{1,0:T(8,128)}, u32[]{:S(2)}) copy-start(f32[128,128]{1,0:T(8,128)} %get-tuple-element.19) | copy-start | bytes 196612
  59.9 4.5 %collective-permute-start.7 = (bf16[512,128]{1,0:T(8,128)(2,1)S(1)}, bf16[512,128]{1,0:T(8,128)(2,1)S(1)}, u32[]{:S(2)}, u32[]{:S(2)}) collective-permute-start(bf16[512,128]{1,0:T(8,128)(2,1)S(1)} %bitcast.43), channel_id=1, source_target_pairs={{32,0},{0,32},{33,1},{1,33},{34,2},{2,34},{35,3},{3,35},{36,4},{4,... | collective-permute-start | bytes 393224 | tf_op jit(solution)/shard_map/ppermute | solution.py:26
  76.5 2.4 %collective-permute-start.8 = (f32[1,128]{1,0:T(1,128)S(1)}, f32[1,128]{1,0:T(1,128)S(1)}, u32[]{:S(2)}, u32[]{:S(2)}) collective-permute-start(f32[1,128]{1,0:T(1,128)S(1)} %bitcast.60), channel_id=1, source_target_pairs={{32,0},{0,32},{33,1},{1,33},{34,2},{2,34},{35,3},{3,35},{36,4},{4,... | collective-permute-start | bytes 1544 | tf_op jit(solution)/shard_map/ppermute | solution.py:26

commit v8 on v7

--- a/solution.py
+++ b/solution.py
@@ -26,13 +26,10 @@
     return lax.ppermute(x, axis, [((i + k) % n, i) for i in range(n)])
 
 
-def shifted(x, axis):
-    return [ahead(x, axis, k) for k in range(1, lax.axis_size(axis))]
-
-
-def in_order(x, others, axis, base):
+def around(x, axis, base):
     n, me = lax.axis_size(axis), lax.axis_index(axis)
-    for k, block in enumerate([x, *others]):
+    for k in range(n):
+        block = ahead(x, axis, k) if k else x
         base = lax.dynamic_update_slice_in_dim(base, block, (me + k) % n * x.shape[0], 0)
     return base
 
@@ -165,12 +162,10 @@
     v0, mask, ek, outgoing, left = prepare(
         observed, lengths, features, length_scale, epoch_gain, lax.axis_size(Z)
     )
-    others = shifted(left, X)
-    outgoing, others = lax.optimization_barrier((outgoing, others))
     here = lax.all_to_all(outgoing, Z, split_axis=0, concat_axis=0, tiled=True)
+    line = around(left, X, jnp.zeros((lax.axis_size(X) * own, width), bf16))
+    lefts = around(line, Y, jnp.zeros((lax.axis_size(Y) * line.shape[0], width), bf16))
     there = ahead(here, C, 1)
-    line = in_order(left, others, X, jnp.zeros((lax.axis_size(X) * own, width), bf16))
-    lefts = in_order(line, shifted(line, Y), Y, here.reshape(-1, width))
     k_here = block_kernel(lefts, here[:, own:].reshape(-1, width))
     k_there = block_kernel(lefts, there[:, own:].reshape(-1, width))
 

time: 96.4 us -> 93.7 us (0.972)
  waiting for transfers between devices: 7.98 us -> 5.54 us
    all_to_all x1, waiting for transfers between devices: 3.6 us -> 0.8 us  [per_device(): here = lax.all_to_all(outgoing, Z, split_axis=0, concat_axis=0, tiled=True)]
    all_to_all x2, blocking collectives: 26.5 us -> 28.8 us  [to_all(): return lax.all_to_all(copies, axes, split_axis=0, concat_axis=0, tiled=True)]
    all_to_all x2, blocking collectives: 25.7 us -> 23.7 us  [product(): lax.all_to_all(jnp.concatenate([part, tail], axis=1), (Y, X), split_axis=...]
  transfers between devices with their start and end apart: 10 -> 10, of which waited for: 6 -> 5; matrix products, arithmetic and copies ran while one was open for 1% -> 2% of each run, Pallas kernels for 0% -> 0%
where the time goes in v8:
time: 93.7 us; the launch traced here: 93.2 us
  blocking collectives  52.5 us (56%)
  starting transfers between devices  26.8 us (29%)
  waiting for transfers between devices  5.54 us (6%)
  matrix products  3.21 us (3%)
  Pallas kernels  1.88 us (2%)
  other arithmetic  1.27 us (1%)
  local copies, waits for them, and re-layouts  1.04 us (1%)
    all_to_all x2, blocking collectives, to_all(): return lax.all_to_all(copies, axes, split_axis=0, concat_axis=0, tiled=True)  28.8 us
    all_to_all x2, blocking collectives, product(): lax.all_to_all(jnp.concatenate([part, tail], axis=1), (Y, X), split_axis=...  23.7 us
    ppermute x9, starting transfers between devices, ahead(): return lax.ppermute(x, axis, [((i + k) % n, i) for i in range(n)])  18.6 us
    all_to_all x1, starting transfers between devices, per_device(): here = lax.all_to_all(outgoing, Z, split_axis=0, concat_axis=0, tiled=True)  8.18 us
    ppermute x9, waiting for transfers between devices, ahead(): return lax.ppermute(x, axis, [((i + k) % n, i) for i in range(n)])  4.73 us
    pallas_call x1, Pallas kernels, prepare(): pl.pallas_call(body, out_shape=(jax.ShapeDtypeStruct((own, width), f32),...  1.88 us
  transfers between devices with their start and end apart: 10, of which 5 were waited for; matrix products, arithmetic and copies ran while one was open for 2% of the time, Pallas kernels for 0%

profile of v8, /device:TPU:1, one launch (start us, length us, event | category | flops | bytes accessed | tf_op | source)
XLA Modules:
  0.0 93.2 jit_solution(18383884455069290505)
XLA Ops:
  0.6 1.9 %prepare.1 = (f32[64,128]{1,0:T(8,128)}, f32[64,128]{1,0:T(8,128)}, f32[128,128]{1,0:T(8,128)}, bf16[8,128,128]{2,1,0:T(8,128)(2,1)}, bf16[64,128]{1,0:T(8,128)(2,1)}) custom-call(f32[64,128]{1,0:T(8,128)} %obs_ref.1, s32[1,64]{1,0:T(1,128)} %bitcast.51, f32[32,64]{1,0:T(8,128)} %bitcast.50, f32[1,32]{1,0:T(1,128)} %bitcast.52, f32[1,128]{1,0:T(1,128)} %bitcast.53), custom_call_target="tpu_custom_call" | custom-call | tf_op jit(solution)/shard_map/prepare/pallas_call | solution.py:109
  2.5 2.0 %collective-permute-start.2 = (bf16[64,128]{1,0:T(8,128)(2,1)}, bf16[64,128]{1,0:T(8,128)(2,1)S(1)}, u32[]{:S(2)}, u32[]{:S(2)}) collective-permute-start(bf16[64,128]{1,0:T(8,128)(2,1)} %get-tuple-element.9), channel_id=1, source_target_pairs={{3,0},{0,1},{1,2},{2,3},{7,4},{4,5},{5,6},{6,7},{11,8},{8,9},{9,10... | collective-permute-start | bytes 49160 | tf_op jit(solution)/shard_map/ppermute | solution.py:26
  4.5 2.4 %collective-permute-start.1 = (bf16[64,128]{1,0:T(8,128)(2,1)}, bf16[64,128]{1,0:T(8,128)(2,1)S(1)}, u32[]{:S(2)}, u32[]{:S(2)}) collective-permute-start(bf16[64,128]{1,0:T(8,128)(2,1)} %get-tuple-element.9), channel_id=1, source_target_pairs={{2,0},{3,1},{0,2},{1,3},{6,4},{7,5},{4,6},{5,7},{10,8},{11,9},{8,1... | collective-permute-start | bytes 49160 | tf_op jit(solution)/shard_map/ppermute | solution.py:26
  7.0 1.2 %collective-permute-start = (bf16[64,128]{1,0:T(8,128)(2,1)}, bf16[64,128]{1,0:T(8,128)(2,1)S(1)}, u32[]{:S(2)}, u32[]{:S(2)}) collective-permute-start(bf16[64,128]{1,0:T(8,128)(2,1)} %get-tuple-element.9), channel_id=1, source_target_pairs={{1,0},{2,1},{3,2},{0,3},{5,4},{6,5},{7,6},{4,7},{9,8},{10,9},{11,1... | collective-permute-start | bytes 49160 | tf_op jit(solution)/shard_map/ppermute | solution.py:26
  8.2 8.2 %all-to-all-start = ((bf16[8,128,128]{2,1,0:T(8,128)(2,1)}), bf16[8,128,128]{2,1,0:T(8,128)(2,1)S(1)}, u32[]{:S(2)}, u32[]{:S(2)}) async-start(bf16[8,128,128]{2,1,0:T(8,128)(2,1)} %get-tuple-element.10), calls=%async_computation | async-start | bytes 524288 | tf_op jit(solution)/shard_map/all_to_all | solution.py:165
  16.4 0.7 constant_dynamic-update-slice_fusion.7
  17.1 1.4 %collective-permute-start.5 = (bf16[256,128]{1,0:T(8,128)(2,1)S(1)}, bf16[256,128]{1,0:T(8,128)(2,1)S(1)}, u32[]{:S(2)}, u32[]{:S(2)}) collective-permute-start(bf16[256,128]{1,0:T(8,128)(2,1)S(1)} %constant_dynamic-update-slice_fusion.4), channel_id=1, source_target_pairs={{192,0},{0,64},{64,128},{128,192},{193,1},{1,65},{65,129},{129,193... | collective-permute-start | bytes 196616 | tf_op jit(solution)/shard_map/ppermute | solution.py:26
  18.5 2.6 %collective-permute-start.4 = (bf16[256,128]{1,0:T(8,128)(2,1)S(1)}, bf16[256,128]{1,0:T(8,128)(2,1)S(1)}, u32[]{:S(2)}, u32[]{:S(2)}) collective-permute-start(bf16[256,128]{1,0:T(8,128)(2,1)S(1)} %constant_dynamic-update-slice_fusion.4), channel_id=1, source_target_pairs={{128,0},{192,64},{0,128},{64,192},{129,1},{193,65},{1,129},{65,193... | collective-permute-start | bytes 196616 | tf_op jit(solution)/shard_map/ppermute | solution.py:26
  21.1 1.1 %collective-permute-start.3 = (bf16[256,128]{1,0:T(8,128)(2,1)S(1)}, bf16[256,128]{1,0:T(8,128)(2,1)S(1)}, u32[]{:S(2)}, u32[]{:S(2)}) collective-permute-start(bf16[256,128]{1,0:T(8,128)(2,1)S(1)} %constant_dynamic-update-slice_fusion.4), channel_id=1, source_target_pairs={{64,0},{128,64},{192,128},{0,192},{65,1},{129,65},{193,129},{1,193... | collective-permute-start | bytes 196616 | tf_op jit(solution)/shard_map/ppermute | solution.py:26
  22.3 2.7 %collective-permute-done.3 = bf16[256,128]{1,0:T(8,128)(2,1)S(1)} collective-permute-done((bf16[256,128]{1,0:T(8,128)(2,1)S(1)}, bf16[256,128]{1,0:T(8,128)(2,1)S(1)}, u32[]{:S(2)}, u32[]{:S(2)}) %collective-permute-start.3) | collective-permute-done | bytes 65568 | tf_op jit(solution)/shard_map/ppermute | solution.py:26
  25.0 0.8 all-to-all-done
  25.8 0.5 exponential_convert_fusion.1
  26.4 3.4 %collective-permute-start.6 = (bf16[8,128,128]{2,1,0:T(8,128)(2,1)S(1)}, bf16[8,128,128]{2,1,0:T(8,128)(2,1)S(1)}, u32[]{:S(2)}, u32[]{:S(2)}) collective-permute-start(bf16[8,128,128]{2,1,0:T(8,128)(2,1)S(1)} %all-to-all-done), channel_id=1, source_target_pairs={{32,0},{0,32},{33,1},{1,33},{34,2},{2,34},{35,3},{3,35},{36,4},{4,... | collective-permute-start | bytes 786440 | tf_op jit(solution)/shard_map/ppermute | solution.py:26
  30.2 0.7 collective-permute-done.6
  31.1 0.5 exponential_convert_fusion
  32.1 12.6 %all_to_all.25 = f16[16,72,128]{2,1,0:T(8,128)(2,1)S(1)} all-to-all(f16[16,72,128]{2,1,0:T(8,128)(2,1)S(1)} %pad_maximum_fusion), channel_id=1, replica_groups=mesh['y'=4,'c'=2,'z'=8,'x'=4] {'y','x'}, dimensions={0} | all-to-all | bytes 589824 | tf_op jit(solution)/shard_map/all_to_all | solution.py:179
  45.1 12.7 %all_to_all.26 = bf16[8,64,128]{2,1,0:T(8,128)(2,1)S(1)} all-to-all(bf16[8,64,128]{2,1,0:T(8,128)(2,1)S(1)} %broadcast_in_dim.57), channel_id=1, replica_groups=mesh['y'=4,'c'=2,'z'=8,'x'=4] {'z'}, dimensions={0} | all-to-all | bytes 262144 | tf_op jit(solution)/shard_map/all_to_all | solution.py:39
  57.8 2.9 %collective-permute-start.7 = (bf16[512,128]{1,0:T(8,128)(2,1)S(1)}, bf16[512,128]{1,0:T(8,128)(2,1)S(1)}, u32[]{:S(2)}, u32[]{:S(2)}) collective-permute-start(bf16[512,128]{1,0:T(8,128)(2,1)S(1)} %bitcast.41), channel_id=1, source_target_pairs={{32,0},{0,32},{33,1},{1,33},{34,2},{2,34},{35,3},{3,35},{36,4},{4,... | collective-permute-start | bytes 393224 | tf_op jit(solution)/shard_map/ppermute | solution.py:26
  61.2 0.5 collective-permute-done.7
  62.4 11.1 %all_to_all.27 = f16[16,72,128]{2,1,0:T(8,128)(2,1)S(1)} all-to-all(f16[16,72,128]{2,1,0:T(8,128)(2,1)S(1)} %pad_maximum_fusion.1), channel_id=1, replica_groups=mesh['y'=4,'c'=2,'z'=8,'x'=4] {'y','x'}, dimensions={0} | all-to-all | bytes 589824 | tf_op jit(solution)/shard_map/all_to_all | solution.py:179
  73.8 1.6 %collective-permute-start.8 = (f32[1,128]{1,0:T(1,128)S(1)}, f32[1,128]{1,0:T(1,128)S(1)}, u32[]{:S(2)}, u32[]{:S(2)}) collective-permute-start(f32[1,128]{1,0:T(1,128)S(1)} %bitcast.58), channel_id=1, source_target_pairs={{32,0},{0,32},{33,1},{1,33},{34,2},{2,34},{35,3},{3,35},{36,4},{4,... | collective-permute-start | bytes 1544 | tf_op jit(solution)/shard_map/ppermute | solution.py:26
  75.3 0.8 collective-permute-done.8
  76.2 16.1 %all_to_all.28 = f32[128,1,128]{2,1,0:T(1,128)S(1)} all-to-all(f32[128,1,128]{2,1,0:T(1,128)S(1)} %broadcast_in_dim.61), channel_id=1, replica_groups=mesh['y'=4,'c'=2,'z'=8,'x'=4] {'y','z','x'}, dimensions={0} | all-to-all | bytes 131072 | tf_op jit(solution)/shard_map/all_to_all | solution.py:39
  92.5 0.6 multiply_add_fusion
  (56 shorter events, 3.2 us)
Async XLA Ops:
  2.5 14.6 %collective-permute-start.2 = (bf16[64,128]{1,0:T(8,128)(2,1)}, bf16[64,128]{1,0:T(8,128)(2,1)S(1)}, u32[]{:S(2)}, u32[]{:S(2)}) collective-permute-start(bf16[64,128]{1,0:T(8,128)(2,1)} %get-tuple-element.9), channel_id=1, source_target_pairs={{3,0},{0,1},{1,2},{2,3},{7,4},{4,5},{5,6},{6,7},{11,8},{8,9},{9,10... | collective-permute-start | bytes 49160 | tf_op jit(solution)/shard_map/ppermute | solution.py:26
  4.5 12.6 %collective-permute-start.1 = (bf16[64,128]{1,0:T(8,128)(2,1)}, bf16[64,128]{1,0:T(8,128)(2,1)S(1)}, u32[]{:S(2)}, u32[]{:S(2)}) collective-permute-start(bf16[64,128]{1,0:T(8,128)(2,1)} %get-tuple-element.9), channel_id=1, source_target_pairs={{2,0},{3,1},{0,2},{1,3},{6,4},{7,5},{4,6},{5,7},{10,8},{11,9},{8,1... | collective-permute-start | bytes 49160 | tf_op jit(solution)/shard_map/ppermute | solution.py:26
  7.0 10.1 %collective-permute-start = (bf16[64,128]{1,0:T(8,128)(2,1)}, bf16[64,128]{1,0:T(8,128)(2,1)S(1)}, u32[]{:S(2)}, u32[]{:S(2)}) collective-permute-start(bf16[64,128]{1,0:T(8,128)(2,1)} %get-tuple-element.9), channel_id=1, source_target_pairs={{1,0},{2,1},{3,2},{0,3},{5,4},{6,5},{7,6},{4,7},{9,8},{10,9},{11,1... | collective-permute-start | bytes 49160 | tf_op jit(solution)/shard_map/ppermute | solution.py:26
  8.2 17.7 %all-to-all-start = ((bf16[8,128,128]{2,1,0:T(8,128)(2,1)}), bf16[8,128,128]{2,1,0:T(8,128)(2,1)S(1)}, u32[]{:S(2)}, u32[]{:S(2)}) async-start(bf16[8,128,128]{2,1,0:T(8,128)(2,1)} %get-tuple-element.10), calls=%async_computation | async-start | bytes 524288 | tf_op jit(solution)/shard_map/all_to_all | solution.py:165
  17.1 7.8 %collective-permute-start.5 = (bf16[256,128]{1,0:T(8,128)(2,1)S(1)}, bf16[256,128]{1,0:T(8,128)(2,1)S(1)}, u32[]{:S(2)}, u32[]{:S(2)}) collective-permute-start(bf16[256,128]{1,0:T(8,128)(2,1)S(1)} %constant_dynamic-update-slice_fusion.4), channel_id=1, source_target_pairs={{192,0},{0,64},{64,128},{128,192},{193,1},{1,65},{65,129},{129,193... | collective-permute-start | bytes 196616 | tf_op jit(solution)/shard_map/ppermute | solution.py:26
  18.5 6.4 %collective-permute-start.4 = (bf16[256,128]{1,0:T(8,128)(2,1)S(1)}, bf16[256,128]{1,0:T(8,128)(2,1)S(1)}, u32[]{:S(2)}, u32[]{:S(2)}) collective-permute-start(bf16[256,128]{1,0:T(8,128)(2,1)S(1)} %constant_dynamic-update-slice_fusion.4), channel_id=1, source_target_pairs={{128,0},{192,64},{0,128},{64,192},{129,1},{193,65},{1,129},{65,193... | collective-permute-start | bytes 196616 | tf_op jit(solution)/shard_map/ppermute | solution.py:26
  21.1 3.8 %collective-permute-start.3 = (bf16[256,128]{1,0:T(8,128)(2,1)S(1)}, bf16[256,128]{1,0:T(8,128)(2,1)S(1)}, u32[]{:S(2)}, u32[]{:S(2)}) collective-permute-start(bf16[256,128]{1,0:T(8,128)(2,1)S(1)} %constant_dynamic-update-slice_fusion.4), channel_id=1, source_target_pairs={{64,0},{128,64},{192,128},{0,192},{65,1},{129,65},{193,129},{1,193... | collective-permute-start | bytes 196616 | tf_op jit(solution)/shard_map/ppermute | solution.py:26
  26.4 4.6 %collective-permute-start.6 = (bf16[8,128,128]{2,1,0:T(8,128)(2,1)S(1)}, bf16[8,128,128]{2,1,0:T(8,128)(2,1)S(1)}, u32[]{:S(2)}, u32[]{:S(2)}) collective-permute-start(bf16[8,128,128]{2,1,0:T(8,128)(2,1)S(1)} %all-to-all-done), channel_id=1, source_target_pairs={{32,0},{0,32},{33,1},{1,33},{34,2},{2,34},{35,3},{3,35},{36,4},{4,... | collective-permute-start | bytes 786440 | tf_op jit(solution)/shard_map/ppermute | solution.py:26
  32.0 12.8 %copy-start = (f32[64,128]{1,0:T(8,128)S(1)}, f32[64,128]{1,0:T(8,128)}, u32[]{:S(2)}) copy-start(f32[64,128]{1,0:T(8,128)} %get-tuple-element.8) | copy-start | bytes 98308
  32.0 12.8 %copy-start.1 = (f32[64,128]{1,0:T(8,128)S(1)}, f32[64,128]{1,0:T(8,128)}, u32[]{:S(2)}) copy-start(f32[64,128]{1,0:T(8,128)} %get-tuple-element.7) | copy-start | bytes 98308
  32.0 12.8 %copy-start.2 = (f32[128,128]{1,0:T(8,128)S(1)}, f32[128,128]{1,0:T(8,128)}, u32[]{:S(2)}) copy-start(f32[128,128]{1,0:T(8,128)} %get-tuple-element.11) | copy-start | bytes 196612
  57.8 3.9 %collective-permute-start.7 = (bf16[512,128]{1,0:T(8,128)(2,1)S(1)}, bf16[512,128]{1,0:T(8,128)(2,1)S(1)}, u32[]{:S(2)}, u32[]{:S(2)}) collective-permute-start(bf16[512,128]{1,0:T(8,128)(2,1)S(1)} %bitcast.41), channel_id=1, source_target_pairs={{32,0},{0,32},{33,1},{1,33},{34,2},{2,34},{35,3},{3,35},{36,4},{4,... | collective-permute-start | bytes 393224 | tf_op jit(solution)/shard_map/ppermute | solution.py:26
  73.8 2.4 %collective-permute-start.8 = (f32[1,128]{1,0:T(1,128)S(1)}, f32[1,128]{1,0:T(1,128)S(1)}, u32[]{:S(2)}, u32[]{:S(2)}) collective-permute-start(f32[1,128]{1,0:T(1,128)S(1)} %bitcast.58), channel_id=1, source_target_pairs={{32,0},{0,32},{33,1},{1,33},{34,2},{2,34},{35,3},{3,35},{36,4},{4,... | collective-permute-start | bytes 1544 | tf_op jit(solution)/shard_map/ppermute | solution.py:26

commit v9 on v8

--- a/solution.py
+++ b/solution.py
@@ -26,10 +26,12 @@
     return lax.ppermute(x, axis, [((i + k) % n, i) for i in range(n)])
 
 
-def around(x, axis, base):
+def around(x, axis, base, behind=None):
     n, me = lax.axis_size(axis), lax.axis_index(axis)
     for k in range(n):
         block = ahead(x, axis, k) if k else x
+        if k == 1 and behind is not None:
+            block, behind = lax.optimization_barrier((block, behind))
         base = lax.dynamic_update_slice_in_dim(base, block, (me + k) % n * x.shape[0], 0)
     return base
 
@@ -109,11 +111,11 @@
     return pl.pallas_call(
         body,
         out_shape=(
-            jax.ShapeDtypeStruct((own, width), f32),
-            jax.ShapeDtypeStruct((own, width), f32),
-            jax.ShapeDtypeStruct((width, width), f32),
+            pltpu.VMEM((own, width), f32),
+            pltpu.VMEM((own, width), f32),
+            pltpu.VMEM((width, width), f32),
             jax.ShapeDtypeStruct((copies, 2 * own, width), bf16),
-            jax.ShapeDtypeStruct((own, width), bf16),
+            pltpu.VMEM((own, width), bf16),
         ),
         in_specs=[VMEM] * 5,
         out_specs=(VMEM,) * 5,
@@ -163,9 +165,9 @@
         observed, lengths, features, length_scale, epoch_gain, lax.axis_size(Z)
     )
     here = lax.all_to_all(outgoing, Z, split_axis=0, concat_axis=0, tiled=True)
+    there = ahead(here, C, 1)
     line = around(left, X, jnp.zeros((lax.axis_size(X) * own, width), bf16))
-    lefts = around(line, Y, jnp.zeros((lax.axis_size(Y) * line.shape[0], width), bf16))
-    there = ahead(here, C, 1)
+    lefts = around(line, Y, jnp.zeros((lax.axis_size(Y) * line.shape[0], width), bf16), there)
     k_here = block_kernel(lefts, here[:, own:].reshape(-1, width))
     k_there = block_kernel(lefts, there[:, own:].reshape(-1, width))
 

time: 93.7 us -> 91.2 us (0.973)
  blocking collectives: 52.5 us -> 50.1 us
  waiting for transfers between devices: 5.54 us -> 6.58 us
    all_to_all x1, waiting for transfers between devices: 0.8 us -> 4.14 us  [per_device(): here = lax.all_to_all(outgoing, Z, split_axis=0, concat_axis=0, tiled=True)]
    all_to_all x2, blocking collectives: 28.8 us -> 26.4 us  [to_all(): return lax.all_to_all(copies, axes, split_axis=0, concat_axis=0, tiled=True)]
    ppermute x9, waiting for transfers between devices: 4.73 us -> 2.44 us  [ahead(): return lax.ppermute(x, axis, [((i + k) % n, i) for i in range(n)])]
  transfers between devices with their start and end apart: 10 -> 10, of which waited for: 5 -> 4; matrix products, arithmetic and copies ran while one was open for 2% -> 1% of each run, Pallas kernels for 0% -> 0%
where the time goes in v9:
time: 91.2 us; the launch traced here: 90.8 us
  blocking collectives  50.1 us (55%)
  starting transfers between devices  26.5 us (29%)
  waiting for transfers between devices  6.58 us (7%)
  matrix products  3.22 us (4%)
  Pallas kernels  1.87 us (2%)
  other arithmetic  1.27 us (1%)
  between operations  0.99 us (1%)
    all_to_all x2, blocking collectives, to_all(): return lax.all_to_all(copies, axes, split_axis=0, concat_axis=0, tiled=True)  26.4 us
    all_to_all x2, blocking collectives, product(): lax.all_to_all(jnp.concatenate([part, tail], axis=1), (Y, X), split_axis=...  23.7 us
    ppermute x9, starting transfers between devices, ahead(): return lax.ppermute(x, axis, [((i + k) % n, i) for i in range(n)])  18.3 us
    all_to_all x1, starting transfers between devices, per_device(): here = lax.all_to_all(outgoing, Z, split_axis=0, concat_axis=0, tiled=True)  8.18 us
    all_to_all x1, waiting for transfers between devices, per_device(): here = lax.all_to_all(outgoing, Z, split_axis=0, concat_axis=0, tiled=True)  4.14 us
    ppermute x9, waiting for transfers between devices, ahead(): return lax.ppermute(x, axis, [((i + k) % n, i) for i in range(n)])  2.44 us
    pallas_call x1, Pallas kernels, prepare(): pl.pallas_call(body, out_shape=(pltpu.VMEM((own, width), f32), pltpu.VMEM...  1.87 us
  transfers between devices with their start and end apart: 10, of which 4 were waited for; matrix products, arithmetic and copies ran while one was open for 1% of the time, Pallas kernels for 0%

profile of v9, /device:TPU:1, one launch (start us, length us, event | category | flops | bytes accessed | tf_op | source)
XLA Modules:
  0.0 90.8 jit_solution(8046814485469808706)
XLA Ops:
  0.6 1.9 %prepare.1 = (f32[64,128]{1,0:T(8,128)S(1)}, f32[64,128]{1,0:T(8,128)S(1)}, f32[128,128]{1,0:T(8,128)S(1)}, bf16[8,128,128]{2,1,0:T(8,128)(2,1)}, bf16[64,128]{1,0:T(8,128)(2,1)S(1)}) custom-call(f32[64,128]{1,0:T(8,128)} %obs_ref.1, s32[1,64]{1,0:T(1,128)} %bitcast.51, f32[32,64]{1,0:T(8,128)} %bitcast.50, f32[1,32]{1,0:T(1,128)} %bitcast.52, f32[1,128]{1,0:T(1,128)} %bitcast.53), custom_call_target="tpu_custom_call" | custom-call | tf_op jit(solution)/shard_map/prepare/pallas_call | solution.py:111
  2.5 2.0 %collective-permute-start.2 = (bf16[64,128]{1,0:T(8,128)(2,1)S(1)}, bf16[64,128]{1,0:T(8,128)(2,1)S(1)}, u32[]{:S(2)}, u32[]{:S(2)}) collective-permute-start(bf16[64,128]{1,0:T(8,128)(2,1)S(1)} %get-tuple-element.10), channel_id=1, source_target_pairs={{3,0},{0,1},{1,2},{2,3},{7,4},{4,5},{5,6},{6,7},{11,8},{8,9},{9,10... | collective-permute-start | bytes 49160 | tf_op jit(solution)/shard_map/ppermute | solution.py:26
  4.5 2.5 %collective-permute-start.1 = (bf16[64,128]{1,0:T(8,128)(2,1)S(1)}, bf16[64,128]{1,0:T(8,128)(2,1)S(1)}, u32[]{:S(2)}, u32[]{:S(2)}) collective-permute-start(bf16[64,128]{1,0:T(8,128)(2,1)S(1)} %get-tuple-element.10), channel_id=1, source_target_pairs={{2,0},{3,1},{0,2},{1,3},{6,4},{7,5},{4,6},{5,7},{10,8},{11,9},{8,1... | collective-permute-start | bytes 49160 | tf_op jit(solution)/shard_map/ppermute | solution.py:26
  7.0 1.2 %collective-permute-start = (bf16[64,128]{1,0:T(8,128)(2,1)S(1)}, bf16[64,128]{1,0:T(8,128)(2,1)S(1)}, u32[]{:S(2)}, u32[]{:S(2)}) collective-permute-start(bf16[64,128]{1,0:T(8,128)(2,1)S(1)} %get-tuple-element.10), channel_id=1, source_target_pairs={{1,0},{2,1},{3,2},{0,3},{5,4},{6,5},{7,6},{4,7},{9,8},{10,9},{11,1... | collective-permute-start | bytes 49160 | tf_op jit(solution)/shard_map/ppermute | solution.py:26
  8.2 8.2 %all-to-all-start = ((bf16[8,128,128]{2,1,0:T(8,128)(2,1)}), bf16[8,128,128]{2,1,0:T(8,128)(2,1)S(1)}, u32[]{:S(2)}, u32[]{:S(2)}) async-start(bf16[8,128,128]{2,1,0:T(8,128)(2,1)} %get-tuple-element.11), calls=%async_computation | async-start | bytes 524288 | tf_op jit(solution)/shard_map/all_to_all | solution.py:167
  16.6 1.4 %collective-permute-start.6 = (bf16[256,128]{1,0:T(8,128)(2,1)S(1)}, bf16[256,128]{1,0:T(8,128)(2,1)S(1)}, u32[]{:S(2)}, u32[]{:S(2)}) collective-permute-start(bf16[256,128]{1,0:T(8,128)(2,1)S(1)} %constant_dynamic-update-slice_fusion.4), channel_id=1, source_target_pairs={{192,0},{0,64},{64,128},{128,192},{193,1},{1,65},{65,129},{129,193... | collective-permute-start | bytes 196616 | tf_op jit(solution)/shard_map/ppermute | solution.py:26
  17.9 2.6 %collective-permute-start.5 = (bf16[256,128]{1,0:T(8,128)(2,1)S(1)}, bf16[256,128]{1,0:T(8,128)(2,1)S(1)}, u32[]{:S(2)}, u32[]{:S(2)}) collective-permute-start(bf16[256,128]{1,0:T(8,128)(2,1)S(1)} %constant_dynamic-update-slice_fusion.4), channel_id=1, source_target_pairs={{128,0},{192,64},{0,128},{64,192},{129,1},{193,65},{1,129},{65,193... | collective-permute-start | bytes 196616 | tf_op jit(solution)/shard_map/ppermute | solution.py:26
  20.6 1.1 %collective-permute-start.3 = (bf16[256,128]{1,0:T(8,128)(2,1)S(1)}, bf16[256,128]{1,0:T(8,128)(2,1)S(1)}, u32[]{:S(2)}, u32[]{:S(2)}) collective-permute-start(bf16[256,128]{1,0:T(8,128)(2,1)S(1)} %constant_dynamic-update-slice_fusion.4), channel_id=1, source_target_pairs={{64,0},{128,64},{192,128},{0,192},{65,1},{129,65},{193,129},{1,193... | collective-permute-start | bytes 196616 | tf_op jit(solution)/shard_map/ppermute | solution.py:26
  21.7 4.1 %all-to-all-done = bf16[8,128,128]{2,1,0:T(8,128)(2,1)S(1)} async-done(((bf16[8,128,128]{2,1,0:T(8,128)(2,1)}), bf16[8,128,128]{2,1,0:T(8,128)(2,1)S(1)}, u32[]{:S(2)}, u32[]{:S(2)}) %all-to-all-start) | async-done | bytes 262176 | tf_op jit(solution)/shard_map/all_to_all | solution.py:167
  25.8 3.3 %collective-permute-start.4 = (bf16[8,128,128]{2,1,0:T(8,128)(2,1)S(1)}, bf16[8,128,128]{2,1,0:T(8,128)(2,1)S(1)}, u32[]{:S(2)}, u32[]{:S(2)}) collective-permute-start(bf16[8,128,128]{2,1,0:T(8,128)(2,1)S(1)} %all-to-all-done), channel_id=1, source_target_pairs={{32,0},{0,32},{33,1},{1,33},{34,2},{2,34},{35,3},{3,35},{36,4},{4,... | collective-permute-start | bytes 786440 | tf_op jit(solution)/shard_map/ppermute | solution.py:26
  29.2 1.1 %collective-permute-done.4 = bf16[8,128,128]{2,1,0:T(8,128)(2,1)S(1)} collective-permute-done((bf16[8,128,128]{2,1,0:T(8,128)(2,1)S(1)}, bf16[8,128,128]{2,1,0:T(8,128)(2,1)S(1)}, u32[]{:S(2)}, u32[]{:S(2)}) %collective-permute-start.4) | collective-permute-done | bytes 262176 | tf_op jit(solution)/shard_map/ppermute | solution.py:26
  30.5 0.5 exponential_convert_fusion
  31.0 0.5 exponential_convert_fusion.1
  31.9 0.5 fusion.3
  32.5 12.6 %all_to_all.25 = f16[16,72,128]{2,1,0:T(8,128)(2,1)S(1)} all-to-all(f16[16,72,128]{2,1,0:T(8,128)(2,1)S(1)} %pad_maximum_fusion), channel_id=1, replica_groups=mesh['y'=4,'c'=2,'z'=8,'x'=4] {'y','x'}, dimensions={0} | all-to-all | bytes 589824 | tf_op jit(solution)/shard_map/all_to_all | solution.py:181
  45.4 10.3 %all_to_all.26 = bf16[8,64,128]{2,1,0:T(8,128)(2,1)S(1)} all-to-all(bf16[8,64,128]{2,1,0:T(8,128)(2,1)S(1)} %broadcast_in_dim.57), channel_id=1, replica_groups=mesh['y'=4,'c'=2,'z'=8,'x'=4] {'z'}, dimensions={0} | all-to-all | bytes 262144 | tf_op jit(solution)/shard_map/all_to_all | solution.py:41
  55.8 2.7 %collective-permute-start.7 = (bf16[512,128]{1,0:T(8,128)(2,1)S(1)}, bf16[512,128]{1,0:T(8,128)(2,1)S(1)}, u32[]{:S(2)}, u32[]{:S(2)}) collective-permute-start(bf16[512,128]{1,0:T(8,128)(2,1)S(1)} %bitcast.41), channel_id=1, source_target_pairs={{32,0},{0,32},{33,1},{1,33},{34,2},{2,34},{35,3},{3,35},{36,4},{4,... | collective-permute-start | bytes 393224 | tf_op jit(solution)/shard_map/ppermute | solution.py:26
  58.9 0.5 collective-permute-done.7
  59.5 0.5 fusion.2
  60.0 11.1 %all_to_all.27 = f16[16,72,128]{2,1,0:T(8,128)(2,1)S(1)} all-to-all(f16[16,72,128]{2,1,0:T(8,128)(2,1)S(1)} %pad_maximum_fusion.1), channel_id=1, replica_groups=mesh['y'=4,'c'=2,'z'=8,'x'=4] {'y','x'}, dimensions={0} | all-to-all | bytes 589824 | tf_op jit(solution)/shard_map/all_to_all | solution.py:181
  71.4 1.6 %collective-permute-start.8 = (f32[1,128]{1,0:T(1,128)S(1)}, f32[1,128]{1,0:T(1,128)S(1)}, u32[]{:S(2)}, u32[]{:S(2)}) collective-permute-start(f32[1,128]{1,0:T(1,128)S(1)} %bitcast.58), channel_id=1, source_target_pairs={{32,0},{0,32},{33,1},{1,33},{34,2},{2,34},{35,3},{3,35},{36,4},{4,... | collective-permute-start | bytes 1544 | tf_op jit(solution)/shard_map/ppermute | solution.py:26
  73.0 0.8 collective-permute-done.8
  73.9 16.1 %all_to_all.28 = f32[128,1,128]{2,1,0:T(1,128)S(1)} all-to-all(f32[128,1,128]{2,1,0:T(1,128)S(1)} %broadcast_in_dim.61), channel_id=1, replica_groups=mesh['y'=4,'c'=2,'z'=8,'x'=4] {'y','z','x'}, dimensions={0} | all-to-all | bytes 131072 | tf_op jit(solution)/shard_map/all_to_all | solution.py:41
  90.2 0.6 multiply_add_fusion
  (50 shorter events, 2.3 us)
Async XLA Ops:
  2.5 14.0 %collective-permute-start.2 = (bf16[64,128]{1,0:T(8,128)(2,1)S(1)}, bf16[64,128]{1,0:T(8,128)(2,1)S(1)}, u32[]{:S(2)}, u32[]{:S(2)}) collective-permute-start(bf16[64,128]{1,0:T(8,128)(2,1)S(1)} %get-tuple-element.10), channel_id=1, source_target_pairs={{3,0},{0,1},{1,2},{2,3},{7,4},{4,5},{5,6},{6,7},{11,8},{8,9},{9,10... | collective-permute-start | bytes 49160 | tf_op jit(solution)/shard_map/ppermute | solution.py:26
  4.5 12.0 %collective-permute-start.1 = (bf16[64,128]{1,0:T(8,128)(2,1)S(1)}, bf16[64,128]{1,0:T(8,128)(2,1)S(1)}, u32[]{:S(2)}, u32[]{:S(2)}) collective-permute-start(bf16[64,128]{1,0:T(8,128)(2,1)S(1)} %get-tuple-element.10), channel_id=1, source_target_pairs={{2,0},{3,1},{0,2},{1,3},{6,4},{7,5},{4,6},{5,7},{10,8},{11,9},{8,1... | collective-permute-start | bytes 49160 | tf_op jit(solution)/shard_map/ppermute | solution.py:26
  7.0 9.5 %collective-permute-start = (bf16[64,128]{1,0:T(8,128)(2,1)S(1)}, bf16[64,128]{1,0:T(8,128)(2,1)S(1)}, u32[]{:S(2)}, u32[]{:S(2)}) collective-permute-start(bf16[64,128]{1,0:T(8,128)(2,1)S(1)} %get-tuple-element.10), channel_id=1, source_target_pairs={{1,0},{2,1},{3,2},{0,3},{5,4},{6,5},{7,6},{4,7},{9,8},{10,9},{11,1... | collective-permute-start | bytes 49160 | tf_op jit(solution)/shard_map/ppermute | solution.py:26
  8.2 17.7 %all-to-all-start = ((bf16[8,128,128]{2,1,0:T(8,128)(2,1)}), bf16[8,128,128]{2,1,0:T(8,128)(2,1)S(1)}, u32[]{:S(2)}, u32[]{:S(2)}) async-start(bf16[8,128,128]{2,1,0:T(8,128)(2,1)} %get-tuple-element.11), calls=%async_computation | async-start | bytes 524288 | tf_op jit(solution)/shard_map/all_to_all | solution.py:167
  16.6 13.9 %collective-permute-start.6 = (bf16[256,128]{1,0:T(8,128)(2,1)S(1)}, bf16[256,128]{1,0:T(8,128)(2,1)S(1)}, u32[]{:S(2)}, u32[]{:S(2)}) collective-permute-start(bf16[256,128]{1,0:T(8,128)(2,1)S(1)} %constant_dynamic-update-slice_fusion.4), channel_id=1, source_target_pairs={{192,0},{0,64},{64,128},{128,192},{193,1},{1,65},{65,129},{129,193... | collective-permute-start | bytes 196616 | tf_op jit(solution)/shard_map/ppermute | solution.py:26
  17.9 12.5 %collective-permute-start.5 = (bf16[256,128]{1,0:T(8,128)(2,1)S(1)}, bf16[256,128]{1,0:T(8,128)(2,1)S(1)}, u32[]{:S(2)}, u32[]{:S(2)}) collective-permute-start(bf16[256,128]{1,0:T(8,128)(2,1)S(1)} %constant_dynamic-update-slice_fusion.4), channel_id=1, source_target_pairs={{128,0},{192,64},{0,128},{64,192},{129,1},{193,65},{1,129},{65,193... | collective-permute-start | bytes 196616 | tf_op jit(solution)/shard_map/ppermute | solution.py:26
  20.6 8.7 %collective-permute-start.3 = (bf16[256,128]{1,0:T(8,128)(2,1)S(1)}, bf16[256,128]{1,0:T(8,128)(2,1)S(1)}, u32[]{:S(2)}, u32[]{:S(2)}) collective-permute-start(bf16[256,128]{1,0:T(8,128)(2,1)S(1)} %constant_dynamic-update-slice_fusion.4), channel_id=1, source_target_pairs={{64,0},{128,64},{192,128},{0,192},{65,1},{129,65},{193,129},{1,193... | collective-permute-start | bytes 196616 | tf_op jit(solution)/shard_map/ppermute | solution.py:26
  25.8 4.5 %collective-permute-start.4 = (bf16[8,128,128]{2,1,0:T(8,128)(2,1)S(1)}, bf16[8,128,128]{2,1,0:T(8,128)(2,1)S(1)}, u32[]{:S(2)}, u32[]{:S(2)}) collective-permute-start(bf16[8,128,128]{2,1,0:T(8,128)(2,1)S(1)} %all-to-all-done), channel_id=1, source_target_pairs={{32,0},{0,32},{33,1},{1,33},{34,2},{2,34},{35,3},{3,35},{36,4},{4,... | collective-permute-start | bytes 786440 | tf_op jit(solution)/shard_map/ppermute | solution.py:26
  55.8 3.6 %collective-permute-start.7 = (bf16[512,128]{1,0:T(8,128)(2,1)S(1)}, bf16[512,128]{1,0:T(8,128)(2,1)S(1)}, u32[]{:S(2)}, u32[]{:S(2)}) collective-permute-start(bf16[512,128]{1,0:T(8,128)(2,1)S(1)} %bitcast.41), channel_id=1, source_target_pairs={{32,0},{0,32},{33,1},{1,33},{34,2},{2,34},{35,3},{3,35},{36,4},{4,... | collective-permute-start | bytes 393224 | tf_op jit(solution)/shard_map/ppermute | solution.py:26
  71.4 2.4 %collective-permute-start.8 = (f32[1,128]{1,0:T(1,128)S(1)}, f32[1,128]{1,0:T(1,128)S(1)}, u32[]{:S(2)}, u32[]{:S(2)}) collective-permute-start(f32[1,128]{1,0:T(1,128)S(1)} %bitcast.58), channel_id=1, source_target_pairs={{32,0},{0,32},{33,1},{1,33},{34,2},{2,34},{35,3},{3,35},{36,4},{4,... | collective-permute-start | bytes 1544 | tf_op jit(solution)/shard_map/ppermute | solution.py:26

commit v10 on v9

--- a/solution.py
+++ b/solution.py
@@ -142,13 +142,10 @@
     m = jnp.sum(moments, axis=0, keepdims=True)
     m = across(jnp.where(pick(4, m.shape[1]), m, 0.0))
     m0, m1, m2, m3 = (m[k : k + 1] for k in range(4))
-    alpha = m0 / m1
-    norm = m0 + alpha * (alpha * m2 - 2.0 * m1)
-    keep = 1.0 + norm / m0
-    curve = keep * (keep * m1 - 2.0 * alpha * m2) + alpha * alpha * m3
-    again = norm / curve
-    on0 = alpha + again * keep
-    on1 = again * alpha
+    t1, t2, t3 = m1 / m0, m2 / m1, m3 / m2
+    alpha = (t2 - t1) / (t2 * (t3 - t2))
+    on0 = (1.0 + alpha * t2) / t1
+    on1 = alpha / t1
     return on0 * v0 - on1 * v1, v0 - on0 * v1 + on1 * v2
 
 
@@ -168,8 +165,8 @@
     there = ahead(here, C, 1)
     line = around(left, X, jnp.zeros((lax.axis_size(X) * own, width), bf16))
     lefts = around(line, Y, jnp.zeros((lax.axis_size(Y) * line.shape[0], width), bf16), there)
-    k_here = block_kernel(lefts, here[:, own:].reshape(-1, width))
-    k_there = block_kernel(lefts, there[:, own:].reshape(-1, width))
+    k_all = block_kernel(lefts, jnp.concatenate([here[:, own:], there[:, own:]]).reshape(-1, width))
+    k_here, k_there = k_all[:, : k_all.shape[1] // 2], k_all[:, k_all.shape[1] // 2 :]
 
     def product(w_here, w_there):
         part = jnp.dot(k_here, w_here, preferred_element_type=f32)

time: 91.2 us -> 91.1 us (level)
  no operation moved by 1% of the time
where the time goes in v10:
time: 91.1 us; the launch traced here: 90.7 us
  blocking collectives  50.1 us (55%)
  starting transfers between devices  26.4 us (29%)
  waiting for transfers between devices  6.58 us (7%)
  matrix products  3.06 us (3%)
  Pallas kernels  1.87 us (2%)
  other arithmetic  1.3 us (1%)
  between operations  0.98 us (1%)
    all_to_all x2, blocking collectives, to_all(): return lax.all_to_all(copies, axes, split_axis=0, concat_axis=0, tiled=True)  26.4 us
    all_to_all x2, blocking collectives, product(): lax.all_to_all(jnp.concatenate([part, tail], axis=1), (Y, X), split_axis=...  23.7 us
    ppermute x9, starting transfers between devices, ahead(): return lax.ppermute(x, axis, [((i + k) % n, i) for i in range(n)])  18.3 us
    all_to_all x1, starting transfers between devices, per_device(): here = lax.all_to_all(outgoing, Z, split_axis=0, concat_axis=0, tiled=True)  8.18 us
    all_to_all x1, waiting for transfers between devices, per_device(): here = lax.all_to_all(outgoing, Z, split_axis=0, concat_axis=0, tiled=True)  4.14 us
    ppermute x9, waiting for transfers between devices, ahead(): return lax.ppermute(x, axis, [((i + k) % n, i) for i in range(n)])  2.44 us
    pallas_call x1, Pallas kernels, prepare(): pl.pallas_call(body, out_shape=(pltpu.VMEM((own, width), f32), pltpu.VMEM...  1.87 us
  transfers between devices with their start and end apart: 10, of which 4 were waited for; matrix products, arithmetic and copies ran while one was open for 1% of the time, Pallas kernels for 0%

profile of v10, /device:TPU:1, one launch (start us, length us, event | category | flops | bytes accessed | tf_op | source)
XLA Modules:
  0.0 90.7 jit_solution(7663538772679848622)
XLA Ops:
  0.6 1.9 %prepare.1 = (f32[64,128]{1,0:T(8,128)S(1)}, f32[64,128]{1,0:T(8,128)S(1)}, f32[128,128]{1,0:T(8,128)S(1)}, bf16[8,128,128]{2,1,0:T(8,128)(2,1)}, bf16[64,128]{1,0:T(8,128)(2,1)S(1)}) custom-call(f32[64,128]{1,0:T(8,128)} %obs_ref.1, s32[1,64]{1,0:T(1,128)} %bitcast.43, f32[32,64]{1,0:T(8,128)} %bitcast.42, f32[1,32]{1,0:T(1,128)} %bitcast.44, f32[1,128]{1,0:T(1,128)} %bitcast.45), custom_call_target="tpu_custom_call" | custom-call | tf_op jit(solution)/shard_map/prepare/pallas_call | solution.py:111
  2.5 2.0 %collective-permute-start.2 = (bf16[64,128]{1,0:T(8,128)(2,1)S(1)}, bf16[64,128]{1,0:T(8,128)(2,1)S(1)}, u32[]{:S(2)}, u32[]{:S(2)}) collective-permute-start(bf16[64,128]{1,0:T(8,128)(2,1)S(1)} %get-tuple-element.10), channel_id=1, source_target_pairs={{3,0},{0,1},{1,2},{2,3},{7,4},{4,5},{5,6},{6,7},{11,8},{8,9},{9,10... | collective-permute-start | bytes 49160 | tf_op jit(solution)/shard_map/ppermute | solution.py:26
  4.5 2.5 %collective-permute-start.1 = (bf16[64,128]{1,0:T(8,128)(2,1)S(1)}, bf16[64,128]{1,0:T(8,128)(2,1)S(1)}, u32[]{:S(2)}, u32[]{:S(2)}) collective-permute-start(bf16[64,128]{1,0:T(8,128)(2,1)S(1)} %get-tuple-element.10), channel_id=1, source_target_pairs={{2,0},{3,1},{0,2},{1,3},{6,4},{7,5},{4,6},{5,7},{10,8},{11,9},{8,1... | collective-permute-start | bytes 49160 | tf_op jit(solution)/shard_map/ppermute | solution.py:26
  7.0 1.2 %collective-permute-start = (bf16[64,128]{1,0:T(8,128)(2,1)S(1)}, bf16[64,128]{1,0:T(8,128)(2,1)S(1)}, u32[]{:S(2)}, u32[]{:S(2)}) collective-permute-start(bf16[64,128]{1,0:T(8,128)(2,1)S(1)} %get-tuple-element.10), channel_id=1, source_target_pairs={{1,0},{2,1},{3,2},{0,3},{5,4},{6,5},{7,6},{4,7},{9,8},{10,9},{11,1... | collective-permute-start | bytes 49160 | tf_op jit(solution)/shard_map/ppermute | solution.py:26
  8.2 8.2 %all-to-all-start = ((bf16[8,128,128]{2,1,0:T(8,128)(2,1)}), bf16[8,128,128]{2,1,0:T(8,128)(2,1)S(1)}, u32[]{:S(2)}, u32[]{:S(2)}) async-start(bf16[8,128,128]{2,1,0:T(8,128)(2,1)} %get-tuple-element.11), calls=%async_computation | async-start | bytes 524288 | tf_op jit(solution)/shard_map/all_to_all | solution.py:164
  16.6 1.4 %collective-permute-start.6 = (bf16[256,128]{1,0:T(8,128)(2,1)S(1)}, bf16[256,128]{1,0:T(8,128)(2,1)S(1)}, u32[]{:S(2)}, u32[]{:S(2)}) collective-permute-start(bf16[256,128]{1,0:T(8,128)(2,1)S(1)} %constant_dynamic-update-slice_fusion.4), channel_id=1, source_target_pairs={{192,0},{0,64},{64,128},{128,192},{193,1},{1,65},{65,129},{129,193... | collective-permute-start | bytes 196616 | tf_op jit(solution)/shard_map/ppermute | solution.py:26
  17.9 2.6 %collective-permute-start.5 = (bf16[256,128]{1,0:T(8,128)(2,1)S(1)}, bf16[256,128]{1,0:T(8,128)(2,1)S(1)}, u32[]{:S(2)}, u32[]{:S(2)}) collective-permute-start(bf16[256,128]{1,0:T(8,128)(2,1)S(1)} %constant_dynamic-update-slice_fusion.4), channel_id=1, source_target_pairs={{128,0},{192,64},{0,128},{64,192},{129,1},{193,65},{1,129},{65,193... | collective-permute-start | bytes 196616 | tf_op jit(solution)/shard_map/ppermute | solution.py:26
  20.6 1.1 %collective-permute-start.3 = (bf16[256,128]{1,0:T(8,128)(2,1)S(1)}, bf16[256,128]{1,0:T(8,128)(2,1)S(1)}, u32[]{:S(2)}, u32[]{:S(2)}) collective-permute-start(bf16[256,128]{1,0:T(8,128)(2,1)S(1)} %constant_dynamic-update-slice_fusion.4), channel_id=1, source_target_pairs={{64,0},{128,64},{192,128},{0,192},{65,1},{129,65},{193,129},{1,193... | collective-permute-start | bytes 196616 | tf_op jit(solution)/shard_map/ppermute | solution.py:26
  21.7 4.1 %all-to-all-done = bf16[8,128,128]{2,1,0:T(8,128)(2,1)S(1)} async-done(((bf16[8,128,128]{2,1,0:T(8,128)(2,1)}), bf16[8,128,128]{2,1,0:T(8,128)(2,1)S(1)}, u32[]{:S(2)}, u32[]{:S(2)}) %all-to-all-start) | async-done | bytes 262176 | tf_op jit(solution)/shard_map/all_to_all | solution.py:164
  25.8 3.3 %collective-permute-start.4 = (bf16[8,128,128]{2,1,0:T(8,128)(2,1)S(1)}, bf16[8,128,128]{2,1,0:T(8,128)(2,1)S(1)}, u32[]{:S(2)}, u32[]{:S(2)}) collective-permute-start(bf16[8,128,128]{2,1,0:T(8,128)(2,1)S(1)} %all-to-all-done), channel_id=1, source_target_pairs={{32,0},{0,32},{33,1},{1,33},{34,2},{2,34},{35,3},{3,35},{36,4},{4,... | collective-permute-start | bytes 786440 | tf_op jit(solution)/shard_map/ppermute | solution.py:26
  29.2 1.1 %collective-permute-done.4 = bf16[8,128,128]{2,1,0:T(8,128)(2,1)S(1)} collective-permute-done((bf16[8,128,128]{2,1,0:T(8,128)(2,1)S(1)}, bf16[8,128,128]{2,1,0:T(8,128)(2,1)S(1)}, u32[]{:S(2)}, u32[]{:S(2)}) %collective-permute-start.4) | collective-permute-done | bytes 262176 | tf_op jit(solution)/shard_map/ppermute | solution.py:26
  30.5 0.8 exponential_convert_fusion
  31.4 0.4 fusion.9
  31.8 0.4 fusion.3
  32.4 12.6 %all_to_all.25 = f16[16,72,128]{2,1,0:T(8,128)(2,1)S(1)} all-to-all(f16[16,72,128]{2,1,0:T(8,128)(2,1)S(1)} %pad_maximum_fusion), channel_id=1, replica_groups=mesh['y'=4,'c'=2,'z'=8,'x'=4] {'y','x'}, dimensions={0} | all-to-all | bytes 589824 | tf_op jit(solution)/shard_map/all_to_all | solution.py:178
  45.3 10.3 %all_to_all.26 = bf16[8,64,128]{2,1,0:T(8,128)(2,1)S(1)} all-to-all(bf16[8,64,128]{2,1,0:T(8,128)(2,1)S(1)} %broadcast_in_dim.57), channel_id=1, replica_groups=mesh['y'=4,'c'=2,'z'=8,'x'=4] {'z'}, dimensions={0} | all-to-all | bytes 262144 | tf_op jit(solution)/shard_map/all_to_all | solution.py:41
  55.6 2.6 %collective-permute-start.7 = (bf16[512,128]{1,0:T(8,128)(2,1)S(1)}, bf16[512,128]{1,0:T(8,128)(2,1)S(1)}, u32[]{:S(2)}, u32[]{:S(2)}) collective-permute-start(bf16[512,128]{1,0:T(8,128)(2,1)S(1)} %bitcast.34), channel_id=1, source_target_pairs={{32,0},{0,32},{33,1},{1,33},{34,2},{2,34},{35,3},{3,35},{36,4},{4,... | collective-permute-start | bytes 393224 | tf_op jit(solution)/shard_map/ppermute | solution.py:26
  58.8 0.5 collective-permute-done.7
  59.3 0.4 fusion.2
  59.9 11.1 %all_to_all.27 = f16[16,72,128]{2,1,0:T(8,128)(2,1)S(1)} all-to-all(f16[16,72,128]{2,1,0:T(8,128)(2,1)S(1)} %pad_maximum_fusion.1), channel_id=1, replica_groups=mesh['y'=4,'c'=2,'z'=8,'x'=4] {'y','x'}, dimensions={0} | all-to-all | bytes 589824 | tf_op jit(solution)/shard_map/all_to_all | solution.py:178
  71.3 1.6 %collective-permute-start.8 = (f32[1,128]{1,0:T(1,128)S(1)}, f32[1,128]{1,0:T(1,128)S(1)}, u32[]{:S(2)}, u32[]{:S(2)}) collective-permute-start(f32[1,128]{1,0:T(1,128)S(1)} %bitcast.50), channel_id=1, source_target_pairs={{32,0},{0,32},{33,1},{1,33},{34,2},{2,34},{35,3},{3,35},{36,4},{4,... | collective-permute-start | bytes 1544 | tf_op jit(solution)/shard_map/ppermute | solution.py:26
  72.9 0.8 collective-permute-done.8
  73.7 16.1 %all_to_all.28 = f32[128,1,128]{2,1,0:T(1,128)S(1)} all-to-all(f32[128,1,128]{2,1,0:T(1,128)S(1)} %broadcast_in_dim.61), channel_id=1, replica_groups=mesh['y'=4,'c'=2,'z'=8,'x'=4] {'y','z','x'}, dimensions={0} | all-to-all | bytes 131072 | tf_op jit(solution)/shard_map/all_to_all | solution.py:41
  90.0 0.6 multiply_add_fusion
  (49 shorter events, 1.9 us)
Async XLA Ops:
  2.5 14.0 %collective-permute-start.2 = (bf16[64,128]{1,0:T(8,128)(2,1)S(1)}, bf16[64,128]{1,0:T(8,128)(2,1)S(1)}, u32[]{:S(2)}, u32[]{:S(2)}) collective-permute-start(bf16[64,128]{1,0:T(8,128)(2,1)S(1)} %get-tuple-element.10), channel_id=1, source_target_pairs={{3,0},{0,1},{1,2},{2,3},{7,4},{4,5},{5,6},{6,7},{11,8},{8,9},{9,10... | collective-permute-start | bytes 49160 | tf_op jit(solution)/shard_map/ppermute | solution.py:26
  4.5 12.0 %collective-permute-start.1 = (bf16[64,128]{1,0:T(8,128)(2,1)S(1)}, bf16[64,128]{1,0:T(8,128)(2,1)S(1)}, u32[]{:S(2)}, u32[]{:S(2)}) collective-permute-start(bf16[64,128]{1,0:T(8,128)(2,1)S(1)} %get-tuple-element.10), channel_id=1, source_target_pairs={{2,0},{3,1},{0,2},{1,3},{6,4},{7,5},{4,6},{5,7},{10,8},{11,9},{8,1... | collective-permute-start | bytes 49160 | tf_op jit(solution)/shard_map/ppermute | solution.py:26
  7.0 9.5 %collective-permute-start = (bf16[64,128]{1,0:T(8,128)(2,1)S(1)}, bf16[64,128]{1,0:T(8,128)(2,1)S(1)}, u32[]{:S(2)}, u32[]{:S(2)}) collective-permute-start(bf16[64,128]{1,0:T(8,128)(2,1)S(1)} %get-tuple-element.10), channel_id=1, source_target_pairs={{1,0},{2,1},{3,2},{0,3},{5,4},{6,5},{7,6},{4,7},{9,8},{10,9},{11,1... | collective-permute-start | bytes 49160 | tf_op jit(solution)/shard_map/ppermute | solution.py:26
  8.2 17.7 %all-to-all-start = ((bf16[8,128,128]{2,1,0:T(8,128)(2,1)}), bf16[8,128,128]{2,1,0:T(8,128)(2,1)S(1)}, u32[]{:S(2)}, u32[]{:S(2)}) async-start(bf16[8,128,128]{2,1,0:T(8,128)(2,1)} %get-tuple-element.11), calls=%async_computation | async-start | bytes 524288 | tf_op jit(solution)/shard_map/all_to_all | solution.py:164
  16.6 14.0 %collective-permute-start.6 = (bf16[256,128]{1,0:T(8,128)(2,1)S(1)}, bf16[256,128]{1,0:T(8,128)(2,1)S(1)}, u32[]{:S(2)}, u32[]{:S(2)}) collective-permute-start(bf16[256,128]{1,0:T(8,128)(2,1)S(1)} %constant_dynamic-update-slice_fusion.4), channel_id=1, source_target_pairs={{192,0},{0,64},{64,128},{128,192},{193,1},{1,65},{65,129},{129,193... | collective-permute-start | bytes 196616 | tf_op jit(solution)/shard_map/ppermute | solution.py:26
  17.9 12.6 %collective-permute-start.5 = (bf16[256,128]{1,0:T(8,128)(2,1)S(1)}, bf16[256,128]{1,0:T(8,128)(2,1)S(1)}, u32[]{:S(2)}, u32[]{:S(2)}) collective-permute-start(bf16[256,128]{1,0:T(8,128)(2,1)S(1)} %constant_dynamic-update-slice_fusion.4), channel_id=1, source_target_pairs={{128,0},{192,64},{0,128},{64,192},{129,1},{193,65},{1,129},{65,193... | collective-permute-start | bytes 196616 | tf_op jit(solution)/shard_map/ppermute | solution.py:26
  20.6 8.7 %collective-permute-start.3 = (bf16[256,128]{1,0:T(8,128)(2,1)S(1)}, bf16[256,128]{1,0:T(8,128)(2,1)S(1)}, u32[]{:S(2)}, u32[]{:S(2)}) collective-permute-start(bf16[256,128]{1,0:T(8,128)(2,1)S(1)} %constant_dynamic-update-slice_fusion.4), channel_id=1, source_target_pairs={{64,0},{128,64},{192,128},{0,192},{65,1},{129,65},{193,129},{1,193... | collective-permute-start | bytes 196616 | tf_op jit(solution)/shard_map/ppermute | solution.py:26
  25.8 4.5 %collective-permute-start.4 = (bf16[8,128,128]{2,1,0:T(8,128)(2,1)S(1)}, bf16[8,128,128]{2,1,0:T(8,128)(2,1)S(1)}, u32[]{:S(2)}, u32[]{:S(2)}) collective-permute-start(bf16[8,128,128]{2,1,0:T(8,128)(2,1)S(1)} %all-to-all-done), channel_id=1, source_target_pairs={{32,0},{0,32},{33,1},{1,33},{34,2},{2,34},{35,3},{3,35},{36,4},{4,... | collective-permute-start | bytes 786440 | tf_op jit(solution)/shard_map/ppermute | solution.py:26
  55.6 3.6 %collective-permute-start.7 = (bf16[512,128]{1,0:T(8,128)(2,1)S(1)}, bf16[512,128]{1,0:T(8,128)(2,1)S(1)}, u32[]{:S(2)}, u32[]{:S(2)}) collective-permute-start(bf16[512,128]{1,0:T(8,128)(2,1)S(1)} %bitcast.34), channel_id=1, source_target_pairs={{32,0},{0,32},{33,1},{1,33},{34,2},{2,34},{35,3},{3,35},{36,4},{4,... | collective-permute-start | bytes 393224 | tf_op jit(solution)/shard_map/ppermute | solution.py:26
  71.3 2.4 %collective-permute-start.8 = (f32[1,128]{1,0:T(1,128)S(1)}, f32[1,128]{1,0:T(1,128)S(1)}, u32[]{:S(2)}, u32[]{:S(2)}) collective-permute-start(f32[1,128]{1,0:T(1,128)S(1)} %bitcast.50), channel_id=1, source_target_pairs={{32,0},{0,32},{33,1},{1,33},{34,2},{2,34},{35,3},{3,35},{36,4},{4,... | collective-permute-start | bytes 1544 | tf_op jit(solution)/shard_map/ppermute | solution.py:26

commit v11 on v9

--- a/solution.py
+++ b/solution.py
@@ -30,7 +30,7 @@
     n, me = lax.axis_size(axis), lax.axis_index(axis)
     for k in range(n):
         block = ahead(x, axis, k) if k else x
-        if k == 1 and behind is not None:
+        if k == n - 1 and behind is not None:
             block, behind = lax.optimization_barrier((block, behind))
         base = lax.dynamic_update_slice_in_dim(base, block, (me + k) % n * x.shape[0], 0)
     return base

time: 91.2 us -> 93.3 us (1.023)
  blocking collectives: 50.1 us -> 51.9 us
    all_to_all x1, waiting for transfers between devices: 4.14 us -> 1.43 us  [per_device(): here = lax.all_to_all(outgoing, Z, split_axis=0, concat_axis=0, tiled=True)]
    ppermute x9, waiting for transfers between devices: 2.44 us -> 5.1 us  [ahead(): return lax.ppermute(x, axis, [((i + k) % n, i) for i in range(n)])]
    all_to_all x2, blocking collectives: 26.4 us -> 28.3 us  [to_all(): return lax.all_to_all(copies, axes, split_axis=0, concat_axis=0, tiled=True)]
  transfers between devices with their start and end apart: 10 -> 10, of which waited for: 4 -> 5; matrix products, arithmetic and copies ran while one was open for 1% -> 1% of each run, Pallas kernels for 0% -> 0%
where the time goes in v11:
time: 93.3 us; the launch traced here: 92.9 us
  blocking collectives  51.9 us (56%)
  starting transfers between devices  26.8 us (29%)
  waiting for transfers between devices  6.53 us (7%)
  matrix products  3.23 us (3%)
  Pallas kernels  1.87 us (2%)
  other arithmetic  1.27 us (1%)
  between operations  0.98 us (1%)
    all_to_all x2, blocking collectives, to_all(): return lax.all_to_all(copies, axes, split_axis=0, concat_axis=0, tiled=True)  28.3 us
    all_to_all x2, blocking collectives, product(): lax.all_to_all(jnp.concatenate([part, tail], axis=1), (Y, X), split_axis=...  23.7 us
    ppermute x9, starting transfers between devices, ahead(): return lax.ppermute(x, axis, [((i + k) % n, i) for i in range(n)])  18.6 us
    all_to_all x1, starting transfers between devices, per_device(): here = lax.all_to_all(outgoing, Z, split_axis=0, concat_axis=0, tiled=True)  8.18 us
    ppermute x9, waiting for transfers between devices, ahead(): return lax.ppermute(x, axis, [((i + k) % n, i) for i in range(n)])  5.1 us
    pallas_call x1, Pallas kernels, prepare(): pl.pallas_call(body, out_shape=(pltpu.VMEM((own, width), f32), pltpu.VMEM...  1.87 us
  transfers between devices with their start and end apart: 10, of which 5 were waited for; matrix products, arithmetic and copies ran while one was open for 1% of the time, Pallas kernels for 0%

profile of v11, /device:TPU:1, one launch (start us, length us, event | category | flops | bytes accessed | tf_op | source)
XLA Modules:
  0.0 92.9 jit_solution(9010708744958046564)
XLA Ops:
  0.6 1.9 %prepare.1 = (f32[64,128]{1,0:T(8,128)S(1)}, f32[64,128]{1,0:T(8,128)S(1)}, f32[128,128]{1,0:T(8,128)S(1)}, bf16[8,128,128]{2,1,0:T(8,128)(2,1)}, bf16[64,128]{1,0:T(8,128)(2,1)S(1)}) custom-call(f32[64,128]{1,0:T(8,128)} %obs_ref.1, s32[1,64]{1,0:T(1,128)} %bitcast.51, f32[32,64]{1,0:T(8,128)} %bitcast.50, f32[1,32]{1,0:T(1,128)} %bitcast.52, f32[1,128]{1,0:T(1,128)} %bitcast.53), custom_call_target="tpu_custom_call" | custom-call | tf_op jit(solution)/shard_map/prepare/pallas_call | solution.py:111
  2.5 2.0 %collective-permute-start.2 = (bf16[64,128]{1,0:T(8,128)(2,1)S(1)}, bf16[64,128]{1,0:T(8,128)(2,1)S(1)}, u32[]{:S(2)}, u32[]{:S(2)}) collective-permute-start(bf16[64,128]{1,0:T(8,128)(2,1)S(1)} %get-tuple-element.10), channel_id=1, source_target_pairs={{3,0},{0,1},{1,2},{2,3},{7,4},{4,5},{5,6},{6,7},{11,8},{8,9},{9,10... | collective-permute-start | bytes 49160 | tf_op jit(solution)/shard_map/ppermute | solution.py:26
  4.5 2.5 %collective-permute-start.1 = (bf16[64,128]{1,0:T(8,128)(2,1)S(1)}, bf16[64,128]{1,0:T(8,128)(2,1)S(1)}, u32[]{:S(2)}, u32[]{:S(2)}) collective-permute-start(bf16[64,128]{1,0:T(8,128)(2,1)S(1)} %get-tuple-element.10), channel_id=1, source_target_pairs={{2,0},{3,1},{0,2},{1,3},{6,4},{7,5},{4,6},{5,7},{10,8},{11,9},{8,1... | collective-permute-start | bytes 49160 | tf_op jit(solution)/shard_map/ppermute | solution.py:26
  7.0 1.2 %collective-permute-start = (bf16[64,128]{1,0:T(8,128)(2,1)S(1)}, bf16[64,128]{1,0:T(8,128)(2,1)S(1)}, u32[]{:S(2)}, u32[]{:S(2)}) collective-permute-start(bf16[64,128]{1,0:T(8,128)(2,1)S(1)} %get-tuple-element.10), channel_id=1, source_target_pairs={{1,0},{2,1},{3,2},{0,3},{5,4},{6,5},{7,6},{4,7},{9,8},{10,9},{11,1... | collective-permute-start | bytes 49160 | tf_op jit(solution)/shard_map/ppermute | solution.py:26
  8.2 8.2 %all-to-all-start = ((bf16[8,128,128]{2,1,0:T(8,128)(2,1)}), bf16[8,128,128]{2,1,0:T(8,128)(2,1)S(1)}, u32[]{:S(2)}, u32[]{:S(2)}) async-start(bf16[8,128,128]{2,1,0:T(8,128)(2,1)} %get-tuple-element.11), calls=%async_computation | async-start | bytes 524288 | tf_op jit(solution)/shard_map/all_to_all | solution.py:167
  16.6 1.4 %collective-permute-start.5 = (bf16[256,128]{1,0:T(8,128)(2,1)S(1)}, bf16[256,128]{1,0:T(8,128)(2,1)S(1)}, u32[]{:S(2)}, u32[]{:S(2)}) collective-permute-start(bf16[256,128]{1,0:T(8,128)(2,1)S(1)} %constant_dynamic-update-slice_fusion.4), channel_id=1, source_target_pairs={{192,0},{0,64},{64,128},{128,192},{193,1},{1,65},{65,129},{129,193... | collective-permute-start | bytes 196616 | tf_op jit(solution)/shard_map/ppermute | solution.py:26
  17.9 2.6 %collective-permute-start.4 = (bf16[256,128]{1,0:T(8,128)(2,1)S(1)}, bf16[256,128]{1,0:T(8,128)(2,1)S(1)}, u32[]{:S(2)}, u32[]{:S(2)}) collective-permute-start(bf16[256,128]{1,0:T(8,128)(2,1)S(1)} %constant_dynamic-update-slice_fusion.4), channel_id=1, source_target_pairs={{128,0},{192,64},{0,128},{64,192},{129,1},{193,65},{1,129},{65,193... | collective-permute-start | bytes 196616 | tf_op jit(solution)/shard_map/ppermute | solution.py:26
  20.6 1.1 %collective-permute-start.3 = (bf16[256,128]{1,0:T(8,128)(2,1)S(1)}, bf16[256,128]{1,0:T(8,128)(2,1)S(1)}, u32[]{:S(2)}, u32[]{:S(2)}) collective-permute-start(bf16[256,128]{1,0:T(8,128)(2,1)S(1)} %constant_dynamic-update-slice_fusion.4), channel_id=1, source_target_pairs={{64,0},{128,64},{192,128},{0,192},{65,1},{129,65},{193,129},{1,193... | collective-permute-start | bytes 196616 | tf_op jit(solution)/shard_map/ppermute | solution.py:26
  21.7 2.7 %collective-permute-done.3 = bf16[256,128]{1,0:T(8,128)(2,1)S(1)} collective-permute-done((bf16[256,128]{1,0:T(8,128)(2,1)S(1)}, bf16[256,128]{1,0:T(8,128)(2,1)S(1)}, u32[]{:S(2)}, u32[]{:S(2)}) %collective-permute-start.3) | collective-permute-done | bytes 65568 | tf_op jit(solution)/shard_map/ppermute | solution.py:26
  24.4 1.4 %all-to-all-done = bf16[8,128,128]{2,1,0:T(8,128)(2,1)S(1)} async-done(((bf16[8,128,128]{2,1,0:T(8,128)(2,1)}), bf16[8,128,128]{2,1,0:T(8,128)(2,1)S(1)}, u32[]{:S(2)}, u32[]{:S(2)}) %all-to-all-start) | async-done | bytes 262176 | tf_op jit(solution)/shard_map/all_to_all | solution.py:167
  25.8 3.3 %collective-permute-start.6 = (bf16[8,128,128]{2,1,0:T(8,128)(2,1)S(1)}, bf16[8,128,128]{2,1,0:T(8,128)(2,1)S(1)}, u32[]{:S(2)}, u32[]{:S(2)}) collective-permute-start(bf16[8,128,128]{2,1,0:T(8,128)(2,1)S(1)} %all-to-all-done), channel_id=1, source_target_pairs={{32,0},{0,32},{33,1},{1,33},{34,2},{2,34},{35,3},{3,35},{36,4},{4,... | collective-permute-start | bytes 786440 | tf_op jit(solution)/shard_map/ppermute | solution.py:26
  29.2 1.1 %collective-permute-done.6 = bf16[8,128,128]{2,1,0:T(8,128)(2,1)S(1)} collective-permute-done((bf16[8,128,128]{2,1,0:T(8,128)(2,1)S(1)}, bf16[8,128,128]{2,1,0:T(8,128)(2,1)S(1)}, u32[]{:S(2)}, u32[]{:S(2)}) %collective-permute-start.6) | collective-permute-done | bytes 262176 | tf_op jit(solution)/shard_map/ppermute | solution.py:26
  30.4 0.5 exponential_convert_fusion
  30.9 0.5 exponential_convert_fusion.1
  32.4 12.6 %all_to_all.25 = f16[16,72,128]{2,1,0:T(8,128)(2,1)S(1)} all-to-all(f16[16,72,128]{2,1,0:T(8,128)(2,1)S(1)} %pad_maximum_fusion), channel_id=1, replica_groups=mesh['y'=4,'c'=2,'z'=8,'x'=4] {'y','x'}, dimensions={0} | all-to-all | bytes 589824 | tf_op jit(solution)/shard_map/all_to_all | solution.py:181
  45.4 12.2 %all_to_all.26 = bf16[8,64,128]{2,1,0:T(8,128)(2,1)S(1)} all-to-all(bf16[8,64,128]{2,1,0:T(8,128)(2,1)S(1)} %broadcast_in_dim.57), channel_id=1, replica_groups=mesh['y'=4,'c'=2,'z'=8,'x'=4] {'z'}, dimensions={0} | all-to-all | bytes 262144 | tf_op jit(solution)/shard_map/all_to_all | solution.py:41
  57.5 2.9 %collective-permute-start.7 = (bf16[512,128]{1,0:T(8,128)(2,1)S(1)}, bf16[512,128]{1,0:T(8,128)(2,1)S(1)}, u32[]{:S(2)}, u32[]{:S(2)}) collective-permute-start(bf16[512,128]{1,0:T(8,128)(2,1)S(1)} %bitcast.41), channel_id=1, source_target_pairs={{32,0},{0,32},{33,1},{1,33},{34,2},{2,34},{35,3},{3,35},{36,4},{4,... | collective-permute-start | bytes 393224 | tf_op jit(solution)/shard_map/ppermute | solution.py:26
  61.0 0.5 collective-permute-done.7
  61.5 0.5 fusion.2
  62.1 11.1 %all_to_all.27 = f16[16,72,128]{2,1,0:T(8,128)(2,1)S(1)} all-to-all(f16[16,72,128]{2,1,0:T(8,128)(2,1)S(1)} %pad_maximum_fusion.1), channel_id=1, replica_groups=mesh['y'=4,'c'=2,'z'=8,'x'=4] {'y','x'}, dimensions={0} | all-to-all | bytes 589824 | tf_op jit(solution)/shard_map/all_to_all | solution.py:181
  73.5 1.6 %collective-permute-start.8 = (f32[1,128]{1,0:T(1,128)S(1)}, f32[1,128]{1,0:T(1,128)S(1)}, u32[]{:S(2)}, u32[]{:S(2)}) collective-permute-start(f32[1,128]{1,0:T(1,128)S(1)} %bitcast.58), channel_id=1, source_target_pairs={{32,0},{0,32},{33,1},{1,33},{34,2},{2,34},{35,3},{3,35},{36,4},{4,... | collective-permute-start | bytes 1544 | tf_op jit(solution)/shard_map/ppermute | solution.py:26
  75.1 0.8 collective-permute-done.8
  75.9 16.1 %all_to_all.28 = f32[128,1,128]{2,1,0:T(1,128)S(1)} all-to-all(f32[128,1,128]{2,1,0:T(1,128)S(1)} %broadcast_in_dim.61), channel_id=1, replica_groups=mesh['y'=4,'c'=2,'z'=8,'x'=4] {'y','z','x'}, dimensions={0} | all-to-all | bytes 131072 | tf_op jit(solution)/shard_map/all_to_all | solution.py:41
  92.2 0.6 multiply_add_fusion
  (50 shorter events, 2.7 us)
Async XLA Ops:
  2.5 14.0 %collective-permute-start.2 = (bf16[64,128]{1,0:T(8,128)(2,1)S(1)}, bf16[64,128]{1,0:T(8,128)(2,1)S(1)}, u32[]{:S(2)}, u32[]{:S(2)}) collective-permute-start(bf16[64,128]{1,0:T(8,128)(2,1)S(1)} %get-tuple-element.10), channel_id=1, source_target_pairs={{3,0},{0,1},{1,2},{2,3},{7,4},{4,5},{5,6},{6,7},{11,8},{8,9},{9,10... | collective-permute-start | bytes 49160 | tf_op jit(solution)/shard_map/ppermute | solution.py:26
  4.5 12.0 %collective-permute-start.1 = (bf16[64,128]{1,0:T(8,128)(2,1)S(1)}, bf16[64,128]{1,0:T(8,128)(2,1)S(1)}, u32[]{:S(2)}, u32[]{:S(2)}) collective-permute-start(bf16[64,128]{1,0:T(8,128)(2,1)S(1)} %get-tuple-element.10), channel_id=1, source_target_pairs={{2,0},{3,1},{0,2},{1,3},{6,4},{7,5},{4,6},{5,7},{10,8},{11,9},{8,1... | collective-permute-start | bytes 49160 | tf_op jit(solution)/shard_map/ppermute | solution.py:26
  7.0 9.5 %collective-permute-start = (bf16[64,128]{1,0:T(8,128)(2,1)S(1)}, bf16[64,128]{1,0:T(8,128)(2,1)S(1)}, u32[]{:S(2)}, u32[]{:S(2)}) collective-permute-start(bf16[64,128]{1,0:T(8,128)(2,1)S(1)} %get-tuple-element.10), channel_id=1, source_target_pairs={{1,0},{2,1},{3,2},{0,3},{5,4},{6,5},{7,6},{4,7},{9,8},{10,9},{11,1... | collective-permute-start | bytes 49160 | tf_op jit(solution)/shard_map/ppermute | solution.py:26
  8.2 17.7 %all-to-all-start = ((bf16[8,128,128]{2,1,0:T(8,128)(2,1)}), bf16[8,128,128]{2,1,0:T(8,128)(2,1)S(1)}, u32[]{:S(2)}, u32[]{:S(2)}) async-start(bf16[8,128,128]{2,1,0:T(8,128)(2,1)} %get-tuple-element.11), calls=%async_computation | async-start | bytes 524288 | tf_op jit(solution)/shard_map/all_to_all | solution.py:167
  16.6 12.7 %collective-permute-start.5 = (bf16[256,128]{1,0:T(8,128)(2,1)S(1)}, bf16[256,128]{1,0:T(8,128)(2,1)S(1)}, u32[]{:S(2)}, u32[]{:S(2)}) collective-permute-start(bf16[256,128]{1,0:T(8,128)(2,1)S(1)} %constant_dynamic-update-slice_fusion.4), channel_id=1, source_target_pairs={{192,0},{0,64},{64,128},{128,192},{193,1},{1,65},{65,129},{129,193... | collective-permute-start | bytes 196616 | tf_op jit(solution)/shard_map/ppermute | solution.py:26
  17.9 6.4 %collective-permute-start.4 = (bf16[256,128]{1,0:T(8,128)(2,1)S(1)}, bf16[256,128]{1,0:T(8,128)(2,1)S(1)}, u32[]{:S(2)}, u32[]{:S(2)}) collective-permute-start(bf16[256,128]{1,0:T(8,128)(2,1)S(1)} %constant_dynamic-update-slice_fusion.4), channel_id=1, source_target_pairs={{128,0},{192,64},{0,128},{64,192},{129,1},{193,65},{1,129},{65,193... | collective-permute-start | bytes 196616 | tf_op jit(solution)/shard_map/ppermute | solution.py:26
  20.6 3.8 %collective-permute-start.3 = (bf16[256,128]{1,0:T(8,128)(2,1)S(1)}, bf16[256,128]{1,0:T(8,128)(2,1)S(1)}, u32[]{:S(2)}, u32[]{:S(2)}) collective-permute-start(bf16[256,128]{1,0:T(8,128)(2,1)S(1)} %constant_dynamic-update-slice_fusion.4), channel_id=1, source_target_pairs={{64,0},{128,64},{192,128},{0,192},{65,1},{129,65},{193,129},{1,193... | collective-permute-start | bytes 196616 | tf_op jit(solution)/shard_map/ppermute | solution.py:26
  25.8 4.5 %collective-permute-start.6 = (bf16[8,128,128]{2,1,0:T(8,128)(2,1)S(1)}, bf16[8,128,128]{2,1,0:T(8,128)(2,1)S(1)}, u32[]{:S(2)}, u32[]{:S(2)}) collective-permute-start(bf16[8,128,128]{2,1,0:T(8,128)(2,1)S(1)} %all-to-all-done), channel_id=1, source_target_pairs={{32,0},{0,32},{33,1},{1,33},{34,2},{2,34},{35,3},{3,35},{36,4},{4,... | collective-permute-start | bytes 786440 | tf_op jit(solution)/shard_map/ppermute | solution.py:26
  57.5 3.9 %collective-permute-start.7 = (bf16[512,128]{1,0:T(8,128)(2,1)S(1)}, bf16[512,128]{1,0:T(8,128)(2,1)S(1)}, u32[]{:S(2)}, u32[]{:S(2)}) collective-permute-start(bf16[512,128]{1,0:T(8,128)(2,1)S(1)} %bitcast.41), channel_id=1, source_target_pairs={{32,0},{0,32},{33,1},{1,33},{34,2},{2,34},{35,3},{3,35},{36,4},{4,... | collective-permute-start | bytes 393224 | tf_op jit(solution)/shard_map/ppermute | solution.py:26
  73.5 2.4 %collective-permute-start.8 = (f32[1,128]{1,0:T(1,128)S(1)}, f32[1,128]{1,0:T(1,128)S(1)}, u32[]{:S(2)}, u32[]{:S(2)}) collective-permute-start(f32[1,128]{1,0:T(1,128)S(1)} %bitcast.58), channel_id=1, source_target_pairs={{32,0},{0,32},{33,1},{1,33},{34,2},{2,34},{35,3},{3,35},{36,4},{4,... | collective-permute-start | bytes 1544 | tf_op jit(solution)/shard_map/ppermute | solution.py:26
